TPU v7x, 256 devices: a whole 4x4x8 slice. The times are simulated.
256 devices in a mesh: gx: 16 (over y, z_hi, core), gy: 16 (over x, z_lo).
Axes of the slice: x: 4, y: 4, z: 8 (z_hi: 2, z_lo: 4; z = z_hi * 4 + z_lo), core: 2. Of those that a mesh axis runs over, the one named last changes fastest.
Arguments:
- template: bfloat16 [512, 512, 256], P('gx', 'gy'), may hold values from -6 to 6
- mismatch: float32 [512, 512, 256], P('gx', 'gy'), may hold values from -6 to 6
- velocity: bfloat16 [2, 3, 512, 512, 256], P(None, None, 'gx', 'gy'), may hold values from -0.29882812 to 0.29882812
- src_ids: int32 [2, 16, 16, 8], P(None, 'gx', 'gy'), may hold values from 0 to 2047, as said below
Outputs:
- velocity_gradient: float32 [2, 3, 512, 512, 256], P(None, None, 'gx', 'gy')
Inputs may be any that keep to these rules, and one draw needn't show every extreme that they name: `src_ids`: for a destination block (i, j, l), the source block (a, b, c) has |a - i| <= 1 and |b - j| <= 1; c is any block along the third dimension.
All inputs are finite; a program needn't handle non-finite values.
Results may differ from a plain program's by a relative error of at most 0.0003.
Values may be sent and summed in bfloat16 or wider, within the bound.
No kernel may reach another device: no remote copies, remote signals or barrier semaphores. Data moves between devices by JAX's collectives and lax.ppermute only.
A program may use at most 64 MiB of HBM per device.

v0:
```python
import jax
import jax.numpy as jnp
from jax import lax
from jax.sharding import PartitionSpec as P


def padded(cells, sides, width):
    for axis, dim in sides:
        count = lax.axis_size(axis)
        ends = count - 1
        head = lax.slice_in_dim(cells, 0, width, axis=dim)
        tail = lax.slice_in_dim(cells, cells.shape[dim] - width, cells.shape[dim], axis=dim)
        cells = jnp.concatenate(
            [
                lax.ppermute(tail, axis, [(i, (i + 1) % count) for i in range(ends)]),
                cells,
                lax.ppermute(head, axis, [((i + 1) % count, i) for i in range(ends)]),
            ],
            axis=dim,
        )
    return cells


def pad_depth(values):
    return jnp.pad(values, [(0, 0)] * (values.ndim - 1) + [(1, 1)])


def upwind(adjoint, speeds):
    advect = -speeds
    first = adjoint[:, 1:-1]
    speed_one = advect[0, :, 1:-1]
    face_speed = 0.5 * (speed_one[:-1] + speed_one[1:])
    fluxes = jnp.maximum(face_speed, 0.0) * first[:-1] + jnp.minimum(face_speed, 0.0) * first[1:]
    divergence = fluxes[1:] - fluxes[:-1]
    second = adjoint[1:-1]
    speed_two = advect[1, 1:-1]
    face_speed = 0.5 * (speed_two[:, :-1] + speed_two[:, 1:])
    fluxes = (
        jnp.maximum(face_speed, 0.0) * second[:, :-1] + jnp.minimum(face_speed, 0.0) * second[:, 1:]
    )
    divergence = divergence + (fluxes[:, 1:] - fluxes[:, :-1])
    centre = adjoint[1:-1, 1:-1]
    third = pad_depth(centre)
    speed_three = pad_depth(advect[2, 1:-1, 1:-1])
    face_speed = 0.5 * (speed_three[:, :, :-1] + speed_three[:, :, 1:])
    fluxes = (
        jnp.maximum(face_speed, 0.0) * third[:, :, :-1]
        + jnp.minimum(face_speed, 0.0) * third[:, :, 1:]
    )
    divergence = divergence + (fluxes[:, :, 1:] - fluxes[:, :, :-1])
    return centre - divergence


def slopes(picture):
    along_one = 0.5 * (picture[..., 2:, 1:-1, :] - picture[..., :-2, 1:-1, :])
    along_two = 0.5 * (picture[..., 1:-1, 2:, :] - picture[..., 1:-1, :-2, :])
    centre = pad_depth(picture[..., 1:-1, 1:-1, :])
    along_three = 0.5 * (centre[..., 2:] - centre[..., :-2])
    return jnp.stack([along_one, along_two, along_three], axis=-4)


def smooth(forces):
    centre = forces[..., 1:-1, 1:-1, :]
    deeper = pad_depth(centre)
    beside_all = forces[..., 2:, 1:-1, :] + forces[..., :-2, 1:-1, :]
    beside_all = beside_all + forces[..., 1:-1, 2:, :] + forces[..., 1:-1, :-2, :]
    beside_all = beside_all + deeper[..., 2:] + deeper[..., :-2]
    return 0.25 * centre + 0.125 * beside_all


def body(template, mismatch, velocity, src_ids):
    block_edge = template.shape[0]
    column_depth = template.shape[2]
    depth_blocks = column_depth // block_edge
    extended = padded(template, (("gx", 0), ("gy", 1)), block_edge)
    index_first = lax.axis_index("gx")
    index_second = lax.axis_index("gy")
    count_second = lax.axis_size("gy")

    def pick_block(source):
        first_block = source // (count_second * depth_blocks)
        second_block = source // depth_blocks % count_second
        third_block = source % depth_blocks
        offsets = (
            (first_block - index_first + 1) * block_edge,
            (second_block - index_second + 1) * block_edge,
            third_block * block_edge,
        )
        return lax.dynamic_slice(extended, offsets, (block_edge, block_edge, block_edge))

    source_ids = src_ids.reshape(-1)
    blocks = jax.vmap(pick_block)(source_ids)
    images = blocks.reshape(2, depth_blocks, block_edge, block_edge, block_edge).transpose(
        0, 2, 3, 1, 4
    )
    images = images.reshape(2, block_edge, block_edge, column_depth)
    speeds_ext = padded(velocity, (("gx", 2), ("gy", 3)), 1)
    adjoint = mismatch
    later = []
    for instant in (1, 0):
        adjoint_ext = padded(adjoint, (("gx", 0), ("gy", 1)), 1)
        adjoint = upwind(adjoint_ext, speeds_ext[instant].astype(jnp.float32))
        later.append(adjoint)
    adjoint_one, adjoint_zero = later
    adjoint_pair = jnp.stack([adjoint_zero, adjoint_one])
    picture_ext = padded(images, (("gx", 1), ("gy", 2)), 1).astype(jnp.float32)
    forces = adjoint_pair[:, None] * slopes(picture_ext)
    forces_ext = padded(forces, (("gx", 2), ("gy", 3)), 1)
    return velocity.astype(jnp.float32) + smooth(forces_ext)


def solution(mesh):
    in_specs = (
        P("gx", "gy", None),
        P("gx", "gy", None),
        P(None, None, "gx", "gy", None),
        P(None, "gx", "gy", None),
    )
    out_specs = P(None, None, "gx", "gy", None)
    return jax.shard_map(body, mesh=mesh, in_specs=in_specs, out_specs=out_specs, check_vma=False)
```

profile of v0, /device:TPU:26, one launch (start us, length us, event | category | flops | bytes accessed | tf_op | source)
XLA Modules:
  0.0 318.6 jit_solution(14345661011396302579)
XLA Ops:
  1.9 8.7 %collective-permute-start.13 = (bf16[32,32,256]{2,1,0:T(8,128)(2,1)}, bf16[32,32,256]{2,1,0:T(8,128)(2,1)}, u32[]{:S(2)}, u32[]{:S(2)}) collective-permute-start(bf16[32,32,256]{2,1,0:T(8,128)(2,1)} %param.4), channel_id=1, source_target_pairs={{16,0},{32,16},{48,32},{64,48},{80,64},{96,80},{112,96},{128,112},... | collective-permute-start | bytes 1572872 | tf_op jit(solution)/shard_map/ppermute | solution.py:17
  14.6 8.0 %collective-permute-start.1 = (bf16[2,3,1,32,256]{4,3,2,1,0:T(8,128)(2,1)S(1)}, bf16[2,3,1,32,256]{4,3,2,1,0:T(8,128)(2,1)S(1)}, u32[]{:S(2)}, u32[]{:S(2)}) collective-permute-start(bf16[2,3,1,32,256]{4,3,2,1,0:T(8,128)(2,1)S(1)} %get-tuple-element.33), channel_id=1, source_target_pairs={{16,0},{32,16},{48,32},{64,48},{80,64},{96,80},{112,96},{128,112},... | collective-permute-start | bytes 294920 | tf_op jit(solution)/shard_map/ppermute | solution.py:17
  32.8 8.4 %collective-permute-start.5 = (f32[1,32,256]{2,0,1:T(1,128)}, f32[1,32,256]{2,0,1:T(1,128)S(1)}, u32[]{:S(2)}, u32[]{:S(2)}) collective-permute-start(f32[1,32,256]{2,0,1:T(1,128)} %copy.28), channel_id=1, source_target_pairs={{16,0},{32,16},{48,32},{64,48},{80,64},{96,80},{112,96},{128,112},... | collective-permute-start | bytes 98312 | tf_op jit(solution)/shard_map/ppermute | solution.py:17
  45.5 5.0 %collective-permute-start.3 = (bf16[2,3,34,1,256]{4,2,3,1,0:T(8,128)(2,1)S(1)}, bf16[2,3,34,1,256]{4,2,3,1,0:T(8,128)(2,1)S(1)}, u32[]{:S(2)}, u32[]{:S(2)}) collective-permute-start(bf16[2,3,34,1,256]{4,2,3,1,0:T(8,128)(2,1)S(1)} %get-tuple-element.31), channel_id=1, source_target_pairs={{1,0},{2,1},{3,2},{4,3},{5,4},{6,5},{7,6},{8,7},{9,8},{10,9},{11,1... | collective-permute-start | bytes 313352 | tf_op jit(solution)/shard_map/ppermute | solution.py:17
  52.4 6.6 %collective-permute-start.7 = (f32[34,1,256]{2,0,1:T(8,128)S(1)}, f32[34,1,256]{2,0,1:T(8,128)S(1)}, u32[]{:S(2)}, u32[]{:S(2)}) collective-permute-start(f32[34,1,256]{2,0,1:T(8,128)S(1)} %get-tuple-element.40), channel_id=1, source_target_pairs={{1,0},{2,1},{3,2},{4,3},{5,4},{6,5},{7,6},{8,7},{9,8},{10,9},{11,1... | collective-permute-start | bytes 104456 | tf_op jit(solution)/shard_map/ppermute | solution.py:17
  70.1 6.6 %collective-permute-start.15 = (bf16[96,32,256]{2,1,0:T(8,128)(2,1)S(1)}, bf16[96,32,256]{2,1,0:T(8,128)(2,1)S(1)}, u32[]{:S(2)}, u32[]{:S(2)}) collective-permute-start(bf16[96,32,256]{2,1,0:T(8,128)(2,1)S(1)} %constant_dynamic-update-slice_fusion), channel_id=1, source_target_pairs={{1,0},{2,1},{3,2},{4,3},{5,4},{6,5},{7,6},{8,7},{9,8},{10,9},{11,1... | collective-permute-start | bytes 4718600 | tf_op jit(solution)/shard_map/ppermute | solution.py:17
  78.7 8.4 %collective-permute-start.9 = (f32[1,32,256]{2,0,1:T(1,128)S(1)}, f32[1,32,256]{2,0,1:T(1,128)S(1)}, u32[]{:S(2)}, u32[]{:S(2)}) collective-permute-start(f32[1,32,256]{2,0,1:T(1,128)S(1)} %get-tuple-element.44), channel_id=1, source_target_pairs={{16,0},{32,16},{48,32},{64,48},{80,64},{96,80},{112,96},{128,112},... | collective-permute-start | bytes 98312 | tf_op jit(solution)/shard_map/ppermute | solution.py:17
  89.5 43.6 %collective-permute-done.8 = f32[1,32,256]{2,0,1:T(1,128)S(1)} collective-permute-done((f32[1,32,256]{2,0,1:T(1,128)S(1)}, f32[1,32,256]{2,0,1:T(1,128)S(1)}, u32[]{:S(2)}, u32[]{:S(2)}) %collective-permute-start.8) | collective-permute-done | bytes 32800 | tf_op jit(solution)/shard_map/ppermute | solution.py:15
  136.5 6.7 %collective-permute-start.10 = (f32[34,1,256]{2,0,1:T(8,128)S(1)}, f32[34,1,256]{2,0,1:T(8,128)S(1)}, u32[]{:S(2)}, u32[]{:S(2)}) collective-permute-start(f32[34,1,256]{2,0,1:T(8,128)S(1)} %get-tuple-element.37), channel_id=1, source_target_pairs={{0,1},{1,2},{2,3},{3,4},{4,5},{5,6},{6,7},{7,8},{8,9},{9,10},{10,1... | collective-permute-start | bytes 104456 | tf_op jit(solution)/shard_map/ppermute | solution.py:15
  151.8 72.3 %while.1 = (s32[]{:T(128)}, bf16[96,96,256]{2,1,0:T(8,128)(2,1)}, s32[16,3]{0,1:T(4,128)S(1)}, bf16[16,32,32,32]{3,2,1,0:T(8,128)(2,1)}, s32[]{:T(128)}) while((s32[]{:T(128)}, bf16[96,96,256]{2,1,0:T(8,128)(2,1)}, s32[16,3]{0,1:T(4,128)S(1)}, bf16[16,32,32,32]{3,2,1,0:T(8,128)(2,1)}, s32[]{:T(128)}) %tuple.35), condition=%wide.while_cond, body=%wide.while_body.sunk | while | flops 2 | bytes 526449 | solution.py:89
  152.5 3.9 %bitcast_dynamic-update-slice_fusion.2 = bf16[16,32,32,32]{3,2,1,0:T(8,128)(2,1)} fusion(bf16[16,32,32,32]{3,2,1,0:T(8,128)(2,1)} %get-tuple-element.91, s32[]{:T(128)} %get-tuple-element.88, bf16[96,96,256]{2,1,0:T(8,128)(2,1)} %get-tuple-element.94, s32[]{:T(128)} %bitcast.49, s32[]{:T(128)} %bitcast.50, s32[]{:T(128)} %bitcast.51), kind=kLoop, calls=%fused_computation.clone.1 | loop fusion | bytes 526336 | tf_op jit(solution)/shard_map/vmap()/gather
  175.0 3.9 %bitcast_dynamic-update-slice_fusion.2 = bf16[16,32,32,32]{3,2,1,0:T(8,128)(2,1)} fusion(bf16[16,32,32,32]{3,2,1,0:T(8,128)(2,1)} %get-tuple-element.91, s32[]{:T(128)} %get-tuple-element.88, bf16[96,96,256]{2,1,0:T(8,128)(2,1)} %get-tuple-element.94, s32[]{:T(128)} %bitcast.49, s32[]{:T(128)} %bitcast.50, s32[]{:T(128)} %bitcast.51), kind=kLoop, calls=%fused_computation.clone.1 | loop fusion | bytes 526336 | tf_op jit(solution)/shard_map/vmap()/gather
  202.1 3.8 %bitcast_dynamic-update-slice_fusion.2 = bf16[16,32,32,32]{3,2,1,0:T(8,128)(2,1)} fusion(bf16[16,32,32,32]{3,2,1,0:T(8,128)(2,1)} %get-tuple-element.91, s32[]{:T(128)} %get-tuple-element.88, bf16[96,96,256]{2,1,0:T(8,128)(2,1)} %get-tuple-element.94, s32[]{:T(128)} %bitcast.49, s32[]{:T(128)} %bitcast.50, s32[]{:T(128)} %bitcast.51), kind=kLoop, calls=%fused_computation.clone.1 | loop fusion | bytes 526336 | tf_op jit(solution)/shard_map/vmap()/gather
  215.5 3.9 %bitcast_dynamic-update-slice_fusion.2 = bf16[16,32,32,32]{3,2,1,0:T(8,128)(2,1)} fusion(bf16[16,32,32,32]{3,2,1,0:T(8,128)(2,1)} %get-tuple-element.91, s32[]{:T(128)} %get-tuple-element.88, bf16[96,96,256]{2,1,0:T(8,128)(2,1)} %get-tuple-element.94, s32[]{:T(128)} %bitcast.49, s32[]{:T(128)} %bitcast.50, s32[]{:T(128)} %bitcast.51), kind=kLoop, calls=%fused_computation.clone.1 | loop fusion | bytes 526336 | tf_op jit(solution)/shard_map/vmap()/gather
  220.1 3.9 %bitcast_dynamic-update-slice_fusion.2 = bf16[16,32,32,32]{3,2,1,0:T(8,128)(2,1)} fusion(bf16[16,32,32,32]{3,2,1,0:T(8,128)(2,1)} %get-tuple-element.91, s32[]{:T(128)} %get-tuple-element.88, bf16[96,96,256]{2,1,0:T(8,128)(2,1)} %get-tuple-element.94, s32[]{:T(128)} %bitcast.49, s32[]{:T(128)} %bitcast.50, s32[]{:T(128)} %bitcast.51), kind=kLoop, calls=%fused_computation.clone.1 | loop fusion | bytes 526336 | tf_op jit(solution)/shard_map/vmap()/gather
  224.1 9.1 %copy.43 = bf16[2,8,32,32,32]{4,1,3,2,0:T(8,128)(2,1)} copy(bf16[2,8,32,32,32]{4,3,2,1,0:T(8,128)(2,1)} %bitcast.54) | data formatting | bytes 2097152 | tf_op jit(solution)/shard_map/reshape | solution.py:93
  233.1 6.2 %reshape.260 = bf16[2,32,32,256]{3,2,1,0:T(8,128)(2,1)} reshape(bf16[2,32,32,8,32]{4,3,2,1,0:T(8,128)(2,1)} %bitcast.53) | data formatting | bytes 2097152 | tf_op jit(solution)/shard_map/reshape | solution.py:96
  244.4 8.4 %collective-permute-start.17 = (bf16[2,1,32,256]{3,2,1,0:T(8,128)(2,1)S(1)}, bf16[2,1,32,256]{3,2,1,0:T(8,128)(2,1)S(1)}, u32[]{:S(2)}, u32[]{:S(2)}) collective-permute-start(bf16[2,1,32,256]{3,2,1,0:T(8,128)(2,1)S(1)} %get-tuple-element.47), channel_id=1, source_target_pairs={{16,0},{32,16},{48,32},{64,48},{80,64},{96,80},{112,96},{128,112},... | collective-permute-start | bytes 98312 | tf_op jit(solution)/shard_map/ppermute | solution.py:17
  256.9 6.5 %collective-permute-start.19 = (bf16[2,34,1,256]{3,2,1,0:T(2,128)(2,1)S(1)}, bf16[2,34,1,256]{3,2,1,0:T(2,128)(2,1)S(1)}, u32[]{:S(2)}, u32[]{:S(2)}) collective-permute-start(bf16[2,34,1,256]{3,2,1,0:T(2,128)(2,1)S(1)} %get-tuple-element.42), channel_id=1, source_target_pairs={{1,0},{2,1},{3,2},{4,3},{5,4},{6,5},{7,6},{8,7},{9,8},{10,9},{11,1... | collective-permute-start | bytes 104456 | tf_op jit(solution)/shard_map/ppermute | solution.py:17
  268.8 8.1 %collective-permute-start.20 = (f32[2,3,1,32,256]{4,3,2,1,0:T(8,128)S(1)}, f32[2,3,1,32,256]{4,3,2,1,0:T(8,128)S(1)}, u32[]{:S(2)}, u32[]{:S(2)}) collective-permute-start(f32[2,3,1,32,256]{4,3,2,1,0:T(8,128)S(1)} %get-tuple-element.27), channel_id=1, source_target_pairs={{16,0},{32,16},{48,32},{64,48},{80,64},{96,80},{112,96},{128,112},... | collective-permute-start | bytes 589832 | tf_op jit(solution)/shard_map/ppermute | solution.py:17
  282.1 7.5 %collective-permute-done.21 = f32[2,3,1,32,256]{4,3,2,1,0:T(8,128)S(1)} collective-permute-done((f32[2,3,1,32,256]{4,3,2,1,0:T(8,128)S(1)}, f32[2,3,1,32,256]{4,3,2,1,0:T(8,128)S(1)}, u32[]{:S(2)}, u32[]{:S(2)}) %collective-permute-start.21) | collective-permute-done | bytes 196640 | tf_op jit(solution)/shard_map/ppermute | solution.py:15
  290.0 6.7 %collective-permute-start.22 = (f32[2,3,34,1,256]{4,2,3,1,0:T(8,128)S(1)}, f32[2,3,34,1,256]{4,2,3,1,0:T(8,128)S(1)}, u32[]{:S(2)}, u32[]{:S(2)}) collective-permute-start(f32[2,3,34,1,256]{4,2,3,1,0:T(8,128)S(1)} %copy.37), channel_id=1, source_target_pairs={{1,0},{2,1},{3,2},{4,3},{5,4},{6,5},{7,6},{8,7},{9,8},{10,9},{11,1... | collective-permute-start | bytes 626696 | tf_op jit(solution)/shard_map/ppermute | solution.py:17
  300.7 6.9 %collective-permute-done.23 = f32[2,3,34,1,256]{4,2,3,1,0:T(8,128)S(1)} collective-permute-done((f32[2,3,34,1,256]{4,2,3,1,0:T(8,128)S(1)}, f32[2,3,34,1,256]{4,2,3,1,0:T(8,128)S(1)}, u32[]{:S(2)}, u32[]{:S(2)}) %collective-permute-start.23) | collective-permute-done | bytes 208928 | tf_op jit(solution)/shard_map/ppermute | solution.py:15
  307.7 10.8 %fusion.4 = f32[2,3,32,32,256]{4,3,2,1,0:T(8,128)} fusion(f32[2,3,32,32,256]{4,3,2,1,0:T(8,128)S(1)} %maximum_multiply_fusion, f32[2,3,34,1,256]{4,3,2,1,0:T(1,128)S(1)} %copy.40, f32[2,3,1,32,256]{4,3,2,1,0:T(8,128)S(1)} %collective-permute-done.20, f32[2,3,1,32,256]{4,3,2,1,0:T(8,128)S(1)} %collective-permute-done.21, f32[2,3,34,1,256]{4,3,2,1,0:T(1,128)S(1)} %copy.38, ...), kind=kLoop, calls=%fused_computation.8 | loop fusion | flops 28311552 | bytes 16539648 | tf_op jit(solution)/shard_map/add | solution.py:109
  (143 shorter events, 126.1 us)
Async XLA Ops:
  0.0 65.9 %collective-permute-start.12 = (bf16[32,32,256]{2,1,0:T(8,128)(2,1)}, bf16[32,32,256]{2,1,0:T(8,128)(2,1)}, u32[]{:S(2)}, u32[]{:S(2)}) collective-permute-start(bf16[32,32,256]{2,1,0:T(8,128)(2,1)} %param.4), channel_id=1, source_target_pairs={{0,16},{16,32},{32,48},{48,64},{64,80},{80,96},{96,112},{112,128},... | collective-permute-start | bytes 1572872 | tf_op jit(solution)/shard_map/ppermute | solution.py:15
  1.9 65.1 %collective-permute-start.13 = (bf16[32,32,256]{2,1,0:T(8,128)(2,1)}, bf16[32,32,256]{2,1,0:T(8,128)(2,1)}, u32[]{:S(2)}, u32[]{:S(2)}) collective-permute-start(bf16[32,32,256]{2,1,0:T(8,128)(2,1)} %param.4), channel_id=1, source_target_pairs={{16,0},{32,16},{48,32},{64,48},{80,64},{96,80},{112,96},{128,112},... | collective-permute-start | bytes 1572872 | tf_op jit(solution)/shard_map/ppermute | solution.py:17
  12.2 20.6 %collective-permute-start = (bf16[2,3,1,32,256]{4,3,2,1,0:T(8,128)(2,1)}, bf16[2,3,1,32,256]{4,3,2,1,0:T(8,128)(2,1)S(1)}, u32[]{:S(2)}, u32[]{:S(2)}) collective-permute-start(bf16[2,3,1,32,256]{4,3,2,1,0:T(8,128)(2,1)} %get-tuple-element.32), channel_id=1, source_target_pairs={{0,16},{16,32},{32,48},{48,64},{64,80},{80,96},{96,112},{112,128},... | collective-permute-start | bytes 294920 | tf_op jit(solution)/shard_map/ppermute | solution.py:15
  14.6 26.8 %collective-permute-start.1 = (bf16[2,3,1,32,256]{4,3,2,1,0:T(8,128)(2,1)S(1)}, bf16[2,3,1,32,256]{4,3,2,1,0:T(8,128)(2,1)S(1)}, u32[]{:S(2)}, u32[]{:S(2)}) collective-permute-start(bf16[2,3,1,32,256]{4,3,2,1,0:T(8,128)(2,1)S(1)} %get-tuple-element.33), channel_id=1, source_target_pairs={{16,0},{32,16},{48,32},{64,48},{80,64},{96,80},{112,96},{128,112},... | collective-permute-start | bytes 294920 | tf_op jit(solution)/shard_map/ppermute | solution.py:17
  23.5 22.0 %collective-permute-start.4 = (f32[1,32,256]{2,0,1:T(1,128)S(1)}, f32[1,32,256]{2,0,1:T(1,128)S(1)}, u32[]{:S(2)}, u32[]{:S(2)}) collective-permute-start(f32[1,32,256]{2,0,1:T(1,128)S(1)} %copy.26), channel_id=1, source_target_pairs={{0,16},{16,32},{32,48},{48,64},{64,80},{80,96},{96,112},{112,128},... | collective-permute-start | bytes 98312 | tf_op jit(solution)/shard_map/ppermute | solution.py:15
  32.8 17.6 %collective-permute-start.5 = (f32[1,32,256]{2,0,1:T(1,128)}, f32[1,32,256]{2,0,1:T(1,128)S(1)}, u32[]{:S(2)}, u32[]{:S(2)}) collective-permute-start(f32[1,32,256]{2,0,1:T(1,128)} %copy.28), channel_id=1, source_target_pairs={{16,0},{32,16},{48,32},{64,48},{80,64},{96,80},{112,96},{128,112},... | collective-permute-start | bytes 98312 | tf_op jit(solution)/shard_map/ppermute | solution.py:17
  41.7 10.7 %collective-permute-start.2 = (bf16[2,3,34,1,256]{4,2,3,1,0:T(8,128)(2,1)S(1)}, bf16[2,3,34,1,256]{4,2,3,1,0:T(8,128)(2,1)S(1)}, u32[]{:S(2)}, u32[]{:S(2)}) collective-permute-start(bf16[2,3,34,1,256]{4,2,3,1,0:T(8,128)(2,1)S(1)} %get-tuple-element.30), channel_id=1, source_target_pairs={{0,1},{1,2},{2,3},{3,4},{4,5},{5,6},{6,7},{7,8},{8,9},{9,10},{10,1... | collective-permute-start | bytes 313352 | tf_op jit(solution)/shard_map/ppermute | solution.py:15
  45.5 13.6 %collective-permute-start.3 = (bf16[2,3,34,1,256]{4,2,3,1,0:T(8,128)(2,1)S(1)}, bf16[2,3,34,1,256]{4,2,3,1,0:T(8,128)(2,1)S(1)}, u32[]{:S(2)}, u32[]{:S(2)}) collective-permute-start(bf16[2,3,34,1,256]{4,2,3,1,0:T(8,128)(2,1)S(1)} %get-tuple-element.31), channel_id=1, source_target_pairs={{1,0},{2,1},{3,2},{4,3},{5,4},{6,5},{7,6},{8,7},{9,8},{10,9},{11,1... | collective-permute-start | bytes 313352 | tf_op jit(solution)/shard_map/ppermute | solution.py:17
  50.5 12.7 %collective-permute-start.6 = (f32[34,1,256]{2,0,1:T(8,128)S(1)}, f32[34,1,256]{2,0,1:T(8,128)S(1)}, u32[]{:S(2)}, u32[]{:S(2)}) collective-permute-start(f32[34,1,256]{2,0,1:T(8,128)S(1)} %get-tuple-element.39), channel_id=1, source_target_pairs={{0,1},{1,2},{2,3},{3,4},{4,5},{5,6},{6,7},{7,8},{8,9},{9,10},{10,1... | collective-permute-start | bytes 104456 | tf_op jit(solution)/shard_map/ppermute | solution.py:15
  52.4 10.8 %collective-permute-start.7 = (f32[34,1,256]{2,0,1:T(8,128)S(1)}, f32[34,1,256]{2,0,1:T(8,128)S(1)}, u32[]{:S(2)}, u32[]{:S(2)}) collective-permute-start(f32[34,1,256]{2,0,1:T(8,128)S(1)} %get-tuple-element.40), channel_id=1, source_target_pairs={{1,0},{2,1},{3,2},{4,3},{5,4},{6,5},{7,6},{8,7},{9,8},{10,9},{11,1... | collective-permute-start | bytes 104456 | tf_op jit(solution)/shard_map/ppermute | solution.py:17
  68.1 81.3 %collective-permute-start.14 = (bf16[96,32,256]{2,1,0:T(8,128)(2,1)S(1)}, bf16[96,32,256]{2,1,0:T(8,128)(2,1)S(1)}, u32[]{:S(2)}, u32[]{:S(2)}) collective-permute-start(bf16[96,32,256]{2,1,0:T(8,128)(2,1)S(1)} %constant_dynamic-update-slice_fusion), channel_id=1, source_target_pairs={{0,1},{1,2},{2,3},{3,4},{4,5},{5,6},{6,7},{7,8},{8,9},{9,10},{10,1... | collective-permute-start | bytes 4718600 | tf_op jit(solution)/shard_map/ppermute | solution.py:15
  70.1 79.4 %collective-permute-start.15 = (bf16[96,32,256]{2,1,0:T(8,128)(2,1)S(1)}, bf16[96,32,256]{2,1,0:T(8,128)(2,1)S(1)}, u32[]{:S(2)}, u32[]{:S(2)}) collective-permute-start(bf16[96,32,256]{2,1,0:T(8,128)(2,1)S(1)} %constant_dynamic-update-slice_fusion), channel_id=1, source_target_pairs={{1,0},{2,1},{3,2},{4,3},{5,4},{6,5},{7,6},{8,7},{9,8},{10,9},{11,1... | collective-permute-start | bytes 4718600 | tf_op jit(solution)/shard_map/ppermute | solution.py:17
  76.8 56.4 %collective-permute-start.8 = (f32[1,32,256]{2,0,1:T(1,128)S(1)}, f32[1,32,256]{2,0,1:T(1,128)S(1)}, u32[]{:S(2)}, u32[]{:S(2)}) collective-permute-start(f32[1,32,256]{2,0,1:T(1,128)S(1)} %get-tuple-element.43), channel_id=1, source_target_pairs={{0,16},{16,32},{32,48},{48,64},{64,80},{80,96},{96,112},{112,128},... | collective-permute-start | bytes 98312 | tf_op jit(solution)/shard_map/ppermute | solution.py:15
  78.7 57.8 %collective-permute-start.9 = (f32[1,32,256]{2,0,1:T(1,128)S(1)}, f32[1,32,256]{2,0,1:T(1,128)S(1)}, u32[]{:S(2)}, u32[]{:S(2)}) collective-permute-start(f32[1,32,256]{2,0,1:T(1,128)S(1)} %get-tuple-element.44), channel_id=1, source_target_pairs={{16,0},{32,16},{48,32},{64,48},{80,64},{96,80},{112,96},{128,112},... | collective-permute-start | bytes 98312 | tf_op jit(solution)/shard_map/ppermute | solution.py:17
  136.5 9.4 %collective-permute-start.10 = (f32[34,1,256]{2,0,1:T(8,128)S(1)}, f32[34,1,256]{2,0,1:T(8,128)S(1)}, u32[]{:S(2)}, u32[]{:S(2)}) collective-permute-start(f32[34,1,256]{2,0,1:T(8,128)S(1)} %get-tuple-element.37), channel_id=1, source_target_pairs={{0,1},{1,2},{2,3},{3,4},{4,5},{5,6},{6,7},{7,8},{8,9},{9,10},{10,1... | collective-permute-start | bytes 104456 | tf_op jit(solution)/shard_map/ppermute | solution.py:15
  143.2 5.9 %collective-permute-start.11 = (f32[34,1,256]{2,0,1:T(8,128)S(1)}, f32[34,1,256]{2,0,1:T(8,128)S(1)}, u32[]{:S(2)}, u32[]{:S(2)}) collective-permute-start(f32[34,1,256]{2,0,1:T(8,128)S(1)} %get-tuple-element.38), channel_id=1, source_target_pairs={{1,0},{2,1},{3,2},{4,3},{5,4},{6,5},{7,6},{8,7},{9,8},{10,9},{11,1... | collective-permute-start | bytes 104456 | tf_op jit(solution)/shard_map/ppermute | solution.py:17
  240.1 12.8 %collective-permute-start.16 = (bf16[2,1,32,256]{3,2,1,0:T(8,128)(2,1)S(1)}, bf16[2,1,32,256]{3,2,1,0:T(8,128)(2,1)S(1)}, u32[]{:S(2)}, u32[]{:S(2)}) collective-permute-start(bf16[2,1,32,256]{3,2,1,0:T(8,128)(2,1)S(1)} %get-tuple-element.48), channel_id=1, source_target_pairs={{0,16},{16,32},{32,48},{48,64},{64,80},{80,96},{96,112},{112,128},... | collective-permute-start | bytes 98312 | tf_op jit(solution)/shard_map/ppermute | solution.py:15
  244.4 10.0 %collective-permute-start.17 = (bf16[2,1,32,256]{3,2,1,0:T(8,128)(2,1)S(1)}, bf16[2,1,32,256]{3,2,1,0:T(8,128)(2,1)S(1)}, u32[]{:S(2)}, u32[]{:S(2)}) collective-permute-start(bf16[2,1,32,256]{3,2,1,0:T(8,128)(2,1)S(1)} %get-tuple-element.47), channel_id=1, source_target_pairs={{16,0},{32,16},{48,32},{64,48},{80,64},{96,80},{112,96},{128,112},... | collective-permute-start | bytes 98312 | tf_op jit(solution)/shard_map/ppermute | solution.py:17
  254.6 10.3 %collective-permute-start.18 = (bf16[2,34,1,256]{3,2,1,0:T(2,128)(2,1)S(1)}, bf16[2,34,1,256]{3,2,1,0:T(2,128)(2,1)S(1)}, u32[]{:S(2)}, u32[]{:S(2)}) collective-permute-start(bf16[2,34,1,256]{3,2,1,0:T(2,128)(2,1)S(1)} %get-tuple-element.41), channel_id=1, source_target_pairs={{0,1},{1,2},{2,3},{3,4},{4,5},{5,6},{6,7},{7,8},{8,9},{9,10},{10,1... | collective-permute-start | bytes 104456 | tf_op jit(solution)/shard_map/ppermute | solution.py:15
  256.9 8.2 %collective-permute-start.19 = (bf16[2,34,1,256]{3,2,1,0:T(2,128)(2,1)S(1)}, bf16[2,34,1,256]{3,2,1,0:T(2,128)(2,1)S(1)}, u32[]{:S(2)}, u32[]{:S(2)}) collective-permute-start(bf16[2,34,1,256]{3,2,1,0:T(2,128)(2,1)S(1)} %get-tuple-element.42), channel_id=1, source_target_pairs={{1,0},{2,1},{3,2},{4,3},{5,4},{6,5},{7,6},{8,7},{9,8},{10,9},{11,1... | collective-permute-start | bytes 104456 | tf_op jit(solution)/shard_map/ppermute | solution.py:17
  268.8 13.4 %collective-permute-start.20 = (f32[2,3,1,32,256]{4,3,2,1,0:T(8,128)S(1)}, f32[2,3,1,32,256]{4,3,2,1,0:T(8,128)S(1)}, u32[]{:S(2)}, u32[]{:S(2)}) collective-permute-start(f32[2,3,1,32,256]{4,3,2,1,0:T(8,128)S(1)} %get-tuple-element.27), channel_id=1, source_target_pairs={{16,0},{32,16},{48,32},{64,48},{80,64},{96,80},{112,96},{128,112},... | collective-permute-start | bytes 589832 | tf_op jit(solution)/shard_map/ppermute | solution.py:17
  276.8 12.9 %collective-permute-start.21 = (f32[2,3,1,32,256]{4,3,2,1,0:T(8,128)S(1)}, f32[2,3,1,32,256]{4,3,2,1,0:T(8,128)S(1)}, u32[]{:S(2)}, u32[]{:S(2)}) collective-permute-start(f32[2,3,1,32,256]{4,3,2,1,0:T(8,128)S(1)} %get-tuple-element.26), channel_id=1, source_target_pairs={{0,16},{16,32},{32,48},{48,64},{64,80},{80,96},{96,112},{112,128},... | collective-permute-start | bytes 589832 | tf_op jit(solution)/shard_map/ppermute | solution.py:15
  290.0 10.4 %collective-permute-start.22 = (f32[2,3,34,1,256]{4,2,3,1,0:T(8,128)S(1)}, f32[2,3,34,1,256]{4,2,3,1,0:T(8,128)S(1)}, u32[]{:S(2)}, u32[]{:S(2)}) collective-permute-start(f32[2,3,34,1,256]{4,2,3,1,0:T(8,128)S(1)} %copy.37), channel_id=1, source_target_pairs={{1,0},{2,1},{3,2},{4,3},{5,4},{6,5},{7,6},{8,7},{9,8},{10,9},{11,1... | collective-permute-start | bytes 626696 | tf_op jit(solution)/shard_map/ppermute | solution.py:17
  296.7 10.8 %collective-permute-start.23 = (f32[2,3,34,1,256]{4,2,3,1,0:T(8,128)S(1)}, f32[2,3,34,1,256]{4,2,3,1,0:T(8,128)S(1)}, u32[]{:S(2)}, u32[]{:S(2)}) collective-permute-start(f32[2,3,34,1,256]{4,2,3,1,0:T(8,128)S(1)} %copy.39), channel_id=1, source_target_pairs={{0,1},{1,2},{2,3},{3,4},{4,5},{5,6},{6,7},{7,8},{8,9},{9,10},{10,1... | collective-permute-start | bytes 626696 | tf_op jit(solution)/shard_map/ppermute | solution.py:15
  (7 other events, 51.6 us)
where the time goes:
time: 323 us; the launch traced here: 319 us
  starting transfers between devices  114 us (35%)
  local copies, waits for them, and re-layouts  103 us (32%)
  waiting for transfers between devices  71.5 us (22%)
  other arithmetic  29.7 us (9%)
    ppermute x12, starting transfers between devices, padded(): lax.ppermute(head, axis, [((i + 1) % count, i) for i in range(ends)])  83.6 us
    gather x48, local copies, waits for them, and re-layouts  72.2 us
    ppermute x12, waiting for transfers between devices, padded(): lax.ppermute(tail, axis, [(i, (i + 1) % count) for i in range(ends)])  58.1 us
    ppermute x12, starting transfers between devices, padded(): lax.ppermute(tail, axis, [(i, (i + 1) % count) for i in range(ends)])  30.7 us
    ppermute x12, waiting for transfers between devices, padded(): lax.ppermute(head, axis, [((i + 1) % count, i) for i in range(ends)])  13.4 us
    add x1, other arithmetic, body(): return velocity.astype(jnp.float32) + smooth(forces_ext)  10.8 us
    reshape x1, local copies, waits for them, and re-layouts, body(): blocks.reshape(2, depth_blocks, block_edge, block_edge, block_edge)  9.06 us
    unnamed x21, local copies, waits for them, and re-layouts  7.39 us
  transfers between devices with their start and end apart: 24, of which 9 were waited for; matrix products, arithmetic and copies ran while one was open for 8% of the time, Pallas kernels for 0%

commit v1 on v0

v1 whole, which is shorter than its diff:
```python
import functools

import jax
import jax.numpy as jnp
from jax import lax
from jax.experimental import pallas as pl
from jax.experimental.pallas import tpu as pltpu
from jax.sharding import PartitionSpec as P

F32 = jnp.float32
BF16 = jnp.bfloat16
VMEM_LIMIT = 48 << 20


def whole(shape):
    return pl.BlockSpec(shape, lambda *_: (0,) * len(shape))


def call(kernel, outs, scratch, name, in_specs, aliases=None, out_specs=None):
    return pl.pallas_call(
        kernel,
        name=name,
        grid=(1,),
        in_specs=in_specs,
        out_specs=out_specs or [whole(o.shape) for o in outs],
        out_shape=outs,
        scratch_shapes=scratch,
        input_output_aliases=aliases or {},
        compiler_params=pltpu.CompilerParams(vmem_limit_bytes=VMEM_LIMIT),
    )


def struct(shape, dtype):
    return jax.ShapeDtypeStruct(shape, dtype)


def face_flux(here, following, speed_here, speed_following):
    total = speed_here + speed_following
    return jnp.minimum(total, 0.0) * here + jnp.maximum(total, 0.0) * following


def upwind_kernel(
    field_at, speed_at,
    p_ref, v_ref, pxl, pxh, pyl, pyh, vxl, vxh, vyl, vyh,
    o_ref, fxl, fxh, fyl, fyh,
    s_pl, s_ph, s_vl, s_vh, s_fl, s_fh,
):
    nx, ny, nz = p_ref.shape
    s_pl[...] = pyl[field_at].astype(F32)
    s_ph[...] = pyh[field_at].astype(F32)
    s_vl[...] = vyl[speed_at].astype(F32)
    s_vh[...] = vyh[speed_at].astype(F32)
    rows = lax.broadcasted_iota(jnp.int32, (ny, nz), 0)
    lanes = lax.broadcasted_iota(jnp.int32, (ny, nz), 1)

    def plane(x, flux_below, p_next, vx_next):
        p = p_ref[x]
        flux_above = face_flux(p, p_next, v_ref[0, 0, x].astype(F32), vx_next)
        change = flux_above - flux_below
        vy = v_ref[0, 1, x].astype(F32)
        at = pl.ds(x, 1)
        p_up = jnp.where(rows == ny - 1, s_ph[at, :], pltpu.roll(p, ny - 1, 0))
        v_up = jnp.where(rows == ny - 1, s_vh[at, :], pltpu.roll(vy, ny - 1, 0))
        upper = face_flux(p, p_up, vy, v_up)
        first = face_flux(s_pl[at, :], p[0:1], s_vl[at, :], vy[0:1])
        change = change + (upper - jnp.where(rows == 0, first, pltpu.roll(upper, 1, 0)))
        vz = v_ref[0, 2, x].astype(F32)
        p_up = jnp.where(lanes == nz - 1, 0.0, pltpu.roll(p, nz - 1, 1))
        v_up = jnp.where(lanes == nz - 1, 0.0, pltpu.roll(vz, nz - 1, 1))
        upper = face_flux(p, p_up, vz, v_up)
        lower = jnp.where(lanes == 0, jnp.maximum(vz, 0.0) * p, pltpu.roll(upper, 1, 1))
        change = change + (upper - lower)
        out = p + 0.5 * change
        o_ref[x] = out
        s_fl[at, :] = out[0:1]
        s_fh[at, :] = out[ny - 1 : ny]
        return flux_above

    flux = face_flux(pxl[field_at].astype(F32), p_ref[0], vxl[speed_at].astype(F32), v_ref[0, 0, 0].astype(F32))
    flux = lax.fori_loop(
        0, nx - 1, lambda x, f: plane(x, f, p_ref[x + 1], v_ref[0, 0, x + 1].astype(F32)), flux
    )
    plane(nx - 1, flux, pxh[field_at].astype(F32), vxh[speed_at].astype(F32))
    fxl[0] = o_ref[0].astype(BF16)
    fxh[0] = o_ref[nx - 1].astype(BF16)
    fyl[0] = s_fl[...].astype(BF16)
    fyh[0] = s_fh[...].astype(BF16)


def upwind(field, velocity, instant, field_halo, field_at, speed_halo, speed_at, name):
    nx, ny, nz = field.shape
    lines = {"x": (1, ny, nz), "y": (1, nx, nz)}
    outs = [struct(field.shape, F32)] + [struct(lines[d], BF16) for d in "xxyy"]
    in_specs = (
        [whole(field.shape), pl.BlockSpec((1, 3, nx, ny, nz), lambda *_: (instant, 0, 0, 0, 0))]
        + [whole(h.shape) for h in field_halo]
        + [whole(h.shape) for h in speed_halo]
    )
    scratch = [pltpu.VMEM((nx, nz), F32)] * 6
    kernel = functools.partial(upwind_kernel, field_at, speed_at)
    return call(kernel, outs, scratch, name, in_specs)(field, velocity, *field_halo, *speed_halo)


def pick_kernel(planes, t_lo, t_own, t_hi, q_ref, *outs):
    nz = t_own.shape[2]
    ny = t_own.shape[1]
    blocks = []
    for ref in (t_lo, t_own, t_hi):
        parts = [ref[a:b].reshape((b - a) * ny, nz) for a, b in planes]
        blocks.append(parts[0] if len(parts) == 1 else jnp.concatenate(parts, axis=0))
    rows = jnp.concatenate(blocks, axis=1)
    count = rows.shape[0] // ny
    for d, out in enumerate(outs):
        got = jnp.dot(rows, q_ref[d], preferred_element_type=F32).astype(BF16)
        out[0] = got[:, :nz].reshape(count, ny, nz)
        out[1] = got[:, nz:].reshape(count, ny, nz)


def pick(columns, choices, planes, name):
    _, ny, nz = columns[0].shape
    count = sum(b - a for a, b in planes)
    outs = [struct((2, count, ny, nz), BF16)] * choices.shape[0]
    in_specs = [whole(c.shape) for c in columns] + [whole(choices.shape)]
    return call(functools.partial(pick_kernel, planes), outs, [], name, in_specs)(*columns, choices)


def edge_kernel(own, la, ra, lb, rb, xlo, xhi, first, last, s_first, s_last):
    _, nx, ny, nz = own.shape

    def put(x, cells):
        at = pl.ds(x, 1)
        for c in range(2):
            s_first[c, at, :] = cells[c : c + 1]
            s_last[c, at, :] = cells[ny - 2 + c : ny - 1 + c]

    put(0, xlo[0, 1].astype(F32))
    put(nx + 1, xhi[0, 0].astype(F32))
    for x, a in ((0, 0), (1, 1), (nx - 2, 2), (nx - 1, 3)):
        put(x + 1, (own[0, x] + la[0, a] + ra[0, a]).astype(F32))

    def step(x, carry):
        put(x + 3, (own[0, x + 2] + lb[0, x] + rb[0, x]).astype(F32))
        return carry

    lax.fori_loop(0, nx - 4, step, 0)
    first[...] = s_first[...].astype(BF16)
    last[...] = s_last[...].astype(BF16)


def at_instant(shape, instant):
    block = (1,) + tuple(shape[1:])
    return pl.BlockSpec(block, lambda *_: (instant,) + (0,) * (len(block) - 1))


def edges(instant, own, la, ra, lb, rb, xlo, xhi):
    _, nx, ny, nz = own.shape
    ins = (own, la, ra, lb, rb, xlo, xhi)
    in_specs = [at_instant(a.shape, instant if a.shape[0] == 2 else 0) for a in ins]
    outs = [struct((2, nx + 2, nz), BF16)] * 2
    scratch = [pltpu.VMEM((2, nx + 2, nz), F32)] * 2
    return call(edge_kernel, outs, scratch, f"edges_{instant}", in_specs)(*ins)


def force_kernel(
    has_old, own, la, ra, lb, rb, xlo, xhi, ylo, yhi, adj, axl, axh, ayl, ayh, vel, *rest
):
    out, img, frc, s_ylo, s_yhi, s_c0, s_c1, s_fl, s_fh, s_al, s_ah = rest[1:] if has_old else rest
    nx, ny, nz = adj.shape
    rows = lax.broadcasted_iota(jnp.int32, (ny, nz), 0)
    lanes = lax.broadcasted_iota(jnp.int32, (ny, nz), 1)

    def fill(x, cells):
        cells = cells.astype(F32)
        img[x + 2] = cells
        return cells

    def fill_inner(x, cells):
        cells = fill(x, cells)
        s_c0[pl.ds(x, 1), :] = cells[0:1]
        s_c1[pl.ds(x, 1), :] = cells[ny - 1 : ny]

    for h in range(2):
        fill(h - 2, xlo[0, h])
        fill(nx + h, xhi[0, h])
    for x, a in ((0, 0), (1, 1), (nx - 2, 2), (nx - 1, 3)):
        fill_inner(x, own[0, x] + la[0, a] + ra[0, a])

    def fill_step(x, carry):
        fill_inner(x + 2, own[0, x + 2] + lb[0, x] + rb[0, x])
        return carry

    lax.fori_loop(0, nx - 4, fill_step, 0)
    s_ylo[...] = ylo[...].astype(F32)
    s_yhi[...] = yhi[...].astype(F32)
    s_al[...] = ayl[0].astype(F32)
    s_ah[...] = ayh[0].astype(F32)

    def along_z(cells, index, length):
        after = jnp.where(index == length - 1, 0.0, pltpu.roll(cells, length - 1, cells.ndim - 1))
        before = jnp.where(index == 0, 0.0, pltpu.roll(cells, 1, cells.ndim - 1))
        return after, before

    def forces(x, half):
        cells = img[x + 2]
        at = pl.ds(x + 1, 1)
        frc[0, x + 1] = half * (img[x + 3] - img[x + 1])
        up = jnp.where(rows == ny - 1, s_yhi[0, at, :], pltpu.roll(cells, ny - 1, 0))
        down = jnp.where(rows == 0, s_ylo[1, at, :], pltpu.roll(cells, 1, 0))
        frc[1, x + 1] = half * (up - down)
        after, before = along_z(cells, lanes, nz)
        frc[2, x + 1] = half * (after - before)

    forces(-1, 0.5 * axl[0].astype(F32))
    forces(nx, 0.5 * axh[0].astype(F32))

    def force_step(x, carry):
        forces(x, 0.5 * adj[x])
        return carry

    lax.fori_loop(0, nx, force_step, 0)
    lines = lax.broadcasted_iota(jnp.int32, (nx, nz), 1)
    for cols, near, far, beside, half, dest, sign in (
        (s_ylo, 1, 0, s_c0, s_al, s_fl, 1.0),
        (s_yhi, 0, 1, s_c1, s_ah, s_fh, -1.0),
    ):
        weight = 0.5 * half[...]
        dest[0] = weight * (cols[near, 2 : nx + 2, :] - cols[near, 0:nx, :])
        dest[1] = (sign * weight) * (beside[...] - cols[far, 1 : nx + 1, :])
        after, before = along_z(cols[near, 1 : nx + 1, :], lines, nz)
        dest[2] = weight * (after - before)

    def smooth_step(x, carry):
        at = pl.ds(x, 1)
        for c in range(3):
            f = frc[c, x + 1]
            up = jnp.where(rows == ny - 1, s_fh[c, at, :], pltpu.roll(f, ny - 1, 0))
            down = jnp.where(rows == 0, s_fl[c, at, :], pltpu.roll(f, 1, 0))
            after, before = along_z(f, lanes, nz)
            beside = (frc[c, x] + frc[c, x + 2]) + (up + down) + (after + before)
            out[0, c, x] = vel[0, c, x].astype(F32) + (0.25 * f + 0.125 * beside)
        return carry

    lax.fori_loop(0, nx, smooth_step, 0)


def force(instant, own, la, ra, lb, rb, xlo, xhi, ylo, yhi, adj, adj_halo, velocity, old):
    nx, ny, nz = adj.shape
    ins = [own, la, ra, lb, rb, xlo, xhi]
    in_specs = [at_instant(a.shape, instant if a.shape[0] == 2 else 0) for a in ins]
    more = [ylo, yhi, adj, *adj_halo]
    in_specs += [whole(a.shape) for a in more]
    block = pl.BlockSpec((1, 3, nx, ny, nz), lambda *_: (instant, 0, 0, 0, 0))
    ins += more + [velocity]
    in_specs += [block]
    aliases = {}
    if old is not None:
        aliases = {len(ins): 0}
        ins += [old]
        in_specs += [pl.BlockSpec(memory_space=pl.ANY)]
    scratch = [
        pltpu.VMEM((nx + 4, ny, nz), F32),
        pltpu.VMEM((3, nx + 2, ny, nz), F32),
        pltpu.VMEM((2, nx + 2, nz), F32),
        pltpu.VMEM((2, nx + 2, nz), F32),
        pltpu.VMEM((nx, nz), F32),
        pltpu.VMEM((nx, nz), F32),
        pltpu.VMEM((3, nx, nz), F32),
        pltpu.VMEM((3, nx, nz), F32),
        pltpu.VMEM((nx, nz), F32),
        pltpu.VMEM((nx, nz), F32),
    ]
    return call(
        functools.partial(force_kernel, old is not None),
        struct((2, 3, nx, ny, nz), F32),
        scratch,
        f"force_{instant}",
        in_specs,
        aliases,
        block,
    )(*ins)


def forward(value, axis):
    ends = lax.axis_size(axis) - 1
    return lax.ppermute(value, axis, [(i, i + 1) for i in range(ends)])


def backward(value, axis):
    ends = lax.axis_size(axis) - 1
    return lax.ppermute(value, axis, [(i + 1, i) for i in range(ends)])


def after(value, *others):
    return lax.optimization_barrier((value,) + others)[0]


def body(template, mismatch, velocity, src_ids):
    nx, ny, nz = template.shape
    depth_blocks = src_ids.shape[3]
    edge = nz // depth_blocks
    index_first = lax.axis_index("gx")
    index_second = lax.axis_index("gy")
    count_second = lax.axis_size("gy")

    t_lo = forward(template, "gx")
    t_hi = backward(template, "gx")
    own_ids = src_ids.reshape(2, depth_blocks)
    left_ids = forward(own_ids, "gy")
    right_ids = backward(own_ids, "gy")

    def face_message(x, y):
        if x is not None:
            parts = [mismatch[x].astype(BF16), velocity[0, 0, x], velocity[1, 0, x]]
        else:
            parts = [mismatch[:, y].astype(BF16), velocity[0, 1, :, y], velocity[1, 1, :, y]]
        return jnp.stack(parts)

    halo = (
        forward(face_message(nx - 1, None), "gx"),
        backward(face_message(0, None), "gx"),
        forward(face_message(None, ny - 1), "gy"),
        backward(face_message(None, 0), "gy"),
    )

    def choice(ids):
        first_block = ids // (count_second * depth_blocks)
        second_block = ids // depth_blocks % count_second
        start = (first_block - index_first + 1) * nz + ids % depth_blocks * edge
        start = jnp.where(second_block == index_second, start, -4 * nz)
        rows = jnp.repeat(start.reshape(-1), edge) + jnp.tile(jnp.arange(edge), 2 * depth_blocks)
        return (jnp.arange(3 * nz)[:, None] == rows[None, :]).astype(BF16)

    send_choice = jnp.stack([choice(left_ids), choice(right_ids)])
    own_choice = choice(own_ids)[None]

    adj_one, *faces = upwind(mismatch, velocity, 1, halo, 0, halo, 2, "upwind_1")

    columns = (t_lo, template, t_hi)
    outer = ((0, 2), (nx - 2, nx))
    inner = ((2, nx - 2),)
    to_left_a, to_right_a = pick(columns, send_choice, outer, "pick_outer")
    from_left_a = forward(to_right_a, "gy")
    from_right_a = backward(to_left_a, "gy")
    to_left_b, to_right_b = pick(columns, send_choice, inner, "pick_inner")
    from_left_b = [forward(to_right_b[k : k + 1], "gy") for k in range(2)]
    from_right_b = [backward(to_left_b[k : k + 1], "gy") for k in range(2)]
    (own,) = pick(columns, own_choice, ((0, nx),), "pick_own")

    def exchange(faces):
        low_x, high_x, low_y, high_y = faces
        return (
            forward(high_x, "gx"),
            backward(low_x, "gx"),
            forward(high_y, "gy"),
            backward(low_y, "gy"),
        )

    adj_one_halo = exchange(faces)
    adj_zero, *faces = upwind(adj_one, velocity, 0, adj_one_halo, 0, halo, 1, "upwind_0")
    adj_zero_halo = exchange(faces)

    own_outer = jnp.concatenate([own[:, :2], own[:, nx - 2 :]], axis=1)
    outer_image = own_outer + from_left_a + from_right_a
    x_lo = forward(outer_image[:, 2:], "gx")
    x_hi = backward(outer_image[:, :2], "gx")

    result = None
    for k, adj, adj_halo in ((0, adj_zero, adj_zero_halo), (1, adj_one, adj_one_halo)):
        parts = (own, from_left_a, from_right_a, from_left_b[k], from_right_b[k], x_lo, x_hi)
        first, last = edges(k, *parts)
        y_lo = forward(last, "gy")
        y_hi = backward(first, "gy")
        result = force(k, *parts, y_lo, y_hi, adj, adj_halo, velocity, result)
    return result


def solution(mesh):
    in_specs = (
        P("gx", "gy", None),
        P("gx", "gy", None),
        P(None, None, "gx", "gy", None),
        P(None, "gx", "gy", None),
    )
    out_specs = P(None, None, "gx", "gy", None)
    return jax.shard_map(body, mesh=mesh, in_specs=in_specs, out_specs=out_specs, check_vma=False)
```

time: 323 us -> 205 us (0.63)
  local copies, waits for them, and re-layouts: 103 us -> 5.14 us
  Pallas kernels: 0 us -> 34.9 us
  other arithmetic: 29.7 us -> 2.26 us
  waiting for transfers between devices: 71.5 us -> 50 us
    gather x48 -> x0, local copies, waits for them, and re-layouts: 72.2 us -> none
    pallas_call x0 -> x9, Pallas kernels: none -> 34.9 us  [the longest x2 21.1 us: force(): call(functools.partial(force_kernel, old is not None), struct((2, 3, nx,...]
    ppermute x24 -> x28, waiting for transfers between devices: 71.5 us -> 50 us  [the longest x14 33.4 us: backward(): return lax.ppermute(value, axis, [(i + 1, i) for i in range(ends)])]
    add x7 -> x4, other arithmetic: 15.6 us -> 0.25 us  [the longest x3 0.22 us: choice(): jnp.repeat(start.reshape(-1), edge)]
    reshape x3, local copies, waits for them, and re-layouts: 15.3 us -> 0.25 us  [the longest x2 0.16 us: choice(): start.reshape(-1)]
    concatenate x3 -> x0, other arithmetic: 5.08 us -> none  [the longest x2 5.07 us: padded(): jnp.concatenate([lax.ppermute(tail, axis, [(i, (i + 1) % count) for i in...]
    unnamed x21 -> x10, local copies, waits for them, and re-layouts: 7.39 us -> 2.32 us
    another operation x4 -> x5, other arithmetic: 4.44 us -> 0.56 us  [the longest x1 0.3 us: body(): send_choice = jnp.stack([choice(left_ids), choice(right_ids)])]
  transfers between devices with their start and end apart: 24 -> 28, of which waited for: 9 -> 7; matrix products, arithmetic and copies ran while one was open for 8% -> 4% of each run, Pallas kernels for 0% -> 12%
where the time goes in v1:
time: 205 us; the launch traced here: 204 us
  starting transfers between devices  111 us (54%)
  waiting for transfers between devices  50 us (24%)
  Pallas kernels  34.9 us (17%)
  local copies, waits for them, and re-layouts  5.14 us (3%)
  other arithmetic  2.26 us (1%)
    ppermute x14, starting transfers between devices, backward(): return lax.ppermute(value, axis, [(i + 1, i) for i in range(ends)])  75.8 us
    ppermute x14, starting transfers between devices, forward(): return lax.ppermute(value, axis, [(i, i + 1) for i in range(ends)])  34.8 us
    ppermute x14, waiting for transfers between devices, backward(): return lax.ppermute(value, axis, [(i + 1, i) for i in range(ends)])  33.4 us
    pallas_call x2, Pallas kernels, force(): call(functools.partial(force_kernel, old is not None), struct((2, 3, nx,...  21.1 us
    ppermute x14, waiting for transfers between devices, forward(): return lax.ppermute(value, axis, [(i, i + 1) for i in range(ends)])  16.6 us
    pallas_call x2, Pallas kernels, upwind(): call(kernel, outs, scratch, name, in_specs)  10.2 us
  transfers between devices with their start and end apart: 28, of which 7 were waited for; matrix products, arithmetic and copies ran while one was open for 4% of the time, Pallas kernels for 12%

profile of v1, /device:TPU:26, one launch (start us, length us, event | category | flops | bytes accessed | tf_op | source)
XLA Modules:
  0.0 203.5 jit_solution(4781432757582893678)
XLA Ops:
  0.0 6.6 %collective-permute-start.3 = (s32[2,8]{1,0:T(2,128)}, s32[2,8]{1,0:T(2,128)S(1)}, u32[]{:S(2)}, u32[]{:S(2)}) collective-permute-start(s32[2,8]{1,0:T(2,128)} %bitcast.21), channel_id=1, source_target_pairs={{1,0},{2,1},{3,2},{4,3},{5,4},{6,5},{7,6},{8,7},{9,8},{10,9},{11,1... | collective-permute-start | bytes 200 | tf_op jit(solution)/shard_map/ppermute | solution.py:290
  8.6 5.7 %collective-permute-start.1 = (bf16[32,32,256]{2,1,0:T(8,128)(2,1)}, bf16[32,32,256]{2,1,0:T(8,128)(2,1)S(1)}, u32[]{:S(2)}, u32[]{:S(2)}) collective-permute-start(bf16[32,32,256]{2,1,0:T(8,128)(2,1)} %t_own.5), channel_id=1, source_target_pairs={{16,0},{32,16},{48,32},{64,48},{80,64},{96,80},{112,96},{128,112},... | collective-permute-start | bytes 1572872 | tf_op jit(solution)/shard_map/ppermute | solution.py:290
  19.3 2.8 %collective-permute-start.14 = (bf16[3,32,256]{2,1,0:T(8,128)(2,1)S(1)}, bf16[3,32,256]{2,1,0:T(8,128)(2,1)S(1)}, u32[]{:S(2)}, u32[]{:S(2)}) collective-permute-start(bf16[3,32,256]{2,1,0:T(8,128)(2,1)S(1)} %pad_maximum_fusion.2), channel_id=1, source_target_pairs={{0,1},{1,2},{2,3},{3,4},{4,5},{5,6},{6,7},{7,8},{8,9},{9,10},{10,1... | collective-permute-start | bytes 147464 | tf_op jit(solution)/shard_map/ppermute | solution.py:285
  25.1 5.8 %collective-permute-start.15 = (bf16[3,32,256]{2,1,0:T(8,128)(2,1)S(1)}, bf16[3,32,256]{2,1,0:T(8,128)(2,1)S(1)}, u32[]{:S(2)}, u32[]{:S(2)}) collective-permute-start(bf16[3,32,256]{2,1,0:T(8,128)(2,1)S(1)} %pad_maximum_fusion.3), channel_id=1, source_target_pairs={{1,0},{2,1},{3,2},{4,3},{5,4},{6,5},{7,6},{8,7},{9,8},{10,9},{11,1... | collective-permute-start | bytes 147464 | tf_op jit(solution)/shard_map/ppermute | solution.py:290
  31.1 2.7 %collective-permute-start.12 = (bf16[3,32,256]{2,0,1:T(4,128)(2,1)S(1)}, bf16[3,32,256]{2,0,1:T(4,128)(2,1)S(1)}, u32[]{:S(2)}, u32[]{:S(2)}) collective-permute-start(bf16[3,32,256]{2,0,1:T(4,128)(2,1)S(1)} %pad_maximum_fusion), channel_id=1, source_target_pairs={{0,16},{16,32},{32,48},{48,64},{64,80},{80,96},{96,112},{112,128},... | collective-permute-start | bytes 147464 | tf_op jit(solution)/shard_map/ppermute | solution.py:285
  34.6 8.5 %collective-permute-done.12 = bf16[3,32,256]{2,0,1:T(4,128)(2,1)S(1)} collective-permute-done((bf16[3,32,256]{2,0,1:T(4,128)(2,1)S(1)}, bf16[3,32,256]{2,0,1:T(4,128)(2,1)S(1)}, u32[]{:S(2)}, u32[]{:S(2)}) %collective-permute-start.12) | collective-permute-done | bytes 49184 | tf_op jit(solution)/shard_map/ppermute | solution.py:285
  46.9 5.1 %upwind_1.1 = (f32[32,32,256]{2,1,0:T(8,128)S(1)}, bf16[1,32,256]{2,1,0:T(8,128)(2,1)S(1)}, bf16[1,32,256]{2,1,0:T(8,128)(2,1)S(1)}, bf16[1,32,256]{2,1,0:T(8,128)(2,1)S(1)}, bf16[1,32,256]{2,1,0:T(8,128)(2,1)S(1)}) custom-call(f32[32,32,256]{2,1,0:T(8,128)S(1)} %copy-done.2, bf16[2,3,32,32,256]{4,3,2,1,0:T(8,128)(2,1)S(1)} %copy-done, ...), custom_call_target="tpu_custom_call" | custom-call | tf_op jit(solution)/shard_map/upwind_1/pallas_call | solution.py:101
  54.0 8.5 %collective-permute-start.17 = (bf16[1,32,256]{2,1,0:T(8,128)(2,1)S(1)}, bf16[1,32,256]{2,1,0:T(8,128)(2,1)S(1)}, u32[]{:S(2)}, u32[]{:S(2)}) collective-permute-start(bf16[1,32,256]{2,1,0:T(8,128)(2,1)S(1)} %get-tuple-element.31), channel_id=1, source_target_pairs={{16,0},{32,16},{48,32},{64,48},{80,64},{96,80},{112,96},{128,112},... | collective-permute-start | bytes 49160 | tf_op jit(solution)/shard_map/ppermute | solution.py:290
  62.5 5.3 %collective-permute-start.18 = (bf16[1,32,256]{2,1,0:T(8,128)(2,1)S(1)}, bf16[1,32,256]{2,1,0:T(8,128)(2,1)S(1)}, u32[]{:S(2)}, u32[]{:S(2)}) collective-permute-start(bf16[1,32,256]{2,1,0:T(8,128)(2,1)S(1)} %get-tuple-element.32), channel_id=1, source_target_pairs={{0,1},{1,2},{2,3},{3,4},{4,5},{5,6},{6,7},{7,8},{8,9},{9,10},{10,1... | collective-permute-start | bytes 49160 | tf_op jit(solution)/shard_map/ppermute | solution.py:285
  71.8 6.6 %collective-permute-start.5 = (bf16[2,4,32,256]{3,2,1,0:T(8,128)(2,1)S(1)}, bf16[2,4,32,256]{3,2,1,0:T(8,128)(2,1)S(1)}, u32[]{:S(2)}, u32[]{:S(2)}) collective-permute-start(bf16[2,4,32,256]{3,2,1,0:T(8,128)(2,1)S(1)} %get-tuple-element.24), channel_id=1, source_target_pairs={{1,0},{2,1},{3,2},{4,3},{5,4},{6,5},{7,6},{8,7},{9,8},{10,9},{11,1... | collective-permute-start | bytes 393224 | tf_op jit(solution)/shard_map/ppermute | solution.py:290
  81.5 2.6 %collective-permute-start.6 = (bf16[1,28,32,256]{3,2,1,0:T(8,128)(2,1)S(1)}, bf16[1,28,32,256]{3,2,1,0:T(8,128)(2,1)S(1)}, u32[]{:S(2)}, u32[]{:S(2)}) collective-permute-start(bf16[1,28,32,256]{3,2,1,0:T(8,128)(2,1)S(1)} %get-tuple-element.54), channel_id=1, source_target_pairs={{0,1},{1,2},{2,3},{3,4},{4,5},{5,6},{6,7},{7,8},{8,9},{9,10},{10,1... | collective-permute-start | bytes 1376264 | tf_op jit(solution)/shard_map/ppermute | solution.py:285
  84.1 6.0 %collective-permute-start.21 = (bf16[1,28,32,256]{3,2,1,0:T(8,128)(2,1)S(1)}, bf16[1,28,32,256]{3,2,1,0:T(8,128)(2,1)S(1)}, u32[]{:S(2)}, u32[]{:S(2)}) collective-permute-start(bf16[1,28,32,256]{3,2,1,0:T(8,128)(2,1)S(1)} %get-tuple-element.51), channel_id=1, source_target_pairs={{1,0},{2,1},{3,2},{4,3},{5,4},{6,5},{7,6},{8,7},{9,8},{10,9},{11,1... | collective-permute-start | bytes 1376264 | tf_op jit(solution)/shard_map/ppermute | solution.py:290
  90.0 3.9 %collective-permute-start.7 = (bf16[1,28,32,256]{3,2,1,0:T(8,128)(2,1)S(1)}, bf16[1,28,32,256]{3,2,1,0:T(8,128)(2,1)S(1)}, u32[]{:S(2)}, u32[]{:S(2)}) collective-permute-start(bf16[1,28,32,256]{3,2,1,0:T(8,128)(2,1)S(1)} %get-tuple-element.52), channel_id=1, source_target_pairs={{1,0},{2,1},{3,2},{4,3},{5,4},{6,5},{7,6},{8,7},{9,8},{10,9},{11,1... | collective-permute-start | bytes 1376264 | tf_op jit(solution)/shard_map/ppermute | solution.py:290
  96.0 26.2 %collective-permute-done.19.pyh.ayh = bf16[1,32,256]{2,1,0:T(8,128)(2,1)S(1)} collective-permute-done((bf16[1,32,256]{2,1,0:T(8,128)(2,1)S(1)}, bf16[1,32,256]{2,1,0:T(8,128)(2,1)S(1)}, u32[]{:S(2)}, u32[]{:S(2)}) %collective-permute-start.19) | collective-permute-done | bytes 16416 | tf_op jit(solution)/shard_map/ppermute | solution.py:290
  122.2 5.8 %collective-permute-start.9 = (bf16[2,2,32,256]{3,2,1,0:T(8,128)(2,1)S(1)}, bf16[2,2,32,256]{3,2,1,0:T(8,128)(2,1)S(1)}, u32[]{:S(2)}, u32[]{:S(2)}) collective-permute-start(bf16[2,2,32,256]{3,2,1,0:T(8,128)(2,1)S(1)} %get-tuple-element.59), channel_id=1, source_target_pairs={{16,0},{32,16},{48,32},{64,48},{80,64},{96,80},{112,96},{128,112},... | collective-permute-start | bytes 196616 | tf_op jit(solution)/shard_map/ppermute | solution.py:290
  129.9 3.6 %collective-permute-start.8 = (bf16[2,2,32,256]{3,2,1,0:T(8,128)(2,1)S(1)}, bf16[2,2,32,256]{3,2,1,0:T(8,128)(2,1)S(1)}, u32[]{:S(2)}, u32[]{:S(2)}) collective-permute-start(bf16[2,2,32,256]{3,2,1,0:T(8,128)(2,1)S(1)} %get-tuple-element.60), channel_id=1, source_target_pairs={{0,16},{16,32},{32,48},{48,64},{64,80},{80,96},{96,112},{112,128},... | collective-permute-start | bytes 196616 | tf_op jit(solution)/shard_map/ppermute | solution.py:285
  133.5 5.1 %upwind_0.1 = (f32[32,32,256]{2,1,0:T(8,128)S(1)}, bf16[1,32,256]{2,1,0:T(8,128)(2,1)S(1)}, bf16[1,32,256]{2,1,0:T(8,128)(2,1)S(1)}, bf16[1,32,256]{2,1,0:T(8,128)(2,1)S(1)}, bf16[1,32,256]{2,1,0:T(8,128)(2,1)S(1)}) custom-call(f32[32,32,256]{2,1,0:T(8,128)S(1)} %get-tuple-element.29.p_ref.adj, bf16[2,3,32,32,256]{4,3,2,1,0:T(8,128)(2,1)S(1)} %copy-done, ...), custom_call_target="tpu_custom_call" | custom-call | tf_op jit(solution)/shard_map/upwind_0/pallas_call | solution.py:101
  142.2 8.4 %collective-permute-start.25 = (bf16[1,32,256]{2,1,0:T(8,128)(2,1)S(1)}, bf16[1,32,256]{2,1,0:T(8,128)(2,1)S(1)}, u32[]{:S(2)}, u32[]{:S(2)}) collective-permute-start(bf16[1,32,256]{2,1,0:T(8,128)(2,1)S(1)} %get-tuple-element.38), channel_id=1, source_target_pairs={{16,0},{32,16},{48,32},{64,48},{80,64},{96,80},{112,96},{128,112},... | collective-permute-start | bytes 49160 | tf_op jit(solution)/shard_map/ppermute | solution.py:290
  153.5 6.0 %collective-permute-start.23 = (bf16[2,34,256]{2,1,0:T(8,128)(2,1)S(1)}, bf16[2,34,256]{2,1,0:T(8,128)(2,1)S(1)}, u32[]{:S(2)}, u32[]{:S(2)}) collective-permute-start(bf16[2,34,256]{2,1,0:T(8,128)(2,1)S(1)} %get-tuple-element.35), channel_id=1, source_target_pairs={{1,0},{2,1},{3,2},{4,3},{5,4},{6,5},{7,6},{8,7},{9,8},{10,9},{11,1... | collective-permute-start | bytes 104456 | tf_op jit(solution)/shard_map/ppermute | solution.py:290
  161.8 6.6 %collective-permute-start.11 = (bf16[2,34,256]{2,1,0:T(8,128)(2,1)S(1)}, bf16[2,34,256]{2,1,0:T(8,128)(2,1)S(1)}, u32[]{:S(2)}, u32[]{:S(2)}) collective-permute-start(bf16[2,34,256]{2,1,0:T(8,128)(2,1)S(1)} %get-tuple-element.28), channel_id=1, source_target_pairs={{1,0},{2,1},{3,2},{4,3},{5,4},{6,5},{7,6},{8,7},{9,8},{10,9},{11,1... | collective-permute-start | bytes 104456 | tf_op jit(solution)/shard_map/ppermute | solution.py:290
  170.4 6.4 %collective-permute-done.26.ayl = bf16[1,32,256]{2,1,0:T(8,128)(2,1)S(1)} collective-permute-done((bf16[1,32,256]{2,1,0:T(8,128)(2,1)S(1)}, bf16[1,32,256]{2,1,0:T(8,128)(2,1)S(1)}, u32[]{:S(2)}, u32[]{:S(2)}) %collective-permute-start.26) | collective-permute-done | bytes 16416 | tf_op jit(solution)/shard_map/ppermute | solution.py:285
  178.7 3.7 %collective-permute-done.27.ayh = bf16[1,32,256]{2,1,0:T(8,128)(2,1)S(1)} collective-permute-done((bf16[1,32,256]{2,1,0:T(8,128)(2,1)S(1)}, bf16[1,32,256]{2,1,0:T(8,128)(2,1)S(1)}, u32[]{:S(2)}, u32[]{:S(2)}) %collective-permute-start.27) | collective-permute-done | bytes 16416 | tf_op jit(solution)/shard_map/ppermute | solution.py:290
  182.4 10.5 %force_0.1.rest_0_ = f32[2,3,32,32,256]{4,3,2,1,0:T(8,128)} custom-call(bf16[2,32,32,256]{3,2,1,0:T(8,128)(2,1)S(1)} %pick_own.1.own, bf16[2,4,32,256]{3,2,1,0:T(8,128)(2,1)S(1)} %collective-permute-done.4.la, bf16[2,4,32,256]{3,2,1,0:T(8,128)(2,1)S(1)} %collective-permute-done.5.ra, bf16[1,28,32,256]{3,2,1,0:T(8,128)(2,1)S(1)} %collective-permute-done.20.lb, ...), custom_call_target="tpu_custom_call" | custom-call | tf_op jit(solution)/shard_map/force_0/pallas_call | solution.py:272
  193.0 10.5 %force_1.1 = f32[2,3,32,32,256]{4,3,2,1,0:T(8,128)} custom-call(bf16[2,32,32,256]{3,2,1,0:T(8,128)(2,1)S(1)} %pick_own.1.own, bf16[2,4,32,256]{3,2,1,0:T(8,128)(2,1)S(1)} %collective-permute-done.4.la, bf16[2,4,32,256]{3,2,1,0:T(8,128)(2,1)S(1)} %collective-permute-done.5.ra, ...), custom_call_target="tpu_custom_call", output_to_operand_aliasing={{}: (15, {})} | custom-call | tf_op jit(solution)/shard_map/force_1/pallas_call | solution.py:272
  (88 shorter events, 39.8 us)
Async XLA Ops:
  0.0 25.1 %collective-permute-start.3 = (s32[2,8]{1,0:T(2,128)}, s32[2,8]{1,0:T(2,128)S(1)}, u32[]{:S(2)}, u32[]{:S(2)}) collective-permute-start(s32[2,8]{1,0:T(2,128)} %bitcast.21), channel_id=1, source_target_pairs={{1,0},{2,1},{3,2},{4,3},{5,4},{6,5},{7,6},{8,7},{9,8},{10,9},{11,1... | collective-permute-start | bytes 200 | tf_op jit(solution)/shard_map/ppermute | solution.py:290
  6.6 24.5 %collective-permute-start.2 = (s32[2,8]{1,0:T(2,128)}, s32[2,8]{1,0:T(2,128)S(1)}, u32[]{:S(2)}, u32[]{:S(2)}) collective-permute-start(s32[2,8]{1,0:T(2,128)} %bitcast.22), channel_id=1, source_target_pairs={{0,1},{1,2},{2,3},{3,4},{4,5},{5,6},{6,7},{7,8},{8,9},{9,10},{10,1... | collective-permute-start | bytes 200 | tf_op jit(solution)/shard_map/ppermute | solution.py:285
  8.6 59.2 %collective-permute-start.1 = (bf16[32,32,256]{2,1,0:T(8,128)(2,1)}, bf16[32,32,256]{2,1,0:T(8,128)(2,1)S(1)}, u32[]{:S(2)}, u32[]{:S(2)}) collective-permute-start(bf16[32,32,256]{2,1,0:T(8,128)(2,1)} %t_own.5), channel_id=1, source_target_pairs={{16,0},{32,16},{48,32},{64,48},{80,64},{96,80},{112,96},{128,112},... | collective-permute-start | bytes 1572872 | tf_op jit(solution)/shard_map/ppermute | solution.py:290
  14.3 53.5 %collective-permute-start = (bf16[32,32,256]{2,1,0:T(8,128)(2,1)}, bf16[32,32,256]{2,1,0:T(8,128)(2,1)S(1)}, u32[]{:S(2)}, u32[]{:S(2)}) collective-permute-start(bf16[32,32,256]{2,1,0:T(8,128)(2,1)} %t_own.5), channel_id=1, source_target_pairs={{0,16},{16,32},{32,48},{48,64},{64,80},{80,96},{96,112},{112,128},... | collective-permute-start | bytes 1572872 | tf_op jit(solution)/shard_map/ppermute | solution.py:285
  19.3 27.6 %collective-permute-start.14 = (bf16[3,32,256]{2,1,0:T(8,128)(2,1)S(1)}, bf16[3,32,256]{2,1,0:T(8,128)(2,1)S(1)}, u32[]{:S(2)}, u32[]{:S(2)}) collective-permute-start(bf16[3,32,256]{2,1,0:T(8,128)(2,1)S(1)} %pad_maximum_fusion.2), channel_id=1, source_target_pairs={{0,1},{1,2},{2,3},{3,4},{4,5},{5,6},{6,7},{7,8},{8,9},{9,10},{10,1... | collective-permute-start | bytes 147464 | tf_op jit(solution)/shard_map/ppermute | solution.py:285
  25.1 21.8 %collective-permute-start.15 = (bf16[3,32,256]{2,1,0:T(8,128)(2,1)S(1)}, bf16[3,32,256]{2,1,0:T(8,128)(2,1)S(1)}, u32[]{:S(2)}, u32[]{:S(2)}) collective-permute-start(bf16[3,32,256]{2,1,0:T(8,128)(2,1)S(1)} %pad_maximum_fusion.3), channel_id=1, source_target_pairs={{1,0},{2,1},{3,2},{4,3},{5,4},{6,5},{7,6},{8,7},{9,8},{10,9},{11,1... | collective-permute-start | bytes 147464 | tf_op jit(solution)/shard_map/ppermute | solution.py:290
  31.1 11.9 %collective-permute-start.12 = (bf16[3,32,256]{2,0,1:T(4,128)(2,1)S(1)}, bf16[3,32,256]{2,0,1:T(4,128)(2,1)S(1)}, u32[]{:S(2)}, u32[]{:S(2)}) collective-permute-start(bf16[3,32,256]{2,0,1:T(4,128)(2,1)S(1)} %pad_maximum_fusion), channel_id=1, source_target_pairs={{0,16},{16,32},{32,48},{48,64},{64,80},{80,96},{96,112},{112,128},... | collective-permute-start | bytes 147464 | tf_op jit(solution)/shard_map/ppermute | solution.py:285
  52.1 27.5 %collective-permute-start.16 = (bf16[1,32,256]{2,1,0:T(8,128)(2,1)S(1)}, bf16[1,32,256]{2,1,0:T(8,128)(2,1)S(1)}, u32[]{:S(2)}, u32[]{:S(2)}) collective-permute-start(bf16[1,32,256]{2,1,0:T(8,128)(2,1)S(1)} %get-tuple-element.30), channel_id=1, source_target_pairs={{0,16},{16,32},{32,48},{48,64},{64,80},{80,96},{96,112},{112,128},... | collective-permute-start | bytes 49160 | tf_op jit(solution)/shard_map/ppermute | solution.py:285
  54.0 27.5 %collective-permute-start.17 = (bf16[1,32,256]{2,1,0:T(8,128)(2,1)S(1)}, bf16[1,32,256]{2,1,0:T(8,128)(2,1)S(1)}, u32[]{:S(2)}, u32[]{:S(2)}) collective-permute-start(bf16[1,32,256]{2,1,0:T(8,128)(2,1)S(1)} %get-tuple-element.31), channel_id=1, source_target_pairs={{16,0},{32,16},{48,32},{64,48},{80,64},{96,80},{112,96},{128,112},... | collective-permute-start | bytes 49160 | tf_op jit(solution)/shard_map/ppermute | solution.py:290
  62.5 31.5 %collective-permute-start.18 = (bf16[1,32,256]{2,1,0:T(8,128)(2,1)S(1)}, bf16[1,32,256]{2,1,0:T(8,128)(2,1)S(1)}, u32[]{:S(2)}, u32[]{:S(2)}) collective-permute-start(bf16[1,32,256]{2,1,0:T(8,128)(2,1)S(1)} %get-tuple-element.32), channel_id=1, source_target_pairs={{0,1},{1,2},{2,3},{3,4},{4,5},{5,6},{6,7},{7,8},{8,9},{9,10},{10,1... | collective-permute-start | bytes 49160 | tf_op jit(solution)/shard_map/ppermute | solution.py:285
  69.9 14.2 %collective-permute-start.4 = (bf16[2,4,32,256]{3,2,1,0:T(8,128)(2,1)S(1)}, bf16[2,4,32,256]{3,2,1,0:T(8,128)(2,1)S(1)}, u32[]{:S(2)}, u32[]{:S(2)}) collective-permute-start(bf16[2,4,32,256]{3,2,1,0:T(8,128)(2,1)S(1)} %get-tuple-element.23), channel_id=1, source_target_pairs={{0,1},{1,2},{2,3},{3,4},{4,5},{5,6},{6,7},{7,8},{8,9},{9,10},{10,1... | collective-permute-start | bytes 393224 | tf_op jit(solution)/shard_map/ppermute | solution.py:285
  71.8 18.2 %collective-permute-start.5 = (bf16[2,4,32,256]{3,2,1,0:T(8,128)(2,1)S(1)}, bf16[2,4,32,256]{3,2,1,0:T(8,128)(2,1)S(1)}, u32[]{:S(2)}, u32[]{:S(2)}) collective-permute-start(bf16[2,4,32,256]{3,2,1,0:T(8,128)(2,1)S(1)} %get-tuple-element.24), channel_id=1, source_target_pairs={{1,0},{2,1},{3,2},{4,3},{5,4},{6,5},{7,6},{8,7},{9,8},{10,9},{11,1... | collective-permute-start | bytes 393224 | tf_op jit(solution)/shard_map/ppermute | solution.py:290
  79.5 62.7 %collective-permute-start.20 = (bf16[1,28,32,256]{3,2,1,0:T(8,128)(2,1)S(1)}, bf16[1,28,32,256]{3,2,1,0:T(8,128)(2,1)S(1)}, u32[]{:S(2)}, u32[]{:S(2)}) collective-permute-start(bf16[1,28,32,256]{3,2,1,0:T(8,128)(2,1)S(1)} %get-tuple-element.53), channel_id=1, source_target_pairs={{0,1},{1,2},{2,3},{3,4},{4,5},{5,6},{6,7},{7,8},{8,9},{9,10},{10,1... | collective-permute-start | bytes 1376264 | tf_op jit(solution)/shard_map/ppermute | solution.py:285
  81.5 72.1 %collective-permute-start.6 = (bf16[1,28,32,256]{3,2,1,0:T(8,128)(2,1)S(1)}, bf16[1,28,32,256]{3,2,1,0:T(8,128)(2,1)S(1)}, u32[]{:S(2)}, u32[]{:S(2)}) collective-permute-start(bf16[1,28,32,256]{3,2,1,0:T(8,128)(2,1)S(1)} %get-tuple-element.54), channel_id=1, source_target_pairs={{0,1},{1,2},{2,3},{3,4},{4,5},{5,6},{6,7},{7,8},{8,9},{9,10},{10,1... | collective-permute-start | bytes 1376264 | tf_op jit(solution)/shard_map/ppermute | solution.py:285
  84.1 66.6 %collective-permute-start.21 = (bf16[1,28,32,256]{3,2,1,0:T(8,128)(2,1)S(1)}, bf16[1,28,32,256]{3,2,1,0:T(8,128)(2,1)S(1)}, u32[]{:S(2)}, u32[]{:S(2)}) collective-permute-start(bf16[1,28,32,256]{3,2,1,0:T(8,128)(2,1)S(1)} %get-tuple-element.51), channel_id=1, source_target_pairs={{1,0},{2,1},{3,2},{4,3},{5,4},{6,5},{7,6},{8,7},{9,8},{10,9},{11,1... | collective-permute-start | bytes 1376264 | tf_op jit(solution)/shard_map/ppermute | solution.py:290
  90.0 69.5 %collective-permute-start.7 = (bf16[1,28,32,256]{3,2,1,0:T(8,128)(2,1)S(1)}, bf16[1,28,32,256]{3,2,1,0:T(8,128)(2,1)S(1)}, u32[]{:S(2)}, u32[]{:S(2)}) collective-permute-start(bf16[1,28,32,256]{3,2,1,0:T(8,128)(2,1)S(1)} %get-tuple-element.52), channel_id=1, source_target_pairs={{1,0},{2,1},{3,2},{4,3},{5,4},{6,5},{7,6},{8,7},{9,8},{10,9},{11,1... | collective-permute-start | bytes 1376264 | tf_op jit(solution)/shard_map/ppermute | solution.py:290
  94.0 28.2 %collective-permute-start.19 = (bf16[1,32,256]{2,1,0:T(8,128)(2,1)S(1)}, bf16[1,32,256]{2,1,0:T(8,128)(2,1)S(1)}, u32[]{:S(2)}, u32[]{:S(2)}) collective-permute-start(bf16[1,32,256]{2,1,0:T(8,128)(2,1)S(1)} %get-tuple-element.33), channel_id=1, source_target_pairs={{1,0},{2,1},{3,2},{4,3},{5,4},{6,5},{7,6},{8,7},{9,8},{10,9},{11,1... | collective-permute-start | bytes 49160 | tf_op jit(solution)/shard_map/ppermute | solution.py:290
  129.9 10.4 %collective-permute-start.8 = (bf16[2,2,32,256]{3,2,1,0:T(8,128)(2,1)S(1)}, bf16[2,2,32,256]{3,2,1,0:T(8,128)(2,1)S(1)}, u32[]{:S(2)}, u32[]{:S(2)}) collective-permute-start(bf16[2,2,32,256]{3,2,1,0:T(8,128)(2,1)S(1)} %get-tuple-element.60), channel_id=1, source_target_pairs={{0,16},{16,32},{32,48},{48,64},{64,80},{80,96},{96,112},{112,128},... | collective-permute-start | bytes 196616 | tf_op jit(solution)/shard_map/ppermute | solution.py:285
  140.3 21.5 %collective-permute-start.24 = (bf16[1,32,256]{2,1,0:T(8,128)(2,1)S(1)}, bf16[1,32,256]{2,1,0:T(8,128)(2,1)S(1)}, u32[]{:S(2)}, u32[]{:S(2)}) collective-permute-start(bf16[1,32,256]{2,1,0:T(8,128)(2,1)S(1)} %get-tuple-element.37), channel_id=1, source_target_pairs={{0,16},{16,32},{32,48},{48,64},{64,80},{80,96},{96,112},{112,128},... | collective-permute-start | bytes 49160 | tf_op jit(solution)/shard_map/ppermute | solution.py:285
  142.2 26.2 %collective-permute-start.25 = (bf16[1,32,256]{2,1,0:T(8,128)(2,1)S(1)}, bf16[1,32,256]{2,1,0:T(8,128)(2,1)S(1)}, u32[]{:S(2)}, u32[]{:S(2)}) collective-permute-start(bf16[1,32,256]{2,1,0:T(8,128)(2,1)S(1)} %get-tuple-element.38), channel_id=1, source_target_pairs={{16,0},{32,16},{48,32},{64,48},{80,64},{96,80},{112,96},{128,112},... | collective-permute-start | bytes 49160 | tf_op jit(solution)/shard_map/ppermute | solution.py:290
  151.0 31.4 %collective-permute-start.22 = (bf16[2,34,256]{2,1,0:T(8,128)(2,1)S(1)}, bf16[2,34,256]{2,1,0:T(8,128)(2,1)S(1)}, u32[]{:S(2)}, u32[]{:S(2)}) collective-permute-start(bf16[2,34,256]{2,1,0:T(8,128)(2,1)S(1)} %get-tuple-element.34), channel_id=1, source_target_pairs={{0,1},{1,2},{2,3},{3,4},{4,5},{5,6},{6,7},{7,8},{8,9},{9,10},{10,1... | collective-permute-start | bytes 104456 | tf_op jit(solution)/shard_map/ppermute | solution.py:285
  153.5 28.9 %collective-permute-start.23 = (bf16[2,34,256]{2,1,0:T(8,128)(2,1)S(1)}, bf16[2,34,256]{2,1,0:T(8,128)(2,1)S(1)}, u32[]{:S(2)}, u32[]{:S(2)}) collective-permute-start(bf16[2,34,256]{2,1,0:T(8,128)(2,1)S(1)} %get-tuple-element.35), channel_id=1, source_target_pairs={{1,0},{2,1},{3,2},{4,3},{5,4},{6,5},{7,6},{8,7},{9,8},{10,9},{11,1... | collective-permute-start | bytes 104456 | tf_op jit(solution)/shard_map/ppermute | solution.py:290
  159.9 33.1 %collective-permute-start.10 = (bf16[2,34,256]{2,1,0:T(8,128)(2,1)S(1)}, bf16[2,34,256]{2,1,0:T(8,128)(2,1)S(1)}, u32[]{:S(2)}, u32[]{:S(2)}) collective-permute-start(bf16[2,34,256]{2,1,0:T(8,128)(2,1)S(1)} %get-tuple-element.27), channel_id=1, source_target_pairs={{0,1},{1,2},{2,3},{3,4},{4,5},{5,6},{6,7},{7,8},{8,9},{9,10},{10,1... | collective-permute-start | bytes 104456 | tf_op jit(solution)/shard_map/ppermute | solution.py:285
  161.8 31.1 %collective-permute-start.11 = (bf16[2,34,256]{2,1,0:T(8,128)(2,1)S(1)}, bf16[2,34,256]{2,1,0:T(8,128)(2,1)S(1)}, u32[]{:S(2)}, u32[]{:S(2)}) collective-permute-start(bf16[2,34,256]{2,1,0:T(8,128)(2,1)S(1)} %get-tuple-element.28), channel_id=1, source_target_pairs={{1,0},{2,1},{3,2},{4,3},{5,4},{6,5},{7,6},{8,7},{9,8},{10,9},{11,1... | collective-permute-start | bytes 104456 | tf_op jit(solution)/shard_map/ppermute | solution.py:290
  (8 other events, 105.1 us)

commit v2 on v1

v2 whole, which is shorter than its diff:
```python
import functools

import jax
import jax.numpy as jnp
from jax import lax
from jax.experimental import pallas as pl
from jax.experimental.pallas import tpu as pltpu
from jax.sharding import PartitionSpec as P

F32 = jnp.float32
BF16 = jnp.bfloat16
VMEM_LIMIT = 48 << 20


def whole(shape):
    return pl.BlockSpec(shape, lambda *_: (0,) * len(shape))


def call(kernel, outs, scratch, name, in_specs, out_specs=None, steps=1):
    return pl.pallas_call(
        kernel,
        name=name,
        grid=(steps,),
        in_specs=in_specs,
        out_specs=out_specs or [whole(o.shape) for o in outs],
        out_shape=outs,
        scratch_shapes=scratch,
        cost_estimate=pl.CostEstimate(flops=0, transcendentals=0, bytes_accessed=0),
        compiler_params=pltpu.CompilerParams(vmem_limit_bytes=VMEM_LIMIT),
    )


def struct(shape, dtype):
    return jax.ShapeDtypeStruct(shape, dtype)


def face_flux(here, following, speed_here, speed_following):
    total = speed_here + speed_following
    return jnp.minimum(total, 0.0) * here + jnp.maximum(total, 0.0) * following


def depth_change(p, vz):
    nz = p.shape[1]
    lanes = lax.broadcasted_iota(jnp.int32, p.shape, 1)
    p_up = jnp.where(lanes == nz - 1, 0.0, pltpu.roll(p, nz - 1, 1))
    v_up = jnp.where(lanes == nz - 1, 0.0, pltpu.roll(vz, nz - 1, 1))
    upper = face_flux(p, p_up, vz, v_up)
    lower = jnp.where(lanes == 0, jnp.maximum(vz, 0.0) * p, pltpu.roll(upper, 1, 1))
    return upper - lower


def plane_change(p, vy, vz, below, above):
    ny = p.shape[0]
    rows = lax.broadcasted_iota(jnp.int32, p.shape, 0)
    p_up = jnp.where(rows == ny - 1, above[0], pltpu.roll(p, ny - 1, 0))
    v_up = jnp.where(rows == ny - 1, above[1], pltpu.roll(vy, ny - 1, 0))
    upper = face_flux(p, p_up, vy, v_up)
    first = face_flux(below[0], p[0:1], below[1], vy[0:1])
    lower = jnp.where(rows == 0, first, pltpu.roll(upper, 1, 0))
    return (upper - lower) + depth_change(p, vz)


NEAR_P, FAR_P, NEAR_N, FAR_N, NEAR_T, NEAR_Z, NEAR_EARLY = range(7)


def rows_kernel(p_ref, v_ref, hxl, hxh, code, lo, hi, s_lo, s_hi):
    nx, ny, _ = p_ref.shape
    s_lo[...] = jnp.zeros(s_lo.shape, F32)
    s_hi[...] = jnp.zeros(s_hi.shape, F32)

    def put(layer, x, cells, width):
        at = pl.ds(x + 1, 1)
        for d in range(width):
            s_lo[layer + d, at, :] = cells[d : d + 1]
            s_hi[layer + d, at, :] = cells[ny - 1 - d : ny - d]

    def step(x, carry):
        put(NEAR_P, x, p_ref[x], 2)
        put(NEAR_N, x, v_ref[1, 1, x].astype(F32), 2)
        put(NEAR_T, x, v_ref[1, 0, x].astype(F32), 1)
        put(NEAR_Z, x, v_ref[1, 2, x].astype(F32), 1)
        put(NEAR_EARLY, x, v_ref[0, 1, x].astype(F32), 1)
        return carry

    lax.fori_loop(0, nx, step, 0)
    for x, halo in ((-1, hxl), (nx, hxh)):
        put(NEAR_P, x, halo[NEAR_P].astype(F32), 1)
        put(NEAR_N, x, halo[NEAR_T].astype(F32), 1)
        put(NEAR_T, x, halo[NEAR_N].astype(F32), 1)
    s_lo[FAR_P, 0:1, :] = code[...]
    s_hi[FAR_P, 0:1, :] = code[...]
    lo[...] = s_lo[...].astype(BF16)
    hi[...] = s_hi[...].astype(BF16)


def upwind_one_kernel(
    inside, p_ref, v_ref, hxl, hxh, hyl, hyh, out, oxl, oxh, oyl, oyh,
    s_yl, s_yh, s_p0, s_p1, s_v0, s_v1,
):
    nx, ny, nz = p_ref.shape
    s_yl[...] = hyl[...].astype(F32)
    s_yh[...] = hyh[...].astype(F32)

    def plane(x, flux_below, p, speeds, p_next, vx_next):
        vx, vy, vz = speeds
        flux_above = face_flux(p, p_next, vx, vx_next)
        at = pl.ds(x + 1, 1)
        below = s_yl[NEAR_P, at, :], s_yl[NEAR_N, at, :]
        above = s_yh[NEAR_P, at, :], s_yh[NEAR_N, at, :]
        change = (flux_above - flux_below) + plane_change(p, vy, vz, below, above)
        return p + 0.5 * change, flux_above

    def speed(c, x):
        return v_ref[0, c, x].astype(F32)

    def halo_plane(halo):
        return [halo[i].astype(F32) for i in (NEAR_P, FAR_P, NEAR_N, FAR_N, NEAR_T, NEAR_Z)]

    p, p_far, vx, vx_far, vy, vz = halo_plane(hxl)
    flux = face_flux(p_far, p, vx_far, vx)
    got, flux = plane(-1, flux, p, (vx, vy, vz), p_ref[0], speed(0, 0))
    oxl[...] = got * inside[0]
    p_high, p_far, vx_high, vx_far, vy_high, vz_high = halo_plane(hxh)

    def inner(x, flux, p_next, vx_next):
        p = p_ref[x]
        vy = speed(1, x)
        got, flux = plane(x, flux, p, (speed(0, x), vy, speed(2, x)), p_next, vx_next)
        out[x] = got
        at = pl.ds(x, 1)
        s_p0[at, :] = p[0:1]
        s_p1[at, :] = p[ny - 1 : ny]
        s_v0[at, :] = vy[0:1]
        s_v1[at, :] = vy[ny - 1 : ny]
        return flux

    flux = lax.fori_loop(0, nx - 1, lambda x, f: inner(x, f, p_ref[x + 1], speed(0, x + 1)), flux)
    flux = inner(nx - 1, flux, p_high, vx_high)
    got, _ = plane(nx, flux, p_high, (vx_high, vy_high, vz_high), p_far, vx_far)
    oxh[...] = got * inside[1]

    for scr, edge_p, edge_v, dest, flag, sign in (
        (s_yl, s_p0, s_v0, oyl, inside[2], 1.0),
        (s_yh, s_p1, s_v1, oyh, inside[3], -1.0),
    ):
        mid = slice(1, nx + 1)
        p, vy = scr[NEAR_P, mid, :], scr[NEAR_N, mid, :]
        flux_x = face_flux(
            scr[NEAR_P, 0 : nx + 1, :], scr[NEAR_P, 1 : nx + 2, :],
            scr[NEAR_T, 0 : nx + 1, :], scr[NEAR_T, 1 : nx + 2, :],
        )
        change = flux_x[1:] - flux_x[:-1]
        far = (scr[FAR_P, mid, :], scr[FAR_N, mid, :])
        near = (edge_p[...], edge_v[...])
        before, following = (far, near) if sign > 0 else (near, far)
        change = change + (
            face_flux(p, following[0], vy, following[1]) - face_flux(before[0], p, before[1], vy)
        )
        change = change + depth_change(p, scr[NEAR_Z, mid, :])
        dest[...] = (p + 0.5 * change) * flag


def upwind_zero_kernel(
    p_ref, v_ref, pxl, pxh, pyl, pyh, hxl, hxh, hyl, hyh, out, fxl, fxh, fyl, fyh,
    s_vl, s_vh, s_fl, s_fh,
):
    nx, ny, nz = p_ref.shape
    s_vl[...] = hyl[NEAR_EARLY].astype(F32)
    s_vh[...] = hyh[NEAR_EARLY].astype(F32)

    def speed(c, x):
        return v_ref[0, c, x].astype(F32)

    def plane(x, flux_below, p_next, vx_next):
        p = p_ref[x]
        flux_above = face_flux(p, p_next, speed(0, x), vx_next)
        at, halo_at = pl.ds(x, 1), pl.ds(x + 1, 1)
        below = pyl[at, :], s_vl[halo_at, :]
        above = pyh[at, :], s_vh[halo_at, :]
        change = (flux_above - flux_below) + plane_change(p, speed(1, x), speed(2, x), below, above)
        got = p + 0.5 * change
        out[x] = got
        s_fl[at, :] = got[0:1]
        s_fh[at, :] = got[ny - 1 : ny]
        return flux_above

    flux = face_flux(pxl[...], p_ref[0], hxl[NEAR_EARLY].astype(F32), speed(0, 0))
    flux = lax.fori_loop(0, nx - 1, lambda x, f: plane(x, f, p_ref[x + 1], speed(0, x + 1)), flux)
    plane(nx - 1, flux, pxh[...], hxh[NEAR_EARLY].astype(F32))
    fxl[0] = out[0].astype(BF16)
    fxh[0] = out[nx - 1].astype(BF16)
    fyl[0] = s_fl[...].astype(BF16)
    fyh[0] = s_fh[...].astype(BF16)


def speeds_spec(velocity, instant):
    block = (1,) + velocity.shape[1:]
    return pl.BlockSpec(block, lambda *_: (instant,) + (0,) * (len(block) - 1))


def upwind_one(inside, field, velocity, halo):
    nx, ny, nz = field.shape
    line = struct((ny, nz), F32)
    in_specs = [pl.BlockSpec(memory_space=pltpu.SMEM), whole(field.shape), speeds_spec(velocity, 1)]
    in_specs += [whole(h.shape) for h in halo]
    scratch = [pltpu.VMEM(halo[2].shape, F32)] * 2 + [pltpu.VMEM((nx, nz), F32)] * 4
    outs = [struct(field.shape, F32)] + [line] * 4
    return call(upwind_one_kernel, outs, scratch, "upwind_one", in_specs)(inside, field, velocity, *halo)


def upwind_zero(field, velocity, field_halo, halo):
    nx, ny, nz = field.shape
    in_specs = [whole(field.shape), speeds_spec(velocity, 0)]
    in_specs += [whole(h.shape) for h in (*field_halo, *halo)]
    scratch = [pltpu.VMEM((nx + 2, nz), F32)] * 2 + [pltpu.VMEM((nx, nz), F32)] * 2
    outs = [struct(field.shape, F32)] + [struct((1, ny, nz), BF16)] * 4
    return call(upwind_zero_kernel, outs, scratch, "upwind_zero", in_specs)(
        field, velocity, *field_halo, *halo
    )


def pick_kernel(planes, t_lo, t_own, t_hi, q_ref, *outs):
    nz = t_own.shape[2]
    ny = t_own.shape[1]
    blocks = []
    for ref in (t_lo, t_own, t_hi):
        parts = [ref[a:b].reshape((b - a) * ny, nz) for a, b in planes]
        blocks.append(parts[0] if len(parts) == 1 else jnp.concatenate(parts, axis=0))
    rows = jnp.concatenate(blocks, axis=1)
    count = rows.shape[0] // ny
    for d, out in enumerate(outs):
        got = jnp.dot(rows, q_ref[d], preferred_element_type=F32).astype(BF16)
        out[0] = got[:, :nz].reshape(count, ny, nz)
        out[1] = got[:, nz:].reshape(count, ny, nz)


def pick(columns, choices, planes, name):
    _, ny, nz = columns[0].shape
    count = sum(b - a for a, b in planes)
    outs = [struct((2, count, ny, nz), BF16)] * choices.shape[0]
    in_specs = [whole(c.shape) for c in columns] + [whole(choices.shape)]
    return call(functools.partial(pick_kernel, planes), outs, [], name, in_specs)(*columns, choices)


def outer_kernel(own, la, ra, face_lo, face_hi, low, high):
    nx, count = own.shape[1], la.shape[1]
    for k in range(2):
        for c in range(2):
            low[2 * k + c] = own[k, c] + la[k, c] + ra[k, c]
            x, a = nx - 2 + c, count - 2 + c
            high[2 * k + c] = own[k, x] + la[k, a] + ra[k, a]
    low[4] = face_lo[0]
    high[4] = face_hi[0]


def each_plane(groups, own, la, ra, lb, rb, k, visit):
    for planes, lefts, rights in ((groups[0], la, ra), (groups[1], lb, rb)):
        at = 0
        for a, b in planes:

            def step(x, carry, shift=at - a, lefts=lefts, rights=rights):
                visit(x, own[k, x] + lefts[k, x + shift] + rights[k, x + shift])
                return carry

            lax.fori_loop(a, b, step, 0)
            at += b - a


def edge_kernel(
    groups, own, la, ra, lb, rb, xlo, xhi, face_lo, face_hi, first, final, s_first, s_final
):
    _, nx, ny, nz = own.shape
    for k in range(2):

        def put(x, cells, k=k):
            at = pl.ds(x + 1, 1)
            cells = cells.astype(F32)
            for c in range(2):
                s_first[2 * k + c, at, :] = cells[c : c + 1]
                s_final[2 * k + c, at, :] = cells[ny - 2 + c : ny - 1 + c]

        put(-1, xlo[2 * k + 1])
        put(nx, xhi[2 * k])
        each_plane(groups, own, la, ra, lb, rb, k, put)
    for faces, scr, msg in ((face_lo, s_first, first), (face_hi, s_final, final)):
        msg[0:4] = scr[...].astype(BF16)
        msg[4] = jnp.zeros(msg.shape[1:], BF16)
        msg[4, 0:nx] = faces[0]


def force_kernel(
    groups, own, la, ra, lb, rb, band, xlo, xhi, ylo, yhi, adj0, adj1, bxl, bxh, byl, byh, vel,
    out, img, packed, frc, s_ylo, s_yhi, s_c0, s_c1, s_fl, s_fh, s_al, s_ah,
):
    k = pl.program_id(0)
    nx, ny, nz = adj0.shape
    rows = lax.broadcasted_iota(jnp.int32, (ny, nz), 0)
    lanes = lax.broadcasted_iota(jnp.int32, (ny, nz), 1)
    first_image = k == 0

    def this(zero, one):
        return jnp.where(first_image, zero.astype(F32), one.astype(F32))

    for h in range(2):
        img[h] = xlo[2 * k + h].astype(F32)
        img[nx + 2 + h] = xhi[2 * k + h].astype(F32)

    def fill(x, cells):
        packed[x] = cells
        cells = cells.astype(F32)
        img[x + 2] = cells
        s_c0[pl.ds(x, 1), :] = cells[0:1]
        s_c1[pl.ds(x, 1), :] = cells[ny - 1 : ny]

    each_plane(groups, own, la, ra, lb, rb, 0, fill)
    every = packed[...].reshape(nx * ny, nz)
    frc[2, 1 : nx + 1] = jnp.dot(every, band[...], preferred_element_type=F32).reshape(nx, ny, nz)
    for h in range(2):
        s_ylo[h] = ylo[2 * k + h].astype(F32)
        s_yhi[h] = yhi[2 * k + h].astype(F32)
    s_al[...] = this(ylo[4, 0:nx], byl[...])
    s_ah[...] = this(yhi[4, 0:nx], byh[...])

    def along_z(cells, index, length):
        following = jnp.where(index == length - 1, 0.0, pltpu.roll(cells, length - 1, 1))
        before = jnp.where(index == 0, 0.0, pltpu.roll(cells, 1, 1))
        return following, before

    def forces(x, half, slope_z):
        cells = img[x + 2]
        at = pl.ds(x + 1, 1)
        frc[0, x + 1] = half * (img[x + 3] - img[x + 1])
        up = jnp.where(rows == ny - 1, s_yhi[0, at, :], pltpu.roll(cells, ny - 1, 0))
        down = jnp.where(rows == 0, s_ylo[1, at, :], pltpu.roll(cells, 1, 0))
        frc[1, x + 1] = half * (up - down)
        frc[2, x + 1] = half * slope_z

    for x, half in ((-1, 0.5 * this(xlo[4], bxl[...])), (nx, 0.5 * this(xhi[4], bxh[...]))):
        following, before = along_z(img[x + 2], lanes, nz)
        forces(x, half, following - before)

    def force_step(x, carry):
        forces(x, 0.5 * this(adj0[x], adj1[x]), frc[2, x + 1])
        return carry

    lax.fori_loop(0, nx, force_step, 0)
    lines = lax.broadcasted_iota(jnp.int32, (nx, nz), 1)
    for cols, near, far, beside, half, dest, sign in (
        (s_ylo, 1, 0, s_c0, s_al, s_fl, 1.0),
        (s_yhi, 0, 1, s_c1, s_ah, s_fh, -1.0),
    ):
        weight = 0.5 * half[...]
        dest[0] = weight * (cols[near, 2 : nx + 2, :] - cols[near, 0:nx, :])
        dest[1] = (sign * weight) * (beside[...] - cols[far, 1 : nx + 1, :])
        following, before = along_z(cols[near, 1 : nx + 1, :], lines, nz)
        dest[2] = weight * (following - before)

    def smooth_step(x, carry):
        at = pl.ds(x, 1)
        for c in range(3):
            f = frc[c, x + 1]
            up = jnp.where(rows == ny - 1, s_fh[c, at, :], pltpu.roll(f, ny - 1, 0))
            down = jnp.where(rows == 0, s_fl[c, at, :], pltpu.roll(f, 1, 0))
            following, before = along_z(f, lanes, nz)
            beside = (frc[c, x] + frc[c, x + 2]) + (up + down) + (following + before)
            out[0, c, x] = vel[0, c, x].astype(F32) + (0.25 * f + 0.125 * beside)
        return carry

    lax.fori_loop(0, nx, smooth_step, 0)


def force(groups, images, band, x_lo, x_hi, y_lo, y_hi, adj_zero, adj_one, halo_one, velocity):
    nx, ny, nz = adj_zero.shape
    block = pl.BlockSpec((1, 3, nx, ny, nz), lambda k: (k, 0, 0, 0, 0))
    middle = [band, x_lo, x_hi, y_lo, y_hi, adj_zero, adj_one, *halo_one]
    in_specs = [pl.BlockSpec((1,) + a.shape[1:], lambda k: (k, 0, 0, 0)) for a in images]
    in_specs += [whole(a.shape) for a in middle] + [block]
    scratch = [
        pltpu.VMEM((nx + 4, ny, nz), F32),
        pltpu.VMEM((nx, ny, nz), BF16),
        pltpu.VMEM((3, nx + 2, ny, nz), F32),
        pltpu.VMEM((2, nx + 2, nz), F32),
        pltpu.VMEM((2, nx + 2, nz), F32),
        pltpu.VMEM((nx, nz), F32),
        pltpu.VMEM((nx, nz), F32),
        pltpu.VMEM((3, nx, nz), F32),
        pltpu.VMEM((3, nx, nz), F32),
        pltpu.VMEM((nx, nz), F32),
        pltpu.VMEM((nx, nz), F32),
    ]
    return call(
        functools.partial(force_kernel, groups),
        struct((2, 3, nx, ny, nz), F32),
        scratch,
        "force",
        in_specs,
        block,
        2,
    )(*images, *middle, velocity)


def forward(value, axis):
    ends = lax.axis_size(axis) - 1
    return lax.ppermute(value, axis, [(i, i + 1) for i in range(ends)])


def backward(value, axis):
    ends = lax.axis_size(axis) - 1
    return lax.ppermute(value, axis, [(i + 1, i) for i in range(ends)])


def body(template, mismatch, velocity, src_ids):
    nx, ny, nz = template.shape
    depth_blocks = src_ids.shape[3]
    edge = nz // depth_blocks
    slots = 2 * depth_blocks
    index_first = lax.axis_index("gx")
    index_second = lax.axis_index("gy")
    count_first = lax.axis_size("gx")
    count_second = lax.axis_size("gy")

    def x_message(near, far):
        parts = [mismatch[near].astype(BF16), mismatch[far].astype(BF16)]
        parts += [velocity[1, 0, near], velocity[1, 0, far], velocity[1, 1, near]]
        return jnp.stack(parts + [velocity[1, 2, near], velocity[0, 0, near]])

    halo_xl = forward(x_message(nx - 1, nx - 2), "gx")
    halo_xh = backward(x_message(0, 1), "gx")
    t_lo = forward(template, "gx")
    t_hi = backward(template, "gx")

    ids = src_ids.reshape(slots)
    first_block = ids // (count_second * depth_blocks)
    second_block = ids // depth_blocks % count_second
    start = (first_block - index_first + 1) * depth_blocks + ids % depth_blocks
    side = second_block - index_second + 1
    code = (side * (3 * depth_blocks) + start).astype(F32)
    code = jnp.pad(code.reshape(1, slots), ((0, 0), (0, nz - slots)))
    ins = (mismatch, velocity, halo_xl, halo_xh, code)
    rows = struct((7, nx + 2, nz), BF16)
    low, high = call(
        rows_kernel,
        [rows] * 2,
        [pltpu.VMEM(rows.shape, F32)] * 2,
        "rows",
        [whole(a.shape) for a in ins],
    )(*ins)
    halo_yl = forward(high, "gy")
    halo_yh = backward(low, "gy")
    halo = (halo_xl, halo_xh, halo_yl, halo_yh)

    within = jnp.arange(edge)[None, :]

    def choice(wanted, start):
        rows = (jnp.where(wanted, start, -4 * depth_blocks)[:, None] * edge + within).reshape(1, -1)
        return (jnp.arange(3 * nz)[:, None] == rows).astype(BF16)

    def far_choice(message, side):
        code = message[FAR_P, 0, :slots].astype(jnp.int32)
        return choice(code // (3 * depth_blocks) == side, code % (3 * depth_blocks))

    send_choice = jnp.stack([far_choice(halo_yl, 2), far_choice(halo_yh, 0)])
    own_choice = choice(side == 1, start)[None]
    z = jnp.arange(nz)
    band = (z[:, None] == z[None] + 1).astype(BF16) - (z[:, None] == z[None] - 1).astype(BF16)

    columns = (t_lo, template, t_hi)
    margin = nx // 8
    groups = (((0, margin), (nx - margin, nx)), ((margin, nx - margin),))
    to_left_a, to_right_a = pick(columns, send_choice, groups[0], "pick_outer")
    from_left_a = forward(to_right_a, "gy")
    from_right_a = backward(to_left_a, "gy")
    columns, _ = lax.optimization_barrier((columns, to_left_a))
    to_left_b, to_right_b = pick(columns, send_choice, groups[1], "pick_inner")
    from_left_b = forward(to_right_b, "gy")
    from_right_b = backward(to_left_b, "gy")

    late_mismatch, late_choice, _ = lax.optimization_barrier((mismatch, own_choice, to_left_b))
    (own,) = pick(columns, late_choice, ((0, nx),), "pick_own")
    inside = jnp.stack(
        [index_first > 0, index_first < count_first - 1, index_second > 0, index_second < count_second - 1]
    ).astype(F32)
    adj_one, *halo_one = upwind_one(inside, late_mismatch, velocity, halo)
    adj_zero, low_x, high_x, low_y, high_y = upwind_zero(adj_one, velocity, halo_one, halo)

    ins = (own, from_left_a, from_right_a, low_x, high_x)
    low, high = call(
        outer_kernel, [struct((5, ny, nz), BF16)] * 2, [], "outer", [whole(a.shape) for a in ins]
    )(*ins)
    x_lo = forward(high, "gx")
    x_hi = backward(low, "gx")

    images = (own, from_left_a, from_right_a, from_left_b, from_right_b)
    ins = (*images, x_lo, x_hi, low_y, high_y)
    first, final = call(
        functools.partial(edge_kernel, groups),
        [struct((5, nx + 2, nz), BF16)] * 2,
        [pltpu.VMEM((4, nx + 2, nz), F32)] * 2,
        "edges",
        [whole(a.shape) for a in ins],
    )(*ins)
    y_lo = forward(final, "gy")
    y_hi = backward(first, "gy")
    return force(groups, images, band, x_lo, x_hi, y_lo, y_hi, adj_zero, adj_one, halo_one, velocity)


def solution(mesh):
    in_specs = (
        P("gx", "gy", None),
        P("gx", "gy", None),
        P(None, None, "gx", "gy", None),
        P(None, "gx", "gy", None),
    )
    out_specs = P(None, None, "gx", "gy", None)
    return jax.shard_map(body, mesh=mesh, in_specs=in_specs, out_specs=out_specs, check_vma=False)
```

time: 205 us -> 164 us (0.80)
  the two profiles are of different devices: /device:TPU:26 before, /device:TPU:225 now
where the time goes in v2:
time: 164 us; the launch traced here: 163 us
  starting transfers between devices  66.7 us (41%)
  waiting for transfers between devices  50 us (30%)
  Pallas kernels  33.1 us (20%)
  local copies, waits for them, and re-layouts  8.9 us (5%)
  other arithmetic  3.57 us (2%)
    ppermute x7, starting transfers between devices, forward(): return lax.ppermute(value, axis, [(i, i + 1) for i in range(ends)])  52 us
    ppermute x7, waiting for transfers between devices, backward(): return lax.ppermute(value, axis, [(i + 1, i) for i in range(ends)])  28 us
    ppermute x7, waiting for transfers between devices, forward(): return lax.ppermute(value, axis, [(i, i + 1) for i in range(ends)])  22 us
    ppermute x7, starting transfers between devices, backward(): return lax.ppermute(value, axis, [(i + 1, i) for i in range(ends)])  14.7 us
    pallas_call x1, Pallas kernels, force(): call(functools.partial(force_kernel, groups), struct((2, 3, nx, ny, nz),...  14.3 us
    unnamed x34, local copies, waits for them, and re-layouts  7.75 us
    pallas_call x1, Pallas kernels, upwind_one(): call(upwind_one_kernel, outs, scratch, 'upwind_one', in_specs)  6.09 us
    pallas_call x1, Pallas kernels, upwind_zero(): call(upwind_zero_kernel, outs, scratch, 'upwind_zero', in_specs)  5.15 us
  transfers between devices with their start and end apart: 14, of which 5 were waited for; matrix products, arithmetic and copies ran while one was open for 2% of the time, Pallas kernels for 8%

profile of v2, /device:TPU:225, one launch (start us, length us, event | category | flops | bytes accessed | tf_op | source)
XLA Modules:
  0.0 162.7 jit_solution(9895479326606141244)
XLA Ops:
  5.1 2.6 %collective-permute-start.3 = (bf16[7,32,256]{2,1,0:T(8,128)(2,1)S(1)}, bf16[7,32,256]{2,1,0:T(8,128)(2,1)S(1)}, u32[]{:S(2)}, u32[]{:S(2)}) collective-permute-start(bf16[7,32,256]{2,1,0:T(8,128)(2,1)S(1)} %get-tuple-element.55), channel_id=1, source_target_pairs={{16,0},{32,16},{48,32},{64,48},{80,64},{96,80},{112,96},{128,112},... | collective-permute-start | bytes 344072 | tf_op jit(solution)/shard_map/ppermute | solution.py:409
  7.7 7.8 %collective-permute-start.2 = (bf16[7,32,256]{2,1,0:T(8,128)(2,1)S(1)}, bf16[7,32,256]{2,1,0:T(8,128)(2,1)S(1)}, u32[]{:S(2)}, u32[]{:S(2)}) collective-permute-start(bf16[7,32,256]{2,1,0:T(8,128)(2,1)S(1)} %get-tuple-element.56), channel_id=1, source_target_pairs={{0,16},{16,32},{32,48},{48,64},{64,80},{80,96},{96,112},{112,128},... | collective-permute-start | bytes 344072 | tf_op jit(solution)/shard_map/ppermute | solution.py:404
  17.3 1.9 %copy-done = bf16[2,3,32,32,256]{4,3,2,1,0:T(8,128)(2,1)S(1)} copy-done((bf16[2,3,32,32,256]{4,3,2,1,0:T(8,128)(2,1)S(1)}, bf16[2,3,32,32,256]{4,3,2,1,0:T(8,128)(2,1)}, u32[]{:S(2)}) %copy-start) | copy-done | bytes 3145752
  19.8 4.6 %collective-permute-start.4 = (bf16[7,34,256]{2,1,0:T(8,128)(2,1)S(1)}, bf16[7,34,256]{2,1,0:T(8,128)(2,1)S(1)}, u32[]{:S(2)}, u32[]{:S(2)}) collective-permute-start(bf16[7,34,256]{2,1,0:T(8,128)(2,1)S(1)} %get-tuple-element.30), channel_id=1, source_target_pairs={{0,1},{1,2},{2,3},{3,4},{4,5},{5,6},{6,7},{7,8},{8,9},{9,10},{10,1... | collective-permute-start | bytes 365576 | tf_op jit(solution)/shard_map/ppermute | solution.py:404
  24.5 2.6 %collective-permute-start.1 = (bf16[32,32,256]{2,1,0:T(8,128)(2,1)S(1)}, bf16[32,32,256]{2,1,0:T(8,128)(2,1)S(1)}, u32[]{:S(2)}, u32[]{:S(2)}) collective-permute-start(bf16[32,32,256]{2,1,0:T(8,128)(2,1)S(1)} %copy-done.3), channel_id=1, source_target_pairs={{16,0},{32,16},{48,32},{64,48},{80,64},{96,80},{112,96},{128,112},... | collective-permute-start | bytes 1572872 | tf_op jit(solution)/shard_map/ppermute | solution.py:409
  27.0 8.8 %collective-permute-start = (bf16[32,32,256]{2,1,0:T(8,128)(2,1)S(1)}, bf16[32,32,256]{2,1,0:T(8,128)(2,1)S(1)}, u32[]{:S(2)}, u32[]{:S(2)}) collective-permute-start(bf16[32,32,256]{2,1,0:T(8,128)(2,1)S(1)} %copy-done.3), channel_id=1, source_target_pairs={{0,16},{16,32},{32,48},{48,64},{64,80},{80,96},{96,112},{112,128},... | collective-permute-start | bytes 1572872 | tf_op jit(solution)/shard_map/ppermute | solution.py:404
  36.0 1.9 %collective-permute-start.5 = (bf16[7,34,256]{2,1,0:T(8,128)(2,1)S(1)}, bf16[7,34,256]{2,1,0:T(8,128)(2,1)S(1)}, u32[]{:S(2)}, u32[]{:S(2)}) collective-permute-start(bf16[7,34,256]{2,1,0:T(8,128)(2,1)S(1)} %get-tuple-element.31), channel_id=1, source_target_pairs={{1,0},{2,1},{3,2},{4,3},{5,4},{6,5},{7,6},{8,7},{9,8},{10,9},{11,1... | collective-permute-start | bytes 365576 | tf_op jit(solution)/shard_map/ppermute | solution.py:409
  38.1 13.3 %collective-permute-done.5.hyh = bf16[7,34,256]{2,1,0:T(8,128)(2,1)S(1)} collective-permute-done((bf16[7,34,256]{2,1,0:T(8,128)(2,1)S(1)}, bf16[7,34,256]{2,1,0:T(8,128)(2,1)S(1)}, u32[]{:S(2)}, u32[]{:S(2)}) %collective-permute-start.5) | collective-permute-done | bytes 121888 | tf_op jit(solution)/shard_map/ppermute | solution.py:409
  54.4 2.4 %pick_inner.1 = (bf16[2,24,32,256]{3,2,1,0:T(8,128)(2,1)}, bf16[2,24,32,256]{3,2,1,0:T(8,128)(2,1)}) custom-call(bf16[32,32,256]{2,1,0:T(8,128)(2,1)S(1)} %collective-permute-done.t_lo, bf16[32,32,256]{2,1,0:T(8,128)(2,1)S(1)} %copy-done.3, bf16[32,32,256]{2,1,0:T(8,128)(2,1)S(1)} %collective-permute-done.1.t_hi, bf16[2,768,512]{2,1,0:T(8,128)(2,1)S(1)} %add_convert_fusion.q_ref), custom_call_target="tpu_custom_call" | custom-call | tf_op jit(solution)/shard_map/pick_inner/pallas_call | solution.py:242
  56.8 8.7 %collective-permute-start.8 = (bf16[2,24,32,256]{3,2,1,0:T(8,128)(2,1)}, bf16[2,24,32,256]{3,2,1,0:T(8,128)(2,1)S(1)}, u32[]{:S(2)}, u32[]{:S(2)}) collective-permute-start(bf16[2,24,32,256]{3,2,1,0:T(8,128)(2,1)} %get-tuple-element.39), channel_id=1, source_target_pairs={{0,1},{1,2},{2,3},{3,4},{4,5},{5,6},{6,7},{7,8},{8,9},{9,10},{10,1... | collective-permute-start | bytes 2359304 | tf_op jit(solution)/shard_map/ppermute | solution.py:404
  65.5 1.9 %collective-permute-start.9 = (bf16[2,24,32,256]{3,2,1,0:T(8,128)(2,1)}, bf16[2,24,32,256]{3,2,1,0:T(8,128)(2,1)}, u32[]{:S(2)}, u32[]{:S(2)}) collective-permute-start(bf16[2,24,32,256]{3,2,1,0:T(8,128)(2,1)} %get-tuple-element.36), channel_id=1, source_target_pairs={{1,0},{2,1},{3,2},{4,3},{5,4},{6,5},{7,6},{8,7},{9,8},{10,9},{11,1... | collective-permute-start | bytes 2359304 | tf_op jit(solution)/shard_map/ppermute | solution.py:409
  67.5 1.9 %collective-permute-start.7 = (bf16[2,8,32,256]{3,2,1,0:T(8,128)(2,1)}, bf16[2,8,32,256]{3,2,1,0:T(8,128)(2,1)}, u32[]{:S(2)}, u32[]{:S(2)}) collective-permute-start(bf16[2,8,32,256]{3,2,1,0:T(8,128)(2,1)} %copy-done.10), channel_id=1, source_target_pairs={{1,0},{2,1},{3,2},{4,3},{5,4},{6,5},{7,6},{8,7},{9,8},{10,9},{11,1... | collective-permute-start | bytes 786440 | tf_op jit(solution)/shard_map/ppermute | solution.py:409
  69.4 6.1 %collective-permute-start.6 = (bf16[2,8,32,256]{3,2,1,0:T(8,128)(2,1)}, bf16[2,8,32,256]{3,2,1,0:T(8,128)(2,1)}, u32[]{:S(2)}, u32[]{:S(2)}) collective-permute-start(bf16[2,8,32,256]{3,2,1,0:T(8,128)(2,1)} %copy-done.11), channel_id=1, source_target_pairs={{0,1},{1,2},{2,3},{3,4},{4,5},{5,6},{6,7},{7,8},{8,9},{9,10},{10,1... | collective-permute-start | bytes 786440 | tf_op jit(solution)/shard_map/ppermute | solution.py:404
  77.9 6.1 %upwind_one.1 = (f32[32,32,256]{2,1,0:T(8,128)S(1)}, f32[32,256]{1,0:T(8,128)S(1)}, f32[32,256]{1,0:T(8,128)S(1)}, f32[32,256]{1,0:T(8,128)S(1)}, f32[32,256]{1,0:T(8,128)S(1)}) custom-call(f32[4]{0:T(128)S(1)} %add_convert_fusion.1.inside, f32[32,32,256]{2,1,0:T(8,128)S(1)} %copy-done.2, bf16[2,3,32,32,256]{4,3,2,1,0:T(8,128)(2,1)S(1)} %copy-done.1, ...), custom_call_target="tpu_custom_call" | custom-call | tf_op jit(solution)/shard_map/upwind_one/pallas_call | solution.py:208
  84.0 5.2 %upwind_zero.1 = (f32[32,32,256]{2,1,0:T(8,128)S(1)}, bf16[1,32,256]{2,1,0:T(8,128)(2,1)S(1)}, bf16[1,32,256]{2,1,0:T(8,128)(2,1)S(1)}, bf16[1,32,256]{2,1,0:T(8,128)(2,1)S(1)}, bf16[1,32,256]{2,1,0:T(8,128)(2,1)S(1)}) custom-call(f32[32,32,256]{2,1,0:T(8,128)S(1)} %get-tuple-element.41.p_ref.adj1, bf16[2,3,32,32,256]{4,3,2,1,0:T(8,128)(2,1)S(1)} %copy-done.1, ...), custom_call_target="tpu_custom_call" | custom-call | tf_op jit(solution)/shard_map/upwind_zero/pallas_call | solution.py:217
  89.1 21.5 %collective-permute-done.6.la = bf16[2,8,32,256]{3,2,1,0:T(8,128)(2,1)} collective-permute-done((bf16[2,8,32,256]{3,2,1,0:T(8,128)(2,1)}, bf16[2,8,32,256]{3,2,1,0:T(8,128)(2,1)}, u32[]{:S(2)}, u32[]{:S(2)}) %collective-permute-start.6) | collective-permute-done | bytes 262176 | tf_op jit(solution)/shard_map/ppermute | solution.py:404
  111.7 9.2 %collective-permute-start.10 = (bf16[5,32,256]{2,1,0:T(8,128)(2,1)S(1)}, bf16[5,32,256]{2,1,0:T(8,128)(2,1)S(1)}, u32[]{:S(2)}, u32[]{:S(2)}) collective-permute-start(bf16[5,32,256]{2,1,0:T(8,128)(2,1)S(1)} %get-tuple-element.48), channel_id=1, source_target_pairs={{0,16},{16,32},{32,48},{48,64},{64,80},{80,96},{96,112},{112,128},... | collective-permute-start | bytes 245768 | tf_op jit(solution)/shard_map/ppermute | solution.py:404
  120.9 1.9 %collective-permute-start.11 = (bf16[5,32,256]{2,1,0:T(8,128)(2,1)S(1)}, bf16[5,32,256]{2,1,0:T(8,128)(2,1)S(1)}, u32[]{:S(2)}, u32[]{:S(2)}) collective-permute-start(bf16[5,32,256]{2,1,0:T(8,128)(2,1)S(1)} %get-tuple-element.49), channel_id=1, source_target_pairs={{16,0},{32,16},{48,32},{64,48},{80,64},{96,80},{112,96},{128,112},... | collective-permute-start | bytes 245768 | tf_op jit(solution)/shard_map/ppermute | solution.py:409
  122.8 8.6 %collective-permute-done.11.xhi = bf16[5,32,256]{2,1,0:T(8,128)(2,1)S(1)} collective-permute-done((bf16[5,32,256]{2,1,0:T(8,128)(2,1)S(1)}, bf16[5,32,256]{2,1,0:T(8,128)(2,1)S(1)}, u32[]{:S(2)}, u32[]{:S(2)}) %collective-permute-start.11) | collective-permute-done | bytes 81952 | tf_op jit(solution)/shard_map/ppermute | solution.py:409
  131.5 2.0 %edges.1 = (bf16[5,34,256]{2,1,0:T(8,128)(2,1)S(1)}, bf16[5,34,256]{2,1,0:T(8,128)(2,1)S(1)}) custom-call(bf16[2,32,32,256]{3,2,1,0:T(8,128)(2,1)S(1)} %pick_own.1.own, bf16[2,8,32,256]{3,2,1,0:T(8,128)(2,1)} %collective-permute-done.6.la, bf16[2,8,32,256]{3,2,1,0:T(8,128)(2,1)} %collective-permute-done.7.ra, ...), custom_call_target="tpu_custom_call" | custom-call | tf_op jit(solution)/shard_map/edges/pallas_call | solution.py:495
  133.4 6.8 %collective-permute-start.12 = (bf16[5,34,256]{2,1,0:T(8,128)(2,1)S(1)}, bf16[5,34,256]{2,1,0:T(8,128)(2,1)S(1)}, u32[]{:S(2)}, u32[]{:S(2)}) collective-permute-start(bf16[5,34,256]{2,1,0:T(8,128)(2,1)S(1)} %get-tuple-element.52), channel_id=1, source_target_pairs={{0,1},{1,2},{2,3},{3,4},{4,5},{5,6},{6,7},{7,8},{8,9},{9,10},{10,1... | collective-permute-start | bytes 261128 | tf_op jit(solution)/shard_map/ppermute | solution.py:404
  140.3 1.9 %collective-permute-start.13 = (bf16[5,34,256]{2,1,0:T(8,128)(2,1)S(1)}, bf16[5,34,256]{2,1,0:T(8,128)(2,1)S(1)}, u32[]{:S(2)}, u32[]{:S(2)}) collective-permute-start(bf16[5,34,256]{2,1,0:T(8,128)(2,1)S(1)} %get-tuple-element.53), channel_id=1, source_target_pairs={{1,0},{2,1},{3,2},{4,3},{5,4},{6,5},{7,6},{8,7},{9,8},{10,9},{11,1... | collective-permute-start | bytes 261128 | tf_op jit(solution)/shard_map/ppermute | solution.py:409
  142.3 6.1 %collective-permute-done.13.yhi = bf16[5,34,256]{2,1,0:T(8,128)(2,1)S(1)} collective-permute-done((bf16[5,34,256]{2,1,0:T(8,128)(2,1)S(1)}, bf16[5,34,256]{2,1,0:T(8,128)(2,1)S(1)}, u32[]{:S(2)}, u32[]{:S(2)}) %collective-permute-start.13) | collective-permute-done | bytes 87072 | tf_op jit(solution)/shard_map/ppermute | solution.py:409
  148.4 14.3 %force.1 = f32[2,3,32,32,256]{4,3,2,1,0:T(8,128)} custom-call(bf16[2,32,32,256]{3,2,1,0:T(8,128)(2,1)S(1)} %pick_own.1.own, bf16[2,8,32,256]{3,2,1,0:T(8,128)(2,1)} %collective-permute-done.6.la, bf16[2,8,32,256]{3,2,1,0:T(8,128)(2,1)} %collective-permute-done.7.ra, bf16[2,24,32,256]{3,2,1,0:T(8,128)(2,1)S(1)} %collective-permute-done.8.lb, ...), custom_call_target="tpu_custom_call" | custom-call | tf_op jit(solution)/shard_map/force/pallas_call | solution.py:391
  (69 shorter events, 14.2 us)
Async XLA Ops:
  0.0 17.3 %copy-start.2 = (f32[32,32,256]{2,1,0:T(8,128)S(1)}, f32[32,32,256]{2,1,0:T(8,128)}, u32[]{:S(2)}) copy-start(f32[32,32,256]{2,1,0:T(8,128)} %p_ref.2) | copy-start | bytes 3145732
  0.0 16.0 %copy-start.12 = (s32[2,1,1,8]{3,2,1,0:T(1,128)S(1)}, s32[2,1,1,8]{3,2,1,0:T(1,128)}, u32[]{:S(2)}) copy-start(s32[2,1,1,8]{3,2,1,0:T(1,128)} %param.7) | copy-start | bytes 196
  5.1 11.7 %collective-permute-start.3 = (bf16[7,32,256]{2,1,0:T(8,128)(2,1)S(1)}, bf16[7,32,256]{2,1,0:T(8,128)(2,1)S(1)}, u32[]{:S(2)}, u32[]{:S(2)}) collective-permute-start(bf16[7,32,256]{2,1,0:T(8,128)(2,1)S(1)} %get-tuple-element.55), channel_id=1, source_target_pairs={{16,0},{32,16},{48,32},{64,48},{80,64},{96,80},{112,96},{128,112},... | collective-permute-start | bytes 344072 | tf_op jit(solution)/shard_map/ppermute | solution.py:409
  7.7 9.6 %collective-permute-start.2 = (bf16[7,32,256]{2,1,0:T(8,128)(2,1)S(1)}, bf16[7,32,256]{2,1,0:T(8,128)(2,1)S(1)}, u32[]{:S(2)}, u32[]{:S(2)}) collective-permute-start(bf16[7,32,256]{2,1,0:T(8,128)(2,1)S(1)} %get-tuple-element.56), channel_id=1, source_target_pairs={{0,16},{16,32},{32,48},{48,64},{64,80},{80,96},{96,112},{112,128},... | collective-permute-start | bytes 344072 | tf_op jit(solution)/shard_map/ppermute | solution.py:404
  17.3 1.9 %copy-start = (bf16[2,3,32,32,256]{4,3,2,1,0:T(8,128)(2,1)S(1)}, bf16[2,3,32,32,256]{4,3,2,1,0:T(8,128)(2,1)}, u32[]{:S(2)}) copy-start(bf16[2,3,32,32,256]{4,3,2,1,0:T(8,128)(2,1)} %vel.1) | copy-start | bytes 9437188
  19.2 5.3 %copy-start.3 = (bf16[32,32,256]{2,1,0:T(8,128)(2,1)S(1)}, bf16[32,32,256]{2,1,0:T(8,128)(2,1)}, u32[]{:S(2)}) copy-start(bf16[32,32,256]{2,1,0:T(8,128)(2,1)} %t_own.3) | copy-start | bytes 1572868
  19.8 18.1 %collective-permute-start.4 = (bf16[7,34,256]{2,1,0:T(8,128)(2,1)S(1)}, bf16[7,34,256]{2,1,0:T(8,128)(2,1)S(1)}, u32[]{:S(2)}, u32[]{:S(2)}) collective-permute-start(bf16[7,34,256]{2,1,0:T(8,128)(2,1)S(1)} %get-tuple-element.30), channel_id=1, source_target_pairs={{0,1},{1,2},{2,3},{3,4},{4,5},{5,6},{6,7},{7,8},{8,9},{9,10},{10,1... | collective-permute-start | bytes 365576 | tf_op jit(solution)/shard_map/ppermute | solution.py:404
  24.5 27.9 %collective-permute-start.1 = (bf16[32,32,256]{2,1,0:T(8,128)(2,1)S(1)}, bf16[32,32,256]{2,1,0:T(8,128)(2,1)S(1)}, u32[]{:S(2)}, u32[]{:S(2)}) collective-permute-start(bf16[32,32,256]{2,1,0:T(8,128)(2,1)S(1)} %copy-done.3), channel_id=1, source_target_pairs={{16,0},{32,16},{48,32},{64,48},{80,64},{96,80},{112,96},{128,112},... | collective-permute-start | bytes 1572872 | tf_op jit(solution)/shard_map/ppermute | solution.py:409
  27.0 25.4 %collective-permute-start = (bf16[32,32,256]{2,1,0:T(8,128)(2,1)S(1)}, bf16[32,32,256]{2,1,0:T(8,128)(2,1)S(1)}, u32[]{:S(2)}, u32[]{:S(2)}) collective-permute-start(bf16[32,32,256]{2,1,0:T(8,128)(2,1)S(1)} %copy-done.3), channel_id=1, source_target_pairs={{0,16},{16,32},{32,48},{48,64},{64,80},{80,96},{96,112},{112,128},... | collective-permute-start | bytes 1572872 | tf_op jit(solution)/shard_map/ppermute | solution.py:404
  36.0 15.4 %collective-permute-start.5 = (bf16[7,34,256]{2,1,0:T(8,128)(2,1)S(1)}, bf16[7,34,256]{2,1,0:T(8,128)(2,1)S(1)}, u32[]{:S(2)}, u32[]{:S(2)}) collective-permute-start(bf16[7,34,256]{2,1,0:T(8,128)(2,1)S(1)} %get-tuple-element.31), channel_id=1, source_target_pairs={{1,0},{2,1},{3,2},{4,3},{5,4},{6,5},{7,6},{8,7},{9,8},{10,9},{11,1... | collective-permute-start | bytes 365576 | tf_op jit(solution)/shard_map/ppermute | solution.py:409
  37.9 14.5 %copy-start.6 = (bf16[7,34,256]{2,1,0:T(8,128)(2,1)}, bf16[7,34,256]{2,1,0:T(8,128)(2,1)S(1)}, u32[]{:S(2)}) copy-start(bf16[7,34,256]{2,1,0:T(8,128)(2,1)S(1)} %collective-permute-done.4.hyl) | copy-start | bytes 365572
  51.4 1.0 copy-start.8
  56.8 74.7 %collective-permute-start.8 = (bf16[2,24,32,256]{3,2,1,0:T(8,128)(2,1)}, bf16[2,24,32,256]{3,2,1,0:T(8,128)(2,1)S(1)}, u32[]{:S(2)}, u32[]{:S(2)}) collective-permute-start(bf16[2,24,32,256]{3,2,1,0:T(8,128)(2,1)} %get-tuple-element.39), channel_id=1, source_target_pairs={{0,1},{1,2},{2,3},{3,4},{4,5},{5,6},{6,7},{7,8},{8,9},{9,10},{10,1... | collective-permute-start | bytes 2359304 | tf_op jit(solution)/shard_map/ppermute | solution.py:404
  65.5 66.0 %collective-permute-start.9 = (bf16[2,24,32,256]{3,2,1,0:T(8,128)(2,1)}, bf16[2,24,32,256]{3,2,1,0:T(8,128)(2,1)}, u32[]{:S(2)}, u32[]{:S(2)}) collective-permute-start(bf16[2,24,32,256]{3,2,1,0:T(8,128)(2,1)} %get-tuple-element.36), channel_id=1, source_target_pairs={{1,0},{2,1},{3,2},{4,3},{5,4},{6,5},{7,6},{8,7},{9,8},{10,9},{11,1... | collective-permute-start | bytes 2359304 | tf_op jit(solution)/shard_map/ppermute | solution.py:409
  67.5 43.1 %collective-permute-start.7 = (bf16[2,8,32,256]{3,2,1,0:T(8,128)(2,1)}, bf16[2,8,32,256]{3,2,1,0:T(8,128)(2,1)}, u32[]{:S(2)}, u32[]{:S(2)}) collective-permute-start(bf16[2,8,32,256]{3,2,1,0:T(8,128)(2,1)} %copy-done.10), channel_id=1, source_target_pairs={{1,0},{2,1},{3,2},{4,3},{5,4},{6,5},{7,6},{8,7},{9,8},{10,9},{11,1... | collective-permute-start | bytes 786440 | tf_op jit(solution)/shard_map/ppermute | solution.py:409
  69.4 41.2 %collective-permute-start.6 = (bf16[2,8,32,256]{3,2,1,0:T(8,128)(2,1)}, bf16[2,8,32,256]{3,2,1,0:T(8,128)(2,1)}, u32[]{:S(2)}, u32[]{:S(2)}) collective-permute-start(bf16[2,8,32,256]{3,2,1,0:T(8,128)(2,1)} %copy-done.11), channel_id=1, source_target_pairs={{0,1},{1,2},{2,3},{3,4},{4,5},{5,6},{6,7},{7,8},{8,9},{9,10},{10,1... | collective-permute-start | bytes 786440 | tf_op jit(solution)/shard_map/ppermute | solution.py:404
  75.7 1.3 copy-start.9
  75.9 1.9 %copy-start.1 = (bf16[2,3,32,32,256]{4,3,2,1,0:T(8,128)(2,1)S(1)}, bf16[2,3,32,32,256]{4,3,2,1,0:T(8,128)(2,1)}, u32[]{:S(2)}) copy-start(bf16[2,3,32,32,256]{4,3,2,1,0:T(8,128)(2,1)} %vel.1) | copy-start | bytes 9437188
  76.0 1.9 %copy-start.5 = (bf16[7,32,256]{2,1,0:T(8,128)(2,1)S(1)}, bf16[7,32,256]{2,1,0:T(8,128)(2,1)}, u32[]{:S(2)}) copy-start(bf16[7,32,256]{2,1,0:T(8,128)(2,1)} %copy-done.4) | copy-start | bytes 344068
  76.0 1.9 %copy-start.7 = (bf16[7,34,256]{2,1,0:T(8,128)(2,1)S(1)}, bf16[7,34,256]{2,1,0:T(8,128)(2,1)}, u32[]{:S(2)}) copy-start(bf16[7,34,256]{2,1,0:T(8,128)(2,1)} %copy-done.6) | copy-start | bytes 365572
  111.7 11.1 %collective-permute-start.10 = (bf16[5,32,256]{2,1,0:T(8,128)(2,1)S(1)}, bf16[5,32,256]{2,1,0:T(8,128)(2,1)S(1)}, u32[]{:S(2)}, u32[]{:S(2)}) collective-permute-start(bf16[5,32,256]{2,1,0:T(8,128)(2,1)S(1)} %get-tuple-element.48), channel_id=1, source_target_pairs={{0,16},{16,32},{32,48},{48,64},{64,80},{80,96},{96,112},{112,128},... | collective-permute-start | bytes 245768 | tf_op jit(solution)/shard_map/ppermute | solution.py:404
  120.9 10.6 %collective-permute-start.11 = (bf16[5,32,256]{2,1,0:T(8,128)(2,1)S(1)}, bf16[5,32,256]{2,1,0:T(8,128)(2,1)S(1)}, u32[]{:S(2)}, u32[]{:S(2)}) collective-permute-start(bf16[5,32,256]{2,1,0:T(8,128)(2,1)S(1)} %get-tuple-element.49), channel_id=1, source_target_pairs={{16,0},{32,16},{48,32},{64,48},{80,64},{96,80},{112,96},{128,112},... | collective-permute-start | bytes 245768 | tf_op jit(solution)/shard_map/ppermute | solution.py:409
  133.4 8.8 %collective-permute-start.12 = (bf16[5,34,256]{2,1,0:T(8,128)(2,1)S(1)}, bf16[5,34,256]{2,1,0:T(8,128)(2,1)S(1)}, u32[]{:S(2)}, u32[]{:S(2)}) collective-permute-start(bf16[5,34,256]{2,1,0:T(8,128)(2,1)S(1)} %get-tuple-element.52), channel_id=1, source_target_pairs={{0,1},{1,2},{2,3},{3,4},{4,5},{5,6},{6,7},{7,8},{8,9},{9,10},{10,1... | collective-permute-start | bytes 261128 | tf_op jit(solution)/shard_map/ppermute | solution.py:404
  140.3 8.1 %collective-permute-start.13 = (bf16[5,34,256]{2,1,0:T(8,128)(2,1)S(1)}, bf16[5,34,256]{2,1,0:T(8,128)(2,1)S(1)}, u32[]{:S(2)}, u32[]{:S(2)}) collective-permute-start(bf16[5,34,256]{2,1,0:T(8,128)(2,1)S(1)} %get-tuple-element.53), channel_id=1, source_target_pairs={{1,0},{2,1},{3,2},{4,3},{5,4},{6,5},{7,6},{8,7},{9,8},{10,9},{11,1... | collective-permute-start | bytes 261128 | tf_op jit(solution)/shard_map/ppermute | solution.py:409
  (3 other events, 2.1 us)

commit v3 on v2

--- a/solution.py
+++ b/solution.py
@@ -63,16 +63,39 @@
 NEAR_P, FAR_P, NEAR_N, FAR_N, NEAR_T, NEAR_Z, NEAR_EARLY = range(7)
 
 
-def rows_kernel(p_ref, v_ref, hxl, hxh, code, lo, hi, s_lo, s_hi):
+def column_kernel(p_lo, p_hi, v_lo, v_hi, low, high):
+    for msg, p, v, near, far in ((low, p_lo, v_lo, 0, 1), (high, p_hi, v_hi, 1, 0)):
+        msg[NEAR_P] = p[near].astype(BF16)
+        msg[FAR_P] = p[far].astype(BF16)
+        msg[NEAR_N] = v[1, 0, near]
+        msg[FAR_N] = v[1, 0, far]
+        msg[NEAR_T] = v[1, 1, near]
+        msg[NEAR_Z] = v[1, 2, near]
+        msg[NEAR_EARLY] = v[0, 0, near]
+
+
+def column_messages(field, velocity):
+    nx, ny, nz = field.shape
+    in_specs = [pl.BlockSpec((2, ny, nz), lambda *_, b=b: (b, 0, 0)) for b in (0, nx // 2 - 1)]
+    in_specs += [
+        pl.BlockSpec((2, 3, 2, ny, nz), lambda *_, b=b: (0, 0, b, 0, 0)) for b in (0, nx // 2 - 1)
+    ]
+    outs = [struct((7, ny, nz), BF16)] * 2
+    return call(column_kernel, outs, [], "columns", in_specs)(
+        field, field, velocity, velocity
+    )
+
+
+def rows_kernel(p_ref, v_ref, lo, hi):
     nx, ny, _ = p_ref.shape
-    s_lo[...] = jnp.zeros(s_lo.shape, F32)
-    s_hi[...] = jnp.zeros(s_hi.shape, F32)
+    lo[...] = jnp.zeros(lo.shape, F32)
+    hi[...] = jnp.zeros(hi.shape, F32)
 
     def put(layer, x, cells, width):
-        at = pl.ds(x + 1, 1)
         for d in range(width):
-            s_lo[layer + d, at, :] = cells[d : d + 1]
-            s_hi[layer + d, at, :] = cells[ny - 1 - d : ny - d]
+            at = pl.ds((layer + d) * (nx + 2) + x + 1, 1)
+            lo[at, :] = cells[d : d + 1]
+            hi[at, :] = cells[ny - 1 - d : ny - d]
 
     def step(x, carry):
         put(NEAR_P, x, p_ref[x], 2)
@@ -83,23 +106,22 @@
         return carry
 
     lax.fori_loop(0, nx, step, 0)
-    for x, halo in ((-1, hxl), (nx, hxh)):
-        put(NEAR_P, x, halo[NEAR_P].astype(F32), 1)
-        put(NEAR_N, x, halo[NEAR_T].astype(F32), 1)
-        put(NEAR_T, x, halo[NEAR_N].astype(F32), 1)
-    s_lo[FAR_P, 0:1, :] = code[...]
-    s_hi[FAR_P, 0:1, :] = code[...]
-    lo[...] = s_lo[...].astype(BF16)
-    hi[...] = s_hi[...].astype(BF16)
+
+
+def unpack(ref, flat, layers):
+    flat[...] = ref[...].reshape(flat.shape).astype(F32)
+    count = layers.shape[1]
+    for layer in range(layers.shape[0]):
+        layers[layer] = flat[layer * count : (layer + 1) * count, :]
 
 
 def upwind_one_kernel(
     inside, p_ref, v_ref, hxl, hxh, hyl, hyh, out, oxl, oxh, oyl, oyh,
-    s_yl, s_yh, s_p0, s_p1, s_v0, s_v1,
+    s_flat, s_yl, s_yh, s_p0, s_p1, s_v0, s_v1,
 ):
     nx, ny, nz = p_ref.shape
-    s_yl[...] = hyl[...].astype(F32)
-    s_yh[...] = hyh[...].astype(F32)
+    unpack(hyl, s_flat, s_yl)
+    unpack(hyh, s_flat, s_yh)
 
     def plane(x, flux_below, p, speeds, p_next, vx_next):
         vx, vy, vz = speeds
@@ -162,11 +184,11 @@
 
 def upwind_zero_kernel(
     p_ref, v_ref, pxl, pxh, pyl, pyh, hxl, hxh, hyl, hyh, out, fxl, fxh, fyl, fyh,
-    s_vl, s_vh, s_fl, s_fh,
+    s_flat, s_vl, s_vh, s_fl, s_fh,
 ):
     nx, ny, nz = p_ref.shape
-    s_vl[...] = hyl[NEAR_EARLY].astype(F32)
-    s_vh[...] = hyh[NEAR_EARLY].astype(F32)
+    unpack(hyl, s_flat, s_vl)
+    unpack(hyh, s_flat, s_vh)
 
     def speed(c, x):
         return v_ref[0, c, x].astype(F32)
@@ -175,8 +197,8 @@
         p = p_ref[x]
         flux_above = face_flux(p, p_next, speed(0, x), vx_next)
         at, halo_at = pl.ds(x, 1), pl.ds(x + 1, 1)
-        below = pyl[at, :], s_vl[halo_at, :]
-        above = pyh[at, :], s_vh[halo_at, :]
+        below = pyl[at, :], s_vl[NEAR_EARLY, halo_at, :]
+        above = pyh[at, :], s_vh[NEAR_EARLY, halo_at, :]
         change = (flux_above - flux_below) + plane_change(p, speed(1, x), speed(2, x), below, above)
         got = p + 0.5 * change
         out[x] = got
@@ -198,12 +220,23 @@
     return pl.BlockSpec(block, lambda *_: (instant,) + (0,) * (len(block) - 1))
 
 
+def halo_specs(field, halo):
+    nx, ny, nz = field.shape
+    planes = halo[2].shape[0] - 8
+    return [whole(halo[0].shape)] * 2 + [pl.BlockSpec((8, ny, nz), lambda *_: (planes // 8, 0, 0))] * 2
+
+
+def halo_scratch(field):
+    nx, ny, nz = field.shape
+    return [pltpu.VMEM((8 * ny, nz), F32)] + [pltpu.VMEM((7, nx + 2, nz), F32)] * 2
+
+
 def upwind_one(inside, field, velocity, halo):
     nx, ny, nz = field.shape
     line = struct((ny, nz), F32)
     in_specs = [pl.BlockSpec(memory_space=pltpu.SMEM), whole(field.shape), speeds_spec(velocity, 1)]
-    in_specs += [whole(h.shape) for h in halo]
-    scratch = [pltpu.VMEM(halo[2].shape, F32)] * 2 + [pltpu.VMEM((nx, nz), F32)] * 4
+    in_specs += halo_specs(field, halo)
+    scratch = halo_scratch(field) + [pltpu.VMEM((nx, nz), F32)] * 4
     outs = [struct(field.shape, F32)] + [line] * 4
     return call(upwind_one_kernel, outs, scratch, "upwind_one", in_specs)(inside, field, velocity, *halo)
 
@@ -211,55 +244,96 @@
 def upwind_zero(field, velocity, field_halo, halo):
     nx, ny, nz = field.shape
     in_specs = [whole(field.shape), speeds_spec(velocity, 0)]
-    in_specs += [whole(h.shape) for h in (*field_halo, *halo)]
-    scratch = [pltpu.VMEM((nx + 2, nz), F32)] * 2 + [pltpu.VMEM((nx, nz), F32)] * 2
+    in_specs += [whole(h.shape) for h in field_halo] + halo_specs(field, halo)
+    scratch = halo_scratch(field) + [pltpu.VMEM((nx, nz), F32)] * 2
     outs = [struct(field.shape, F32)] + [struct((1, ny, nz), BF16)] * 4
     return call(upwind_zero_kernel, outs, scratch, "upwind_zero", in_specs)(
         field, velocity, *field_halo, *halo
     )
 
 
-def pick_kernel(planes, t_lo, t_own, t_hi, q_ref, *outs):
-    nz = t_own.shape[2]
-    ny = t_own.shape[1]
-    blocks = []
-    for ref in (t_lo, t_own, t_hi):
-        parts = [ref[a:b].reshape((b - a) * ny, nz) for a, b in planes]
-        blocks.append(parts[0] if len(parts) == 1 else jnp.concatenate(parts, axis=0))
-    rows = jnp.concatenate(blocks, axis=1)
+def choice_kernel(edge, blocks, left, right, own, send, keep):
+    _, height, width = keep.shape
+    slots = width // edge
+    lane = lax.broadcasted_iota(jnp.int32, (slots, width), 1)
+    slot = lax.broadcasted_iota(jnp.int32, (slots, width), 0)
+    spread = jnp.where(lane // edge == slot, 1.0, 0.0).astype(BF16)
+    row = lax.broadcasted_iota(jnp.int32, (height, width), 0)
+    within = lax.broadcasted_iota(jnp.int32, (8, width), 1) % edge
+    for code, side, out, d in ((left, 2, send, 0), (right, 0, send, 1), (own, 1, keep, 0)):
+        codes = jnp.broadcast_to(code[...], (8, slots)).astype(BF16)
+        code = jnp.dot(codes, spread, preferred_element_type=F32).astype(jnp.int32)
+        start = (code - side * blocks) * edge
+        good = (start >= 0) & (start < height)
+        wanted = jnp.where(good, start + within, -1)[0:1]
+        out[d] = jnp.where(row == wanted, 1.0, 0.0).astype(BF16)
+
+
+def choices(left, right, own, edge, nz):
+    slots = own.shape[1]
+    width = slots * edge
+    outs = [struct((count, 3 * nz, width), BF16) for count in (2, 1)]
+    kernel = functools.partial(choice_kernel, edge, 3 * nz // edge)
+    in_specs = [whole(own.shape)] * 3
+    return call(kernel, outs, [], "choices", in_specs)(left, right, own)
+
+
+def planes_of(ref, planes):
+    ny, width = ref.shape[1:]
+    parts = [ref[a:b].reshape((b - a) * ny, width) for a, b in planes]
+    return parts[0] if len(parts) == 1 else jnp.concatenate(parts, axis=0)
+
+
+def pick_kernel(planes, t_lo, t_own, t_hi, q_ref, *rest):
+    ny, nz = t_own.shape[1:]
+    nx = t_own.shape[0]
+    rows = jnp.concatenate([planes_of(ref, planes) for ref in (t_lo, t_own, t_hi)], axis=1)
     count = rows.shape[0] // ny
+    outs = rest[-q_ref.shape[0] :]
+    lines, halos = rest[:2], rest[2:4]
+    if len(rest) == len(outs):
+        lines = ()
     for d, out in enumerate(outs):
         got = jnp.dot(rows, q_ref[d], preferred_element_type=F32).astype(BF16)
-        out[0] = got[:, :nz].reshape(count, ny, nz)
-        out[1] = got[:, nz:].reshape(count, ny, nz)
-
-
-def pick(columns, choices, planes, name):
-    _, ny, nz = columns[0].shape
-    count = sum(b - a for a, b in planes)
-    outs = [struct((2, count, ny, nz), BF16)] * choices.shape[0]
-    in_specs = [whole(c.shape) for c in columns] + [whole(choices.shape)]
-    return call(functools.partial(pick_kernel, planes), outs, [], name, in_specs)(*columns, choices)
-
-
-def outer_kernel(own, la, ra, face_lo, face_hi, low, high):
-    nx, count = own.shape[1], la.shape[1]
+        out[0:count] = got[:, :nz].reshape(count, ny, nz)
+        out[count : 2 * count] = got[:, nz:].reshape(count, ny, nz)
+    for d, ref in enumerate(lines):
+        row = 0 if d == 0 else ny - 1
+        for halo, x in ((halos[0], 0), (halos[1], nx + 1)):
+            for layer, source in ((NEAR_P, NEAR_P), (NEAR_N, NEAR_T), (NEAR_T, NEAR_N)):
+                at = layer * (nx + 2) + x
+                ref[at : at + 1, :] = halo[source].astype(F32)[row : row + 1]
+        outs[d][2 * count :] = ref[...].astype(BF16).reshape(-1, ny, nz)
+
+
+def pick(columns, choices, planes, name, lines=()):
+    _, ny, nz = columns[1].shape
+    count = 2 * sum(b - a for a, b in planes)
+    extra = lines[0].shape[0] // ny if lines else 0
+    outs = [struct((count + extra, ny, nz), BF16)] * choices.shape[0]
+    ins = (*columns, choices, *lines)
+    in_specs = [whole(a.shape) for a in ins]
+    return call(functools.partial(pick_kernel, planes), outs, [], name, in_specs)(*ins)
+
+
+def outer_kernel(nx, count, own, la, ra, low, high):
     for k in range(2):
         for c in range(2):
-            low[2 * k + c] = own[k, c] + la[k, c] + ra[k, c]
-            x, a = nx - 2 + c, count - 2 + c
-            high[2 * k + c] = own[k, x] + la[k, a] + ra[k, a]
-    low[4] = face_lo[0]
-    high[4] = face_hi[0]
-
-
-def each_plane(groups, own, la, ra, lb, rb, k, visit):
+            x, a = k * nx + c, k * count + c
+            low[2 * k + c] = own[x] + la[a] + ra[a]
+            x, a = (k + 1) * nx - 2 + c, (k + 1) * count - 2 + c
+            high[2 * k + c] = own[x] + la[a] + ra[a]
+
+
+def each_plane(groups, images, k, visit):
+    own, la, ra, lb, rb = images
+    nx = sum(b - a for planes in groups for a, b in planes)
     for planes, lefts, rights in ((groups[0], la, ra), (groups[1], lb, rb)):
-        at = 0
+        at = k * sum(b - a for a, b in planes)
         for a, b in planes:
 
             def step(x, carry, shift=at - a, lefts=lefts, rights=rights):
-                visit(x, own[k, x] + lefts[k, x + shift] + rights[k, x + shift])
+                visit(x, own[k * nx + x] + lefts[x + shift] + rights[x + shift])
                 return carry
 
             lax.fori_loop(a, b, step, 0)
@@ -269,7 +343,7 @@
 def edge_kernel(
     groups, own, la, ra, lb, rb, xlo, xhi, face_lo, face_hi, first, final, s_first, s_final
 ):
-    _, nx, ny, nz = own.shape
+    nx, (ny, nz) = own.shape[0] // 2, own.shape[1:]
     for k in range(2):
 
         def put(x, cells, k=k):
@@ -281,7 +355,7 @@
 
         put(-1, xlo[2 * k + 1])
         put(nx, xhi[2 * k])
-        each_plane(groups, own, la, ra, lb, rb, k, put)
+        each_plane(groups, (own, la, ra, lb, rb), k, put)
     for faces, scr, msg in ((face_lo, s_first, first), (face_hi, s_final, final)):
         msg[0:4] = scr[...].astype(BF16)
         msg[4] = jnp.zeros(msg.shape[1:], BF16)
@@ -289,7 +363,7 @@
 
 
 def force_kernel(
-    groups, own, la, ra, lb, rb, band, xlo, xhi, ylo, yhi, adj0, adj1, bxl, bxh, byl, byh, vel,
+    groups, own, la, ra, lb, rb, band, xlo, xhi, zxl, zxh, ylo, yhi, adj0, adj1, bxl, bxh, byl, byh, vel,
     out, img, packed, frc, s_ylo, s_yhi, s_c0, s_c1, s_fl, s_fh, s_al, s_ah,
 ):
     k = pl.program_id(0)
@@ -312,7 +386,7 @@
         s_c0[pl.ds(x, 1), :] = cells[0:1]
         s_c1[pl.ds(x, 1), :] = cells[ny - 1 : ny]
 
-    each_plane(groups, own, la, ra, lb, rb, 0, fill)
+    each_plane(groups, (own, la, ra, lb, rb), 0, fill)
     every = packed[...].reshape(nx * ny, nz)
     frc[2, 1 : nx + 1] = jnp.dot(every, band[...], preferred_element_type=F32).reshape(nx, ny, nz)
     for h in range(2):
@@ -335,7 +409,7 @@
         frc[1, x + 1] = half * (up - down)
         frc[2, x + 1] = half * slope_z
 
-    for x, half in ((-1, 0.5 * this(xlo[4], bxl[...])), (nx, 0.5 * this(xhi[4], bxh[...]))):
+    for x, half in ((-1, 0.5 * this(zxl[0], bxl[...])), (nx, 0.5 * this(zxh[0], bxh[...]))):
         following, before = along_z(img[x + 2], lanes, nz)
         forces(x, half, following - before)
 
@@ -369,11 +443,12 @@
     lax.fori_loop(0, nx, smooth_step, 0)
 
 
-def force(groups, images, band, x_lo, x_hi, y_lo, y_hi, adj_zero, adj_one, halo_one, velocity):
+def force(groups, images, band, x_lo, x_hi, face_lo, face_hi, y_lo, y_hi, adj_zero, adj_one, halo_one, velocity):
     nx, ny, nz = adj_zero.shape
     block = pl.BlockSpec((1, 3, nx, ny, nz), lambda k: (k, 0, 0, 0, 0))
-    middle = [band, x_lo, x_hi, y_lo, y_hi, adj_zero, adj_one, *halo_one]
-    in_specs = [pl.BlockSpec((1,) + a.shape[1:], lambda k: (k, 0, 0, 0)) for a in images]
+    middle = [band, x_lo, x_hi, face_lo, face_hi, y_lo, y_hi, adj_zero, adj_one, *halo_one]
+    counts = [nx] + [sum(b - a for a, b in planes) for planes in groups for _ in range(2)]
+    in_specs = [pl.BlockSpec((count, ny, nz), lambda k: (k, 0, 0)) for count in counts]
     in_specs += [whole(a.shape) for a in middle] + [block]
     scratch = [
         pltpu.VMEM((nx + 4, ny, nz), F32),
@@ -419,76 +494,61 @@
     count_first = lax.axis_size("gx")
     count_second = lax.axis_size("gy")
 
-    def x_message(near, far):
-        parts = [mismatch[near].astype(BF16), mismatch[far].astype(BF16)]
-        parts += [velocity[1, 0, near], velocity[1, 0, far], velocity[1, 1, near]]
-        return jnp.stack(parts + [velocity[1, 2, near], velocity[0, 0, near]])
-
-    halo_xl = forward(x_message(nx - 1, nx - 2), "gx")
-    halo_xh = backward(x_message(0, 1), "gx")
     t_lo = forward(template, "gx")
     t_hi = backward(template, "gx")
+    low, high = column_messages(mismatch, velocity)
+    halo_xl = forward(high, "gx")
+    halo_xh = backward(low, "gx")
 
     ids = src_ids.reshape(slots)
     first_block = ids // (count_second * depth_blocks)
     second_block = ids // depth_blocks % count_second
     start = (first_block - index_first + 1) * depth_blocks + ids % depth_blocks
     side = second_block - index_second + 1
-    code = (side * (3 * depth_blocks) + start).astype(F32)
-    code = jnp.pad(code.reshape(1, slots), ((0, 0), (0, nz - slots)))
-    ins = (mismatch, velocity, halo_xl, halo_xh, code)
-    rows = struct((7, nx + 2, nz), BF16)
-    low, high = call(
+    code = (side * (3 * depth_blocks) + start).astype(BF16).reshape(1, slots)
+    left_code = forward(code, "gy")
+    right_code = backward(code, "gy")
+    lines = call(
         rows_kernel,
-        [rows] * 2,
-        [pltpu.VMEM(rows.shape, F32)] * 2,
+        [struct((8 * ny, nz), F32)] * 2,
+        [],
         "rows",
-        [whole(a.shape) for a in ins],
-    )(*ins)
-    halo_yl = forward(high, "gy")
-    halo_yh = backward(low, "gy")
-    halo = (halo_xl, halo_xh, halo_yl, halo_yh)
-
-    within = jnp.arange(edge)[None, :]
-
-    def choice(wanted, start):
-        rows = (jnp.where(wanted, start, -4 * depth_blocks)[:, None] * edge + within).reshape(1, -1)
-        return (jnp.arange(3 * nz)[:, None] == rows).astype(BF16)
-
-    def far_choice(message, side):
-        code = message[FAR_P, 0, :slots].astype(jnp.int32)
-        return choice(code // (3 * depth_blocks) == side, code % (3 * depth_blocks))
-
-    send_choice = jnp.stack([far_choice(halo_yl, 2), far_choice(halo_yh, 0)])
-    own_choice = choice(side == 1, start)[None]
+        [whole(a.shape) for a in (mismatch, velocity)],
+    )(mismatch, velocity)
+
+    send_choice, own_choice = choices(left_code, right_code, code, edge, nz)
     z = jnp.arange(nz)
     band = (z[:, None] == z[None] + 1).astype(BF16) - (z[:, None] == z[None] - 1).astype(BF16)
 
     columns = (t_lo, template, t_hi)
-    margin = nx // 8
+    margin = nx // 4
     groups = (((0, margin), (nx - margin, nx)), ((margin, nx - margin),))
-    to_left_a, to_right_a = pick(columns, send_choice, groups[0], "pick_outer")
-    from_left_a = forward(to_right_a, "gy")
-    from_right_a = backward(to_left_a, "gy")
+    to_left_a, to_right_a = pick(columns, send_choice, groups[0], "pick_outer", (*lines, halo_xl, halo_xh))
     columns, _ = lax.optimization_barrier((columns, to_left_a))
     to_left_b, to_right_b = pick(columns, send_choice, groups[1], "pick_inner")
     from_left_b = forward(to_right_b, "gy")
     from_right_b = backward(to_left_b, "gy")
+    from_left_a = forward(to_right_a, "gy")
+    from_right_a = backward(to_left_a, "gy")
 
     late_mismatch, late_choice, _ = lax.optimization_barrier((mismatch, own_choice, to_left_b))
     (own,) = pick(columns, late_choice, ((0, nx),), "pick_own")
     inside = jnp.stack(
         [index_first > 0, index_first < count_first - 1, index_second > 0, index_second < count_second - 1]
     ).astype(F32)
+    halo = (halo_xl, halo_xh, from_left_a, from_right_a)
     adj_one, *halo_one = upwind_one(inside, late_mismatch, velocity, halo)
     adj_zero, low_x, high_x, low_y, high_y = upwind_zero(adj_one, velocity, halo_one, halo)
 
-    ins = (own, from_left_a, from_right_a, low_x, high_x)
+    ins = (own, from_left_a, from_right_a)
     low, high = call(
-        outer_kernel, [struct((5, ny, nz), BF16)] * 2, [], "outer", [whole(a.shape) for a in ins]
+        functools.partial(outer_kernel, nx, 2 * margin),
+        [struct((4, ny, nz), BF16)] * 2, [], "outer", [whole(a.shape) for a in ins]
     )(*ins)
     x_lo = forward(high, "gx")
     x_hi = backward(low, "gx")
+    face_lo = forward(high_x, "gx")
+    face_hi = backward(low_x, "gx")
 
     images = (own, from_left_a, from_right_a, from_left_b, from_right_b)
     ins = (*images, x_lo, x_hi, low_y, high_y)
@@ -501,7 +561,9 @@
     )(*ins)
     y_lo = forward(final, "gy")
     y_hi = backward(first, "gy")
-    return force(groups, images, band, x_lo, x_hi, y_lo, y_hi, adj_zero, adj_one, halo_one, velocity)
+    return force(
+        groups, images, band, x_lo, x_hi, face_lo, face_hi, y_lo, y_hi, adj_zero, adj_one, halo_one, velocity
+    )
 
 
 def solution(mesh):

time: 164 us -> 149 us (0.909)
  the two profiles are of different devices: /device:TPU:225 before, /device:TPU:26 now
where the time goes in v3:
time: 149 us; the launch traced here: 147 us
  starting transfers between devices  73.3 us (49%)
  Pallas kernels  40.5 us (27%)
  waiting for transfers between devices  25.8 us (17%)
  local copies, waits for them, and re-layouts  6.12 us (4%)
    ppermute x8, starting transfers between devices, backward(): return lax.ppermute(value, axis, [(i + 1, i) for i in range(ends)])  57.3 us
    ppermute x8, waiting for transfers between devices, backward(): return lax.ppermute(value, axis, [(i + 1, i) for i in range(ends)])  18.9 us
    ppermute x8, starting transfers between devices, forward(): return lax.ppermute(value, axis, [(i, i + 1) for i in range(ends)])  16.1 us
    pallas_call x1, Pallas kernels, force(): call(functools.partial(force_kernel, groups), struct((2, 3, nx, ny, nz),...  14.1 us
    pallas_call x3, Pallas kernels, pick(): call(functools.partial(pick_kernel, planes), outs, [], name, in_specs)(*ins)  8.63 us
    pallas_call x1, Pallas kernels, upwind_one(): call(upwind_one_kernel, outs, scratch, 'upwind_one', in_specs)  6.99 us
    ppermute x8, waiting for transfers between devices, forward(): return lax.ppermute(value, axis, [(i, i + 1) for i in range(ends)])  6.9 us
    pallas_call x1, Pallas kernels, upwind_zero(): call(upwind_zero_kernel, outs, scratch, 'upwind_zero', in_specs)  6.61 us
  transfers between devices with their start and end apart: 16, of which 5 were waited for; matrix products, arithmetic and copies ran while one was open for 1% of the time, Pallas kernels for 16%

profile of v3, /device:TPU:26, one launch (start us, length us, event | category | flops | bytes accessed | tf_op | source)
XLA Modules:
  0.0 146.9 jit_solution(3960859530150845456)
XLA Ops:
  0.0 8.7 %collective-permute-start.1 = (bf16[32,32,256]{2,1,0:T(8,128)(2,1)}, bf16[32,32,256]{2,1,0:T(8,128)(2,1)}, u32[]{:S(2)}, u32[]{:S(2)}) collective-permute-start(bf16[32,32,256]{2,1,0:T(8,128)(2,1)} %t_own.3), channel_id=1, source_target_pairs={{16,0},{32,16},{48,32},{64,48},{80,64},{96,80},{112,96},{128,112},... | collective-permute-start | bytes 1572872 | tf_op jit(solution)/shard_map/ppermute | solution.py:484
  8.7 1.9 %collective-permute-start = (bf16[32,32,256]{2,1,0:T(8,128)(2,1)}, bf16[32,32,256]{2,1,0:T(8,128)(2,1)}, u32[]{:S(2)}, u32[]{:S(2)}) collective-permute-start(bf16[32,32,256]{2,1,0:T(8,128)(2,1)} %t_own.3), channel_id=1, source_target_pairs={{0,16},{16,32},{32,48},{48,64},{64,80},{80,96},{96,112},{112,128},... | collective-permute-start | bytes 1572872 | tf_op jit(solution)/shard_map/ppermute | solution.py:479
  14.4 2.5 %collective-permute-start.4 = (bf16[7,32,256]{2,1,0:T(8,128)(2,1)}, bf16[7,32,256]{2,1,0:T(8,128)(2,1)S(1)}, u32[]{:S(2)}, u32[]{:S(2)}) collective-permute-start(bf16[7,32,256]{2,1,0:T(8,128)(2,1)} %get-tuple-element.37), channel_id=1, source_target_pairs={{0,16},{16,32},{32,48},{48,64},{64,80},{80,96},{96,112},{112,128},... | collective-permute-start | bytes 344072 | tf_op jit(solution)/shard_map/ppermute | solution.py:479
  17.0 8.0 %collective-permute-start.5 = (bf16[7,32,256]{2,1,0:T(8,128)(2,1)S(1)}, bf16[7,32,256]{2,1,0:T(8,128)(2,1)S(1)}, u32[]{:S(2)}, u32[]{:S(2)}) collective-permute-start(bf16[7,32,256]{2,1,0:T(8,128)(2,1)S(1)} %get-tuple-element.38), channel_id=1, source_target_pairs={{16,0},{32,16},{48,32},{64,48},{80,64},{96,80},{112,96},{128,112},... | collective-permute-start | bytes 344072 | tf_op jit(solution)/shard_map/ppermute | solution.py:484
  26.2 3.8 %collective-permute-start.3 = (bf16[1,16]{1,0:T(2,128)(2,1)S(1)}, bf16[1,16]{1,0:T(2,128)(2,1)S(1)}, u32[]{:S(2)}, u32[]{:S(2)}) collective-permute-start(bf16[1,16]{1,0:T(2,128)(2,1)S(1)} %fusion.9.own), channel_id=1, source_target_pairs={{1,0},{2,1},{3,2},{4,3},{5,4},{6,5},{7,6},{8,7},{9,8},{10,9},{11,1... | collective-permute-start | bytes 104 | tf_op jit(solution)/shard_map/ppermute | solution.py:484
  31.9 5.2 %collective-permute-done.3.right = bf16[1,16]{1,0:T(2,128)(2,1)S(1)} collective-permute-done((bf16[1,16]{1,0:T(2,128)(2,1)S(1)}, bf16[1,16]{1,0:T(2,128)(2,1)S(1)}, u32[]{:S(2)}, u32[]{:S(2)}) %collective-permute-start.3) | collective-permute-done | bytes 64 | tf_op jit(solution)/shard_map/ppermute | solution.py:484
  37.1 1.9 %collective-permute-start.2 = (bf16[1,16]{1,0:T(2,128)(2,1)S(1)}, bf16[1,16]{1,0:T(2,128)(2,1)S(1)}, u32[]{:S(2)}, u32[]{:S(2)}) collective-permute-start(bf16[1,16]{1,0:T(2,128)(2,1)S(1)} %fusion.9.own), channel_id=1, source_target_pairs={{0,1},{1,2},{2,3},{3,4},{4,5},{5,6},{6,7},{7,8},{8,9},{9,10},{10,1... | collective-permute-start | bytes 104 | tf_op jit(solution)/shard_map/ppermute | solution.py:479
  39.0 6.2 %collective-permute-done.2.left = bf16[1,16]{1,0:T(2,128)(2,1)S(1)} collective-permute-done((bf16[1,16]{1,0:T(2,128)(2,1)S(1)}, bf16[1,16]{1,0:T(2,128)(2,1)S(1)}, u32[]{:S(2)}, u32[]{:S(2)}) %collective-permute-start.2) | collective-permute-done | bytes 64 | tf_op jit(solution)/shard_map/ppermute | solution.py:479
  46.4 3.5 %pick_outer.1 = (bf16[40,32,256]{2,1,0:T(8,128)(2,1)}, bf16[40,32,256]{2,1,0:T(8,128)(2,1)}) custom-call(bf16[32,32,256]{2,1,0:T(8,128)(2,1)} %collective-permute-done.t_lo, bf16[32,32,256]{2,1,0:T(8,128)(2,1)S(1)} %copy-done.5, bf16[32,32,256]{2,1,0:T(8,128)(2,1)} %collective-permute-done.1.t_hi, bf16[2,768,512]{2,1,0:T(8,128)(2,1)S(1)} %get-tuple-element.34.q_ref, ...), custom_call_target="tpu_custom_call" | custom-call | tf_op jit(solution)/shard_map/pick_outer/pallas_call | solution.py:316
  51.8 6.7 %collective-permute-start.7 = (bf16[40,32,256]{2,1,0:T(8,128)(2,1)}, bf16[40,32,256]{2,1,0:T(8,128)(2,1)S(1)}, u32[]{:S(2)}, u32[]{:S(2)}) collective-permute-start(bf16[40,32,256]{2,1,0:T(8,128)(2,1)} %get-tuple-element.39), channel_id=1, source_target_pairs={{1,0},{2,1},{3,2},{4,3},{5,4},{6,5},{7,6},{8,7},{9,8},{10,9},{11,1... | collective-permute-start | bytes 1966088 | tf_op jit(solution)/shard_map/ppermute | solution.py:484
  58.5 3.0 %pick_inner.1 = (bf16[32,32,256]{2,1,0:T(8,128)(2,1)}, bf16[32,32,256]{2,1,0:T(8,128)(2,1)}) custom-call(bf16[32,32,256]{2,1,0:T(8,128)(2,1)} %collective-permute-done.t_lo, bf16[32,32,256]{2,1,0:T(8,128)(2,1)S(1)} %copy-done.5, bf16[32,32,256]{2,1,0:T(8,128)(2,1)} %collective-permute-done.1.t_hi, bf16[2,768,512]{2,1,0:T(8,128)(2,1)S(1)} %get-tuple-element.34.q_ref), custom_call_target="tpu_custom_call" | custom-call | tf_op jit(solution)/shard_map/pick_inner/pallas_call | solution.py:316
  61.5 2.1 %collective-permute-start.8 = (bf16[32,32,256]{2,1,0:T(8,128)(2,1)}, bf16[32,32,256]{2,1,0:T(8,128)(2,1)S(1)}, u32[]{:S(2)}, u32[]{:S(2)}) collective-permute-start(bf16[32,32,256]{2,1,0:T(8,128)(2,1)} %get-tuple-element.47), channel_id=1, source_target_pairs={{0,1},{1,2},{2,3},{3,4},{4,5},{5,6},{6,7},{7,8},{8,9},{9,10},{10,1... | collective-permute-start | bytes 1572872 | tf_op jit(solution)/shard_map/ppermute | solution.py:479
  63.5 6.6 %collective-permute-start.9 = (bf16[32,32,256]{2,1,0:T(8,128)(2,1)}, bf16[32,32,256]{2,1,0:T(8,128)(2,1)}, u32[]{:S(2)}, u32[]{:S(2)}) collective-permute-start(bf16[32,32,256]{2,1,0:T(8,128)(2,1)} %get-tuple-element.44), channel_id=1, source_target_pairs={{1,0},{2,1},{3,2},{4,3},{5,4},{6,5},{7,6},{8,7},{9,8},{10,9},{11,1... | collective-permute-start | bytes 1572872 | tf_op jit(solution)/shard_map/ppermute | solution.py:484
  71.4 2.2 %pick_own.1.own = bf16[64,32,256]{2,1,0:T(8,128)(2,1)S(1)} custom-call(bf16[32,32,256]{2,1,0:T(8,128)(2,1)} %collective-permute-done.t_lo, bf16[32,32,256]{2,1,0:T(8,128)(2,1)S(1)} %copy-done.6, bf16[32,32,256]{2,1,0:T(8,128)(2,1)} %collective-permute-done.1.t_hi, bf16[1,768,512]{2,1,0:T(8,128)(2,1)S(1)} %copy-done.10), custom_call_target="tpu_custom_call" | custom-call | tf_op jit(solution)/shard_map/pick_own/pallas_call | solution.py:316
  73.6 12.2 %collective-permute-done.7.ra.hyh = bf16[40,32,256]{2,1,0:T(8,128)(2,1)S(1)} collective-permute-done((bf16[40,32,256]{2,1,0:T(8,128)(2,1)}, bf16[40,32,256]{2,1,0:T(8,128)(2,1)S(1)}, u32[]{:S(2)}, u32[]{:S(2)}) %collective-permute-start.7) | collective-permute-done | bytes 655392 | tf_op jit(solution)/shard_map/ppermute | solution.py:484
  85.8 1.9 %collective-permute-start.10 = (bf16[4,32,256]{2,1,0:T(8,128)(2,1)S(1)}, bf16[4,32,256]{2,1,0:T(8,128)(2,1)S(1)}, u32[]{:S(2)}, u32[]{:S(2)}) collective-permute-start(bf16[4,32,256]{2,1,0:T(8,128)(2,1)S(1)} %get-tuple-element.48), channel_id=1, source_target_pairs={{0,16},{16,32},{32,48},{48,64},{64,80},{80,96},{96,112},{112,128},... | collective-permute-start | bytes 196616 | tf_op jit(solution)/shard_map/ppermute | solution.py:479
  87.8 8.4 %collective-permute-start.11 = (bf16[4,32,256]{2,1,0:T(8,128)(2,1)S(1)}, bf16[4,32,256]{2,1,0:T(8,128)(2,1)S(1)}, u32[]{:S(2)}, u32[]{:S(2)}) collective-permute-start(bf16[4,32,256]{2,1,0:T(8,128)(2,1)S(1)} %get-tuple-element.49), channel_id=1, source_target_pairs={{16,0},{32,16},{48,32},{64,48},{80,64},{96,80},{112,96},{128,112},... | collective-permute-start | bytes 196616 | tf_op jit(solution)/shard_map/ppermute | solution.py:484
  96.3 7.0 %upwind_one.1 = (f32[32,32,256]{2,1,0:T(8,128)S(1)}, f32[32,256]{1,0:T(8,128)S(1)}, f32[32,256]{1,0:T(8,128)S(1)}, f32[32,256]{1,0:T(8,128)S(1)}, f32[32,256]{1,0:T(8,128)S(1)}) custom-call(f32[4]{0:T(128)S(1)} %add_convert_fusion.inside, f32[32,32,256]{2,1,0:T(8,128)S(1)} %copy-done.4, bf16[2,3,32,32,256]{4,3,2,1,0:T(8,128)(2,1)} %vel.1, ...), custom_call_target="tpu_custom_call" | custom-call | tf_op jit(solution)/shard_map/upwind_one/pallas_call | solution.py:241
  103.3 6.6 %upwind_zero.1 = (f32[32,32,256]{2,1,0:T(8,128)S(1)}, bf16[1,32,256]{2,1,0:T(8,128)(2,1)S(1)}, bf16[1,32,256]{2,1,0:T(8,128)(2,1)S(1)}, bf16[1,32,256]{2,1,0:T(8,128)(2,1)S(1)}, bf16[1,32,256]{2,1,0:T(8,128)(2,1)S(1)}) custom-call(f32[32,32,256]{2,1,0:T(8,128)S(1)} %get-tuple-element.51.p_ref.adj1, bf16[2,3,32,32,256]{4,3,2,1,0:T(8,128)(2,1)} %vel.1, ...), custom_call_target="tpu_custom_call" | custom-call | tf_op jit(solution)/shard_map/upwind_zero/pallas_call | solution.py:250
  109.9 1.9 %collective-permute-start.12 = (bf16[1,32,256]{2,1,0:T(8,128)(2,1)S(1)}, bf16[1,32,256]{2,1,0:T(8,128)(2,1)S(1)}, u32[]{:S(2)}, u32[]{:S(2)}) collective-permute-start(bf16[1,32,256]{2,1,0:T(8,128)(2,1)S(1)} %get-tuple-element.56), channel_id=1, source_target_pairs={{0,16},{16,32},{32,48},{48,64},{64,80},{80,96},{96,112},{112,128},... | collective-permute-start | bytes 49160 | tf_op jit(solution)/shard_map/ppermute | solution.py:479
  111.8 8.4 %collective-permute-start.13 = (bf16[1,32,256]{2,1,0:T(8,128)(2,1)S(1)}, bf16[1,32,256]{2,1,0:T(8,128)(2,1)S(1)}, u32[]{:S(2)}, u32[]{:S(2)}) collective-permute-start(bf16[1,32,256]{2,1,0:T(8,128)(2,1)S(1)} %get-tuple-element.57), channel_id=1, source_target_pairs={{16,0},{32,16},{48,32},{64,48},{80,64},{96,80},{112,96},{128,112},... | collective-permute-start | bytes 49160 | tf_op jit(solution)/shard_map/ppermute | solution.py:484
  122.1 1.9 %collective-permute-start.14 = (bf16[5,34,256]{2,1,0:T(8,128)(2,1)S(1)}, bf16[5,34,256]{2,1,0:T(8,128)(2,1)S(1)}, u32[]{:S(2)}, u32[]{:S(2)}) collective-permute-start(bf16[5,34,256]{2,1,0:T(8,128)(2,1)S(1)} %get-tuple-element.60), channel_id=1, source_target_pairs={{0,1},{1,2},{2,3},{3,4},{4,5},{5,6},{6,7},{7,8},{8,9},{9,10},{10,1... | collective-permute-start | bytes 261128 | tf_op jit(solution)/shard_map/ppermute | solution.py:479
  124.0 6.6 %collective-permute-start.15 = (bf16[5,34,256]{2,1,0:T(8,128)(2,1)S(1)}, bf16[5,34,256]{2,1,0:T(8,128)(2,1)S(1)}, u32[]{:S(2)}, u32[]{:S(2)}) collective-permute-start(bf16[5,34,256]{2,1,0:T(8,128)(2,1)S(1)} %get-tuple-element.61), channel_id=1, source_target_pairs={{1,0},{2,1},{3,2},{4,3},{5,4},{6,5},{7,6},{8,7},{9,8},{10,9},{11,1... | collective-permute-start | bytes 261128 | tf_op jit(solution)/shard_map/ppermute | solution.py:484
  132.8 14.1 %force.1 = f32[2,3,32,32,256]{4,3,2,1,0:T(8,128)} custom-call(bf16[64,32,256]{2,1,0:T(8,128)(2,1)S(1)} %pick_own.1.own, bf16[40,32,256]{2,1,0:T(8,128)(2,1)S(1)} %collective-permute-done.6.la.hyl, bf16[40,32,256]{2,1,0:T(8,128)(2,1)S(1)} %collective-permute-done.7.ra.hyh, bf16[32,32,256]{2,1,0:T(8,128)(2,1)S(1)} %collective-permute-done.8.lb, ...), custom_call_target="tpu_custom_call" | custom-call | tf_op jit(solution)/shard_map/force/pallas_call | solution.py:466
  (50 shorter events, 15.2 us)
Async XLA Ops:
  0.0 46.4 %collective-permute-start.1 = (bf16[32,32,256]{2,1,0:T(8,128)(2,1)}, bf16[32,32,256]{2,1,0:T(8,128)(2,1)}, u32[]{:S(2)}, u32[]{:S(2)}) collective-permute-start(bf16[32,32,256]{2,1,0:T(8,128)(2,1)} %t_own.3), channel_id=1, source_target_pairs={{16,0},{32,16},{48,32},{64,48},{80,64},{96,80},{112,96},{128,112},... | collective-permute-start | bytes 1572872 | tf_op jit(solution)/shard_map/ppermute | solution.py:484
  8.7 37.7 %collective-permute-start = (bf16[32,32,256]{2,1,0:T(8,128)(2,1)}, bf16[32,32,256]{2,1,0:T(8,128)(2,1)}, u32[]{:S(2)}, u32[]{:S(2)}) collective-permute-start(bf16[32,32,256]{2,1,0:T(8,128)(2,1)} %t_own.3), channel_id=1, source_target_pairs={{0,16},{16,32},{32,48},{48,64},{64,80},{80,96},{96,112},{112,128},... | collective-permute-start | bytes 1572872 | tf_op jit(solution)/shard_map/ppermute | solution.py:479
  13.8 11.7 %copy-start.11 = (s32[2,1,1,8]{3,2,1,0:T(1,128)S(1)}, s32[2,1,1,8]{3,2,1,0:T(1,128)}, u32[]{:S(2)}) copy-start(s32[2,1,1,8]{3,2,1,0:T(1,128)} %param.7) | copy-start | bytes 196
  13.8 16.3 %copy-start.1 = (bf16[2,3,32,32,256]{4,3,2,1,0:T(8,128)(2,1)S(1)}, bf16[2,3,32,32,256]{4,3,2,1,0:T(8,128)(2,1)}, u32[]{:S(2)}) copy-start(bf16[2,3,32,32,256]{4,3,2,1,0:T(8,128)(2,1)} %vel.1) | copy-start | bytes 9437188
  14.4 31.9 %collective-permute-start.4 = (bf16[7,32,256]{2,1,0:T(8,128)(2,1)}, bf16[7,32,256]{2,1,0:T(8,128)(2,1)S(1)}, u32[]{:S(2)}, u32[]{:S(2)}) collective-permute-start(bf16[7,32,256]{2,1,0:T(8,128)(2,1)} %get-tuple-element.37), channel_id=1, source_target_pairs={{0,16},{16,32},{32,48},{48,64},{64,80},{80,96},{96,112},{112,128},... | collective-permute-start | bytes 344072 | tf_op jit(solution)/shard_map/ppermute | solution.py:479
  17.0 29.4 %collective-permute-start.5 = (bf16[7,32,256]{2,1,0:T(8,128)(2,1)S(1)}, bf16[7,32,256]{2,1,0:T(8,128)(2,1)S(1)}, u32[]{:S(2)}, u32[]{:S(2)}) collective-permute-start(bf16[7,32,256]{2,1,0:T(8,128)(2,1)S(1)} %get-tuple-element.38), channel_id=1, source_target_pairs={{16,0},{32,16},{48,32},{64,48},{80,64},{96,80},{112,96},{128,112},... | collective-permute-start | bytes 344072 | tf_op jit(solution)/shard_map/ppermute | solution.py:484
  26.2 10.9 %collective-permute-start.3 = (bf16[1,16]{1,0:T(2,128)(2,1)S(1)}, bf16[1,16]{1,0:T(2,128)(2,1)S(1)}, u32[]{:S(2)}, u32[]{:S(2)}) collective-permute-start(bf16[1,16]{1,0:T(2,128)(2,1)S(1)} %fusion.9.own), channel_id=1, source_target_pairs={{1,0},{2,1},{3,2},{4,3},{5,4},{6,5},{7,6},{8,7},{9,8},{10,9},{11,1... | collective-permute-start | bytes 104 | tf_op jit(solution)/shard_map/ppermute | solution.py:484
  31.3 15.1 %copy-start.5 = (bf16[32,32,256]{2,1,0:T(8,128)(2,1)S(1)}, bf16[32,32,256]{2,1,0:T(8,128)(2,1)}, u32[]{:S(2)}) copy-start(bf16[32,32,256]{2,1,0:T(8,128)(2,1)} %t_own.3) | copy-start | bytes 1572868
  37.1 8.1 %collective-permute-start.2 = (bf16[1,16]{1,0:T(2,128)(2,1)S(1)}, bf16[1,16]{1,0:T(2,128)(2,1)S(1)}, u32[]{:S(2)}, u32[]{:S(2)}) collective-permute-start(bf16[1,16]{1,0:T(2,128)(2,1)S(1)} %fusion.9.own), channel_id=1, source_target_pairs={{0,1},{1,2},{2,3},{3,4},{4,5},{5,6},{6,7},{7,8},{8,9},{9,10},{10,1... | collective-permute-start | bytes 104 | tf_op jit(solution)/shard_map/ppermute | solution.py:479
  46.3 15.1 %copy-start.9 = (bf16[1,768,512]{2,1,0:T(8,128)(2,1)}, bf16[1,768,512]{2,1,0:T(8,128)(2,1)S(1)}, u32[]{:S(2)}) copy-start(bf16[1,768,512]{2,1,0:T(8,128)(2,1)S(1)} %get-tuple-element.45.q_ref) | copy-start | bytes 2359300
  46.4 15.1 %copy-start.7 = (bf16[7,32,256]{2,1,0:T(8,128)(2,1)}, bf16[7,32,256]{2,1,0:T(8,128)(2,1)S(1)}, u32[]{:S(2)}) copy-start(bf16[7,32,256]{2,1,0:T(8,128)(2,1)S(1)} %collective-permute-done.5.rest_3_.hxh) | copy-start | bytes 344068
  46.4 23.8 %copy-start.6 = (bf16[32,32,256]{2,1,0:T(8,128)(2,1)S(1)}, bf16[32,32,256]{2,1,0:T(8,128)(2,1)}, u32[]{:S(2)}) copy-start(bf16[32,32,256]{2,1,0:T(8,128)(2,1)} %t_own.3) | copy-start | bytes 1572868
  49.9 23.6 %collective-permute-start.6 = (bf16[40,32,256]{2,1,0:T(8,128)(2,1)}, bf16[40,32,256]{2,1,0:T(8,128)(2,1)S(1)}, u32[]{:S(2)}, u32[]{:S(2)}) collective-permute-start(bf16[40,32,256]{2,1,0:T(8,128)(2,1)} %get-tuple-element.46), channel_id=1, source_target_pairs={{0,1},{1,2},{2,3},{3,4},{4,5},{5,6},{6,7},{7,8},{8,9},{9,10},{10,1... | collective-permute-start | bytes 1966088 | tf_op jit(solution)/shard_map/ppermute | solution.py:479
  51.8 34.0 %collective-permute-start.7 = (bf16[40,32,256]{2,1,0:T(8,128)(2,1)}, bf16[40,32,256]{2,1,0:T(8,128)(2,1)S(1)}, u32[]{:S(2)}, u32[]{:S(2)}) collective-permute-start(bf16[40,32,256]{2,1,0:T(8,128)(2,1)} %get-tuple-element.39), channel_id=1, source_target_pairs={{1,0},{2,1},{3,2},{4,3},{5,4},{6,5},{7,6},{8,7},{9,8},{10,9},{11,1... | collective-permute-start | bytes 1966088 | tf_op jit(solution)/shard_map/ppermute | solution.py:484
  61.5 34.8 %copy-start.4 = (f32[32,32,256]{2,1,0:T(8,128)S(1)}, f32[32,32,256]{2,1,0:T(8,128)}, u32[]{:S(2)}) copy-start(f32[32,32,256]{2,1,0:T(8,128)} %p_ref.2) | copy-start | bytes 3145732
  61.5 50.4 %collective-permute-start.8 = (bf16[32,32,256]{2,1,0:T(8,128)(2,1)}, bf16[32,32,256]{2,1,0:T(8,128)(2,1)S(1)}, u32[]{:S(2)}, u32[]{:S(2)}) collective-permute-start(bf16[32,32,256]{2,1,0:T(8,128)(2,1)} %get-tuple-element.47), channel_id=1, source_target_pairs={{0,1},{1,2},{2,3},{3,4},{4,5},{5,6},{6,7},{7,8},{8,9},{9,10},{10,1... | collective-permute-start | bytes 1572872 | tf_op jit(solution)/shard_map/ppermute | solution.py:479
  63.5 56.8 %collective-permute-start.9 = (bf16[32,32,256]{2,1,0:T(8,128)(2,1)}, bf16[32,32,256]{2,1,0:T(8,128)(2,1)}, u32[]{:S(2)}, u32[]{:S(2)}) collective-permute-start(bf16[32,32,256]{2,1,0:T(8,128)(2,1)} %get-tuple-element.44), channel_id=1, source_target_pairs={{1,0},{2,1},{3,2},{4,3},{5,4},{6,5},{7,6},{8,7},{9,8},{10,9},{11,1... | collective-permute-start | bytes 1572872 | tf_op jit(solution)/shard_map/ppermute | solution.py:484
  70.2 26.1 %copy-start.8 = (bf16[7,32,256]{2,1,0:T(8,128)(2,1)S(1)}, bf16[7,32,256]{2,1,0:T(8,128)(2,1)}, u32[]{:S(2)}) copy-start(bf16[7,32,256]{2,1,0:T(8,128)(2,1)} %copy-done.7) | copy-start | bytes 344068
  85.8 34.5 %collective-permute-start.10 = (bf16[4,32,256]{2,1,0:T(8,128)(2,1)S(1)}, bf16[4,32,256]{2,1,0:T(8,128)(2,1)S(1)}, u32[]{:S(2)}, u32[]{:S(2)}) collective-permute-start(bf16[4,32,256]{2,1,0:T(8,128)(2,1)S(1)} %get-tuple-element.48), channel_id=1, source_target_pairs={{0,16},{16,32},{32,48},{48,64},{64,80},{80,96},{96,112},{112,128},... | collective-permute-start | bytes 196616 | tf_op jit(solution)/shard_map/ppermute | solution.py:479
  87.8 32.6 %collective-permute-start.11 = (bf16[4,32,256]{2,1,0:T(8,128)(2,1)S(1)}, bf16[4,32,256]{2,1,0:T(8,128)(2,1)S(1)}, u32[]{:S(2)}, u32[]{:S(2)}) collective-permute-start(bf16[4,32,256]{2,1,0:T(8,128)(2,1)S(1)} %get-tuple-element.49), channel_id=1, source_target_pairs={{16,0},{32,16},{48,32},{64,48},{80,64},{96,80},{112,96},{128,112},... | collective-permute-start | bytes 196616 | tf_op jit(solution)/shard_map/ppermute | solution.py:484
  109.9 20.8 %collective-permute-start.12 = (bf16[1,32,256]{2,1,0:T(8,128)(2,1)S(1)}, bf16[1,32,256]{2,1,0:T(8,128)(2,1)S(1)}, u32[]{:S(2)}, u32[]{:S(2)}) collective-permute-start(bf16[1,32,256]{2,1,0:T(8,128)(2,1)S(1)} %get-tuple-element.56), channel_id=1, source_target_pairs={{0,16},{16,32},{32,48},{48,64},{64,80},{80,96},{96,112},{112,128},... | collective-permute-start | bytes 49160 | tf_op jit(solution)/shard_map/ppermute | solution.py:479
  111.8 18.9 %collective-permute-start.13 = (bf16[1,32,256]{2,1,0:T(8,128)(2,1)S(1)}, bf16[1,32,256]{2,1,0:T(8,128)(2,1)S(1)}, u32[]{:S(2)}, u32[]{:S(2)}) collective-permute-start(bf16[1,32,256]{2,1,0:T(8,128)(2,1)S(1)} %get-tuple-element.57), channel_id=1, source_target_pairs={{16,0},{32,16},{48,32},{64,48},{80,64},{96,80},{112,96},{128,112},... | collective-permute-start | bytes 49160 | tf_op jit(solution)/shard_map/ppermute | solution.py:484
  122.1 9.3 %collective-permute-start.14 = (bf16[5,34,256]{2,1,0:T(8,128)(2,1)S(1)}, bf16[5,34,256]{2,1,0:T(8,128)(2,1)S(1)}, u32[]{:S(2)}, u32[]{:S(2)}) collective-permute-start(bf16[5,34,256]{2,1,0:T(8,128)(2,1)S(1)} %get-tuple-element.60), channel_id=1, source_target_pairs={{0,1},{1,2},{2,3},{3,4},{4,5},{5,6},{6,7},{7,8},{8,9},{9,10},{10,1... | collective-permute-start | bytes 261128 | tf_op jit(solution)/shard_map/ppermute | solution.py:479
  124.0 8.9 %collective-permute-start.15 = (bf16[5,34,256]{2,1,0:T(8,128)(2,1)S(1)}, bf16[5,34,256]{2,1,0:T(8,128)(2,1)S(1)}, u32[]{:S(2)}, u32[]{:S(2)}) collective-permute-start(bf16[5,34,256]{2,1,0:T(8,128)(2,1)S(1)} %get-tuple-element.61), channel_id=1, source_target_pairs={{1,0},{2,1},{3,2},{4,3},{5,4},{6,5},{7,6},{8,7},{9,8},{10,9},{11,1... | collective-permute-start | bytes 261128 | tf_op jit(solution)/shard_map/ppermute | solution.py:484
  (4 other events, 5.5 us)

commit v4 on v2

--- a/solution.py
+++ b/solution.py
@@ -61,6 +61,35 @@
 
 
 NEAR_P, FAR_P, NEAR_N, FAR_N, NEAR_T, NEAR_Z, NEAR_EARLY = range(7)
+
+
+def column_kernel(p_any, v_any, low, high, p_lo, p_hi, v_lo, v_hi, sem):
+    nx = p_any.shape[0]
+    copies = []
+    for at, (p, v, x) in enumerate(((p_lo, v_lo, 0), (p_hi, v_hi, nx - 2))):
+        copies.append(pltpu.make_async_copy(p_any.at[pl.ds(x, 2)], p, sem.at[2 * at]))
+        copies.append(pltpu.make_async_copy(v_any.at[:, :, pl.ds(x, 2)], v, sem.at[2 * at + 1]))
+    for copy in copies:
+        copy.start()
+    for copy in copies:
+        copy.wait()
+    for msg, p, v, near, far in ((low, p_lo, v_lo, 0, 1), (high, p_hi, v_hi, 1, 0)):
+        msg[NEAR_P] = p[near].astype(BF16)
+        msg[FAR_P] = p[far].astype(BF16)
+        msg[NEAR_N] = v[1, 0, near]
+        msg[FAR_N] = v[1, 0, far]
+        msg[NEAR_T] = v[1, 1, near]
+        msg[NEAR_Z] = v[1, 2, near]
+        msg[NEAR_EARLY] = v[0, 0, near]
+
+
+def column_messages(field, velocity):
+    nx, ny, nz = field.shape
+    outs = [struct((7, ny, nz), BF16)] * 2
+    scratch = [pltpu.VMEM((2, ny, nz), F32)] * 2
+    scratch += [pltpu.VMEM((2, 3, 2, ny, nz), BF16)] * 2 + [pltpu.SemaphoreType.DMA((4,))]
+    in_specs = [pl.BlockSpec(memory_space=pltpu.HBM)] * 2
+    return call(column_kernel, outs, scratch, "columns", in_specs)(field, velocity)
 
 
 def rows_kernel(p_ref, v_ref, hxl, hxh, code, lo, hi, s_lo, s_hi):
@@ -219,47 +248,77 @@
     )
 
 
+def choice_kernel(edge, blocks, left, right, own, send, keep):
+    _, height, width = keep.shape
+    nz = own.shape[1]
+    lane = lax.broadcasted_iota(jnp.int32, (nz, width), 1)
+    slot = lax.broadcasted_iota(jnp.int32, (nz, width), 0)
+    spread = jnp.where(lane // edge == slot, 1.0, 0.0).astype(BF16)
+    row = lax.broadcasted_iota(jnp.int32, (height, width), 0)
+    within = lax.broadcasted_iota(jnp.int32, (8, width), 1) % edge
+    codes = (left[FAR_P, 0:1, :].astype(F32), right[FAR_P, 0:1, :].astype(F32), own[...])
+    for code, side, out, d in zip(codes, (2, 0, 1), (send, send, keep), (0, 1, 0)):
+        code = jnp.broadcast_to(code, (8, nz)).astype(BF16)
+        code = jnp.dot(code, spread, preferred_element_type=F32).astype(jnp.int32)
+        start = (code - side * blocks) * edge
+        good = (start >= 0) & (start < height)
+        wanted = jnp.where(good, start + within, -1)[0:1]
+        out[d] = jnp.where(row == wanted, 1.0, 0.0).astype(BF16)
+
+
+def choices(left, right, own, edge, slots):
+    nz = own.shape[1]
+    outs = [struct((count, 3 * nz, slots * edge), BF16) for count in (2, 1)]
+    kernel = functools.partial(choice_kernel, edge, 3 * nz // edge)
+    in_specs = [whole(a.shape) for a in (left, right, own)]
+    return call(kernel, outs, [], "choices", in_specs)(left, right, own)
+
+
+def planes_of(ref, planes):
+    ny, width = ref.shape[1:]
+    parts = [ref[a:b].reshape((b - a) * ny, width) for a, b in planes]
+    return parts[0] if len(parts) == 1 else jnp.concatenate(parts, axis=0)
+
+
 def pick_kernel(planes, t_lo, t_own, t_hi, q_ref, *outs):
-    nz = t_own.shape[2]
-    ny = t_own.shape[1]
-    blocks = []
-    for ref in (t_lo, t_own, t_hi):
-        parts = [ref[a:b].reshape((b - a) * ny, nz) for a, b in planes]
-        blocks.append(parts[0] if len(parts) == 1 else jnp.concatenate(parts, axis=0))
-    rows = jnp.concatenate(blocks, axis=1)
+    ny, nz = t_own.shape[1:]
+    rows = jnp.concatenate([planes_of(ref, planes) for ref in (t_lo, t_own, t_hi)], axis=1)
     count = rows.shape[0] // ny
     for d, out in enumerate(outs):
         got = jnp.dot(rows, q_ref[d], preferred_element_type=F32).astype(BF16)
-        out[0] = got[:, :nz].reshape(count, ny, nz)
-        out[1] = got[:, nz:].reshape(count, ny, nz)
+        out[0:count] = got[:, :nz].reshape(count, ny, nz)
+        out[count : 2 * count] = got[:, nz:].reshape(count, ny, nz)
 
 
 def pick(columns, choices, planes, name):
-    _, ny, nz = columns[0].shape
-    count = sum(b - a for a, b in planes)
-    outs = [struct((2, count, ny, nz), BF16)] * choices.shape[0]
-    in_specs = [whole(c.shape) for c in columns] + [whole(choices.shape)]
-    return call(functools.partial(pick_kernel, planes), outs, [], name, in_specs)(*columns, choices)
-
-
-def outer_kernel(own, la, ra, face_lo, face_hi, low, high):
-    nx, count = own.shape[1], la.shape[1]
+    _, ny, nz = columns[1].shape
+    count = 2 * sum(b - a for a, b in planes)
+    outs = [struct((count, ny, nz), BF16)] * choices.shape[0]
+    ins = (*columns, choices)
+    in_specs = [whole(a.shape) for a in ins]
+    return call(functools.partial(pick_kernel, planes), outs, [], name, in_specs)(*ins)
+
+
+def outer_kernel(nx, count, own, la, ra, face_lo, face_hi, low, high):
     for k in range(2):
         for c in range(2):
-            low[2 * k + c] = own[k, c] + la[k, c] + ra[k, c]
-            x, a = nx - 2 + c, count - 2 + c
-            high[2 * k + c] = own[k, x] + la[k, a] + ra[k, a]
+            x, a = k * nx + c, k * count + c
+            low[2 * k + c] = own[x] + la[a] + ra[a]
+            x, a = (k + 1) * nx - 2 + c, (k + 1) * count - 2 + c
+            high[2 * k + c] = own[x] + la[a] + ra[a]
     low[4] = face_lo[0]
     high[4] = face_hi[0]
 
 
-def each_plane(groups, own, la, ra, lb, rb, k, visit):
+def each_plane(groups, images, k, visit):
+    own, la, ra, lb, rb = images
+    nx = sum(b - a for planes in groups for a, b in planes)
     for planes, lefts, rights in ((groups[0], la, ra), (groups[1], lb, rb)):
-        at = 0
+        at = k * sum(b - a for a, b in planes)
         for a, b in planes:
 
             def step(x, carry, shift=at - a, lefts=lefts, rights=rights):
-                visit(x, own[k, x] + lefts[k, x + shift] + rights[k, x + shift])
+                visit(x, own[k * nx + x] + lefts[x + shift] + rights[x + shift])
                 return carry
 
             lax.fori_loop(a, b, step, 0)
@@ -269,7 +328,7 @@
 def edge_kernel(
     groups, own, la, ra, lb, rb, xlo, xhi, face_lo, face_hi, first, final, s_first, s_final
 ):
-    _, nx, ny, nz = own.shape
+    nx, (ny, nz) = own.shape[0] // 2, own.shape[1:]
     for k in range(2):
 
         def put(x, cells, k=k):
@@ -281,7 +340,7 @@
 
         put(-1, xlo[2 * k + 1])
         put(nx, xhi[2 * k])
-        each_plane(groups, own, la, ra, lb, rb, k, put)
+        each_plane(groups, (own, la, ra, lb, rb), k, put)
     for faces, scr, msg in ((face_lo, s_first, first), (face_hi, s_final, final)):
         msg[0:4] = scr[...].astype(BF16)
         msg[4] = jnp.zeros(msg.shape[1:], BF16)
@@ -312,7 +371,7 @@
         s_c0[pl.ds(x, 1), :] = cells[0:1]
         s_c1[pl.ds(x, 1), :] = cells[ny - 1 : ny]
 
-    each_plane(groups, own, la, ra, lb, rb, 0, fill)
+    each_plane(groups, (own, la, ra, lb, rb), 0, fill)
     every = packed[...].reshape(nx * ny, nz)
     frc[2, 1 : nx + 1] = jnp.dot(every, band[...], preferred_element_type=F32).reshape(nx, ny, nz)
     for h in range(2):
@@ -373,7 +432,8 @@
     nx, ny, nz = adj_zero.shape
     block = pl.BlockSpec((1, 3, nx, ny, nz), lambda k: (k, 0, 0, 0, 0))
     middle = [band, x_lo, x_hi, y_lo, y_hi, adj_zero, adj_one, *halo_one]
-    in_specs = [pl.BlockSpec((1,) + a.shape[1:], lambda k: (k, 0, 0, 0)) for a in images]
+    counts = [nx] + [sum(b - a for a, b in planes) for planes in groups for _ in range(2)]
+    in_specs = [pl.BlockSpec((count, ny, nz), lambda k: (k, 0, 0)) for count in counts]
     in_specs += [whole(a.shape) for a in middle] + [block]
     scratch = [
         pltpu.VMEM((nx + 4, ny, nz), F32),
@@ -419,15 +479,15 @@
     count_first = lax.axis_size("gx")
     count_second = lax.axis_size("gy")
 
-    def x_message(near, far):
-        parts = [mismatch[near].astype(BF16), mismatch[far].astype(BF16)]
-        parts += [velocity[1, 0, near], velocity[1, 0, far], velocity[1, 1, near]]
-        return jnp.stack(parts + [velocity[1, 2, near], velocity[0, 0, near]])
-
-    halo_xl = forward(x_message(nx - 1, nx - 2), "gx")
-    halo_xh = backward(x_message(0, 1), "gx")
-    t_lo = forward(template, "gx")
-    t_hi = backward(template, "gx")
+    low, high = column_messages(
+        pltpu.with_memory_space_constraint(mismatch, pltpu.HBM),
+        pltpu.with_memory_space_constraint(velocity, pltpu.HBM),
+    )
+    halo_xl = forward(high, "gx")
+    halo_xh = backward(low, "gx")
+    late_template, _ = lax.optimization_barrier((template, low))
+    t_lo = forward(late_template, "gx")
+    t_hi = backward(late_template, "gx")
 
     ids = src_ids.reshape(slots)
     first_block = ids // (count_second * depth_blocks)
@@ -448,25 +508,17 @@
     halo_yl = forward(high, "gy")
     halo_yh = backward(low, "gy")
     halo = (halo_xl, halo_xh, halo_yl, halo_yh)
-
-    within = jnp.arange(edge)[None, :]
-
-    def choice(wanted, start):
-        rows = (jnp.where(wanted, start, -4 * depth_blocks)[:, None] * edge + within).reshape(1, -1)
-        return (jnp.arange(3 * nz)[:, None] == rows).astype(BF16)
-
-    def far_choice(message, side):
-        code = message[FAR_P, 0, :slots].astype(jnp.int32)
-        return choice(code // (3 * depth_blocks) == side, code % (3 * depth_blocks))
-
-    send_choice = jnp.stack([far_choice(halo_yl, 2), far_choice(halo_yh, 0)])
-    own_choice = choice(side == 1, start)[None]
+    inside = jnp.stack(
+        [index_first > 0, index_first < count_first - 1, index_second > 0, index_second < count_second - 1]
+    ).astype(F32)
+
+    send_choice, own_choice = choices(halo_yl, halo_yh, code, edge, slots)
     z = jnp.arange(nz)
     band = (z[:, None] == z[None] + 1).astype(BF16) - (z[:, None] == z[None] - 1).astype(BF16)
 
     columns = (t_lo, template, t_hi)
-    margin = nx // 8
-    groups = (((0, margin), (nx - margin, nx)), ((margin, nx - margin),))
+    half = nx // 4
+    groups = (((0, half), (nx - half, nx)), ((half, nx - half),))
     to_left_a, to_right_a = pick(columns, send_choice, groups[0], "pick_outer")
     from_left_a = forward(to_right_a, "gy")
     from_right_a = backward(to_left_a, "gy")
@@ -474,18 +526,15 @@
     to_left_b, to_right_b = pick(columns, send_choice, groups[1], "pick_inner")
     from_left_b = forward(to_right_b, "gy")
     from_right_b = backward(to_left_b, "gy")
-
-    late_mismatch, late_choice, _ = lax.optimization_barrier((mismatch, own_choice, to_left_b))
-    (own,) = pick(columns, late_choice, ((0, nx),), "pick_own")
-    inside = jnp.stack(
-        [index_first > 0, index_first < count_first - 1, index_second > 0, index_second < count_second - 1]
-    ).astype(F32)
+    late_choice, late_mismatch, _ = lax.optimization_barrier((own_choice, mismatch, to_left_b))
     adj_one, *halo_one = upwind_one(inside, late_mismatch, velocity, halo)
     adj_zero, low_x, high_x, low_y, high_y = upwind_zero(adj_one, velocity, halo_one, halo)
+    (own,) = pick(columns, late_choice, ((0, nx),), "pick_own")
 
     ins = (own, from_left_a, from_right_a, low_x, high_x)
     low, high = call(
-        outer_kernel, [struct((5, ny, nz), BF16)] * 2, [], "outer", [whole(a.shape) for a in ins]
+        functools.partial(outer_kernel, nx, 2 * half),
+        [struct((5, ny, nz), BF16)] * 2, [], "outer", [whole(a.shape) for a in ins]
     )(*ins)
     x_lo = forward(high, "gx")
     x_hi = backward(low, "gx")
@@ -501,7 +550,9 @@
     )(*ins)
     y_lo = forward(final, "gy")
     y_hi = backward(first, "gy")
-    return force(groups, images, band, x_lo, x_hi, y_lo, y_hi, adj_zero, adj_one, halo_one, velocity)
+    return force(
+        groups, images, band, x_lo, x_hi, y_lo, y_hi, adj_zero, adj_one, halo_one, velocity
+    )
 
 
 def solution(mesh):

time: 164 us -> 142 us (0.87)
  the two profiles are of different devices: /device:TPU:225 before, /device:TPU:26 now
where the time goes in v4:
time: 142 us; the launch traced here: 141 us
  starting transfers between devices  67.6 us (48%)
  Pallas kernels  41.5 us (29%)
  waiting for transfers between devices  28.2 us (20%)
  local copies, waits for them, and re-layouts  3.11 us (2%)
    ppermute x7, starting transfers between devices, backward(): return lax.ppermute(value, axis, [(i + 1, i) for i in range(ends)])  42 us
    ppermute x7, starting transfers between devices, forward(): return lax.ppermute(value, axis, [(i, i + 1) for i in range(ends)])  25.5 us
    ppermute x7, waiting for transfers between devices, forward(): return lax.ppermute(value, axis, [(i, i + 1) for i in range(ends)])  17.3 us
    pallas_call x1, Pallas kernels, force(): call(functools.partial(force_kernel, groups), struct((2, 3, nx, ny, nz),...  14.4 us
    ppermute x7, waiting for transfers between devices, backward(): return lax.ppermute(value, axis, [(i + 1, i) for i in range(ends)])  10.9 us
    pallas_call x3, Pallas kernels, pick(): call(functools.partial(pick_kernel, planes), outs, [], name, in_specs)(*ins)  8.88 us
    pallas_call x1, Pallas kernels, upwind_one(): call(upwind_one_kernel, outs, scratch, 'upwind_one', in_specs)  6.1 us
    pallas_call x1, Pallas kernels, upwind_zero(): call(upwind_zero_kernel, outs, scratch, 'upwind_zero', in_specs)  5.15 us
  transfers between devices with their start and end apart: 14, of which 7 were waited for; matrix products, arithmetic and copies ran while one was open for 1% of the time, Pallas kernels for 14%

profile of v4, /device:TPU:26, one launch (start us, length us, event | category | flops | bytes accessed | tf_op | source)
XLA Modules:
  0.0 141.5 jit_solution(3573876288020474230)
XLA Ops:
  0.0 1.9 %columns.1 = (bf16[7,32,256]{2,1,0:T(8,128)(2,1)S(1)}, bf16[7,32,256]{2,1,0:T(8,128)(2,1)}) custom-call(f32[32,32,256]{2,1,0:T(8,128)} %p_ref.2, bf16[2,3,32,32,256]{4,3,2,1,0:T(8,128)(2,1)} %vel.1), custom_call_target="tpu_custom_call" | custom-call | tf_op jit(solution)/shard_map/columns/pallas_call | solution.py:92
  1.9 8.7 %collective-permute-start.1 = (bf16[32,32,256]{2,1,0:T(8,128)(2,1)}, bf16[32,32,256]{2,1,0:T(8,128)(2,1)}, u32[]{:S(2)}, u32[]{:S(2)}) collective-permute-start(bf16[32,32,256]{2,1,0:T(8,128)(2,1)} %t_own.3), channel_id=1, source_target_pairs={{16,0},{32,16},{48,32},{64,48},{80,64},{96,80},{112,96},{128,112},... | collective-permute-start | bytes 1572872 | tf_op jit(solution)/shard_map/ppermute | solution.py:469
  10.7 1.9 %collective-permute-start = (bf16[32,32,256]{2,1,0:T(8,128)(2,1)}, bf16[32,32,256]{2,1,0:T(8,128)(2,1)}, u32[]{:S(2)}, u32[]{:S(2)}) collective-permute-start(bf16[32,32,256]{2,1,0:T(8,128)(2,1)} %t_own.3), channel_id=1, source_target_pairs={{0,16},{16,32},{32,48},{48,64},{64,80},{80,96},{96,112},{112,128},... | collective-permute-start | bytes 1572872 | tf_op jit(solution)/shard_map/ppermute | solution.py:464
  12.6 8.4 %collective-permute-start.3 = (bf16[7,32,256]{2,1,0:T(8,128)(2,1)S(1)}, bf16[7,32,256]{2,1,0:T(8,128)(2,1)S(1)}, u32[]{:S(2)}, u32[]{:S(2)}) collective-permute-start(bf16[7,32,256]{2,1,0:T(8,128)(2,1)S(1)} %get-tuple-element.35), channel_id=1, source_target_pairs={{16,0},{32,16},{48,32},{64,48},{80,64},{96,80},{112,96},{128,112},... | collective-permute-start | bytes 344072 | tf_op jit(solution)/shard_map/ppermute | solution.py:469
  24.2 10.6 %collective-permute-done.2.hxl = bf16[7,32,256]{2,1,0:T(8,128)(2,1)S(1)} collective-permute-done((bf16[7,32,256]{2,1,0:T(8,128)(2,1)}, bf16[7,32,256]{2,1,0:T(8,128)(2,1)S(1)}, u32[]{:S(2)}, u32[]{:S(2)}) %collective-permute-start.2) | collective-permute-done | bytes 114720 | tf_op jit(solution)/shard_map/ppermute | solution.py:464
  36.7 8.7 %collective-permute-start.4 = (bf16[7,34,256]{2,1,0:T(8,128)(2,1)S(1)}, bf16[7,34,256]{2,1,0:T(8,128)(2,1)S(1)}, u32[]{:S(2)}, u32[]{:S(2)}) collective-permute-start(bf16[7,34,256]{2,1,0:T(8,128)(2,1)S(1)} %get-tuple-element.38), channel_id=1, source_target_pairs={{0,1},{1,2},{2,3},{3,4},{4,5},{5,6},{6,7},{7,8},{8,9},{9,10},{10,1... | collective-permute-start | bytes 365576 | tf_op jit(solution)/shard_map/ppermute | solution.py:464
  47.3 2.2 %collective-permute-done.4.left.hyl = bf16[7,34,256]{2,1,0:T(8,128)(2,1)S(1)} collective-permute-done((bf16[7,34,256]{2,1,0:T(8,128)(2,1)S(1)}, bf16[7,34,256]{2,1,0:T(8,128)(2,1)S(1)}, u32[]{:S(2)}, u32[]{:S(2)}) %collective-permute-start.4) | collective-permute-done | bytes 121888 | tf_op jit(solution)/shard_map/ppermute | solution.py:464
  49.5 2.9 %collective-permute-done.5.right.hyh = bf16[7,34,256]{2,1,0:T(8,128)(2,1)S(1)} collective-permute-done((bf16[7,34,256]{2,1,0:T(8,128)(2,1)S(1)}, bf16[7,34,256]{2,1,0:T(8,128)(2,1)S(1)}, u32[]{:S(2)}, u32[]{:S(2)}) %collective-permute-start.5) | collective-permute-done | bytes 121888 | tf_op jit(solution)/shard_map/ppermute | solution.py:469
  53.5 3.4 %pick_outer.1 = (bf16[32,32,256]{2,1,0:T(8,128)(2,1)}, bf16[32,32,256]{2,1,0:T(8,128)(2,1)}) custom-call(bf16[32,32,256]{2,1,0:T(8,128)(2,1)} %collective-permute-done.t_lo, bf16[32,32,256]{2,1,0:T(8,128)(2,1)} %t_own.3, bf16[32,32,256]{2,1,0:T(8,128)(2,1)} %collective-permute-done.1.t_hi, bf16[2,768,512]{2,1,0:T(8,128)(2,1)S(1)} %get-tuple-element.40.q_ref), custom_call_target="tpu_custom_call" | custom-call | tf_op jit(solution)/shard_map/pick_outer/pallas_call | solution.py:299
  56.9 2.8 %collective-permute-start.6 = (bf16[32,32,256]{2,1,0:T(8,128)(2,1)}, bf16[32,32,256]{2,1,0:T(8,128)(2,1)}, u32[]{:S(2)}, u32[]{:S(2)}) collective-permute-start(bf16[32,32,256]{2,1,0:T(8,128)(2,1)} %get-tuple-element.48), channel_id=1, source_target_pairs={{0,1},{1,2},{2,3},{3,4},{4,5},{5,6},{6,7},{7,8},{8,9},{9,10},{10,1... | collective-permute-start | bytes 1572872 | tf_op jit(solution)/shard_map/ppermute | solution.py:464
  59.7 5.7 %collective-permute-start.7 = (bf16[32,32,256]{2,1,0:T(8,128)(2,1)}, bf16[32,32,256]{2,1,0:T(8,128)(2,1)}, u32[]{:S(2)}, u32[]{:S(2)}) collective-permute-start(bf16[32,32,256]{2,1,0:T(8,128)(2,1)} %get-tuple-element.41), channel_id=1, source_target_pairs={{1,0},{2,1},{3,2},{4,3},{5,4},{6,5},{7,6},{8,7},{9,8},{10,9},{11,1... | collective-permute-start | bytes 1572872 | tf_op jit(solution)/shard_map/ppermute | solution.py:469
  65.4 3.1 %pick_inner.1 = (bf16[32,32,256]{2,1,0:T(8,128)(2,1)}, bf16[32,32,256]{2,1,0:T(8,128)(2,1)}) custom-call(bf16[32,32,256]{2,1,0:T(8,128)(2,1)} %collective-permute-done.t_lo, bf16[32,32,256]{2,1,0:T(8,128)(2,1)} %t_own.3, bf16[32,32,256]{2,1,0:T(8,128)(2,1)} %collective-permute-done.1.t_hi, bf16[2,768,512]{2,1,0:T(8,128)(2,1)S(1)} %get-tuple-element.40.q_ref), custom_call_target="tpu_custom_call" | custom-call | tf_op jit(solution)/shard_map/pick_inner/pallas_call | solution.py:299
  70.5 6.6 %collective-permute-start.9 = (bf16[32,32,256]{2,1,0:T(8,128)(2,1)}, bf16[32,32,256]{2,1,0:T(8,128)(2,1)}, u32[]{:S(2)}, u32[]{:S(2)}) collective-permute-start(bf16[32,32,256]{2,1,0:T(8,128)(2,1)} %get-tuple-element.46), channel_id=1, source_target_pairs={{1,0},{2,1},{3,2},{4,3},{5,4},{6,5},{7,6},{8,7},{9,8},{10,9},{11,1... | collective-permute-start | bytes 1572872 | tf_op jit(solution)/shard_map/ppermute | solution.py:469
  78.5 2.3 %pick_own.1.own = bf16[64,32,256]{2,1,0:T(8,128)(2,1)S(1)} custom-call(bf16[32,32,256]{2,1,0:T(8,128)(2,1)} %collective-permute-done.t_lo, bf16[32,32,256]{2,1,0:T(8,128)(2,1)} %t_own.3, bf16[32,32,256]{2,1,0:T(8,128)(2,1)} %collective-permute-done.1.t_hi, bf16[1,768,512]{2,1,0:T(8,128)(2,1)S(1)} %copy-done.6), custom_call_target="tpu_custom_call" | custom-call | tf_op jit(solution)/shard_map/pick_own/pallas_call | solution.py:299
  80.8 6.1 %upwind_one.1 = (f32[32,32,256]{2,1,0:T(8,128)S(1)}, f32[32,256]{1,0:T(8,128)S(1)}, f32[32,256]{1,0:T(8,128)S(1)}, f32[32,256]{1,0:T(8,128)S(1)}, f32[32,256]{1,0:T(8,128)S(1)}) custom-call(f32[4]{0:T(128)S(1)} %add_convert_fusion.inside, f32[32,32,256]{2,1,0:T(8,128)S(1)} %copy-done.2, bf16[2,3,32,32,256]{4,3,2,1,0:T(8,128)(2,1)S(1)} %copy-done, ...), custom_call_target="tpu_custom_call" | custom-call | tf_op jit(solution)/shard_map/upwind_one/pallas_call | solution.py:237
  86.9 5.2 %upwind_zero.1 = (f32[32,32,256]{2,1,0:T(8,128)S(1)}, bf16[1,32,256]{2,1,0:T(8,128)(2,1)S(1)}, bf16[1,32,256]{2,1,0:T(8,128)(2,1)S(1)}, bf16[1,32,256]{2,1,0:T(8,128)(2,1)S(1)}, bf16[1,32,256]{2,1,0:T(8,128)(2,1)S(1)}) custom-call(f32[32,32,256]{2,1,0:T(8,128)S(1)} %get-tuple-element.51.p_ref.adj1, bf16[2,3,32,32,256]{4,3,2,1,0:T(8,128)(2,1)S(1)} %copy-done, ...), custom_call_target="tpu_custom_call" | custom-call | tf_op jit(solution)/shard_map/upwind_zero/pallas_call | solution.py:246
  95.3 8.4 %collective-permute-start.11 = (bf16[5,32,256]{2,1,0:T(8,128)(2,1)S(1)}, bf16[5,32,256]{2,1,0:T(8,128)(2,1)S(1)}, u32[]{:S(2)}, u32[]{:S(2)}) collective-permute-start(bf16[5,32,256]{2,1,0:T(8,128)(2,1)S(1)} %get-tuple-element.59), channel_id=1, source_target_pairs={{16,0},{32,16},{48,32},{64,48},{80,64},{96,80},{112,96},{128,112},... | collective-permute-start | bytes 245768 | tf_op jit(solution)/shard_map/ppermute | solution.py:469
  103.7 4.7 %collective-permute-done.9.rb = bf16[32,32,256]{2,1,0:T(8,128)(2,1)} collective-permute-done((bf16[32,32,256]{2,1,0:T(8,128)(2,1)}, bf16[32,32,256]{2,1,0:T(8,128)(2,1)}, u32[]{:S(2)}, u32[]{:S(2)}) %collective-permute-start.9) | collective-permute-done | bytes 524320 | tf_op jit(solution)/shard_map/ppermute | solution.py:469
  108.5 3.1 %collective-permute-done.10.xlo = bf16[5,32,256]{2,1,0:T(8,128)(2,1)S(1)} collective-permute-done((bf16[5,32,256]{2,1,0:T(8,128)(2,1)S(1)}, bf16[5,32,256]{2,1,0:T(8,128)(2,1)S(1)}, u32[]{:S(2)}, u32[]{:S(2)}) %collective-permute-start.10) | collective-permute-done | bytes 81952 | tf_op jit(solution)/shard_map/ppermute | solution.py:464
  111.5 2.2 %edges.1 = (bf16[5,34,256]{2,1,0:T(8,128)(2,1)S(1)}, bf16[5,34,256]{2,1,0:T(8,128)(2,1)S(1)}) custom-call(bf16[64,32,256]{2,1,0:T(8,128)(2,1)S(1)} %pick_own.1.own, bf16[32,32,256]{2,1,0:T(8,128)(2,1)} %collective-permute-done.6.la, bf16[32,32,256]{2,1,0:T(8,128)(2,1)} %collective-permute-done.7.ra, bf16[32,32,256]{2,1,0:T(8,128)(2,1)} %collective-permute-done.8.lb, ...), custom_call_target="tpu_custom_call" | custom-call | tf_op jit(solution)/shard_map/edges/pallas_call | solution.py:544
  113.7 6.4 %collective-permute-start.12 = (bf16[5,34,256]{2,1,0:T(8,128)(2,1)S(1)}, bf16[5,34,256]{2,1,0:T(8,128)(2,1)S(1)}, u32[]{:S(2)}, u32[]{:S(2)}) collective-permute-start(bf16[5,34,256]{2,1,0:T(8,128)(2,1)S(1)} %get-tuple-element.62), channel_id=1, source_target_pairs={{0,1},{1,2},{2,3},{3,4},{4,5},{5,6},{6,7},{7,8},{8,9},{9,10},{10,1... | collective-permute-start | bytes 261128 | tf_op jit(solution)/shard_map/ppermute | solution.py:464
  120.1 2.1 %collective-permute-start.13 = (bf16[5,34,256]{2,1,0:T(8,128)(2,1)S(1)}, bf16[5,34,256]{2,1,0:T(8,128)(2,1)S(1)}, u32[]{:S(2)}, u32[]{:S(2)}) collective-permute-start(bf16[5,34,256]{2,1,0:T(8,128)(2,1)S(1)} %get-tuple-element.63), channel_id=1, source_target_pairs={{1,0},{2,1},{3,2},{4,3},{5,4},{6,5},{7,6},{8,7},{9,8},{10,9},{11,1... | collective-permute-start | bytes 261128 | tf_op jit(solution)/shard_map/ppermute | solution.py:469
  123.8 3.3 %collective-permute-done.13.yhi = bf16[5,34,256]{2,1,0:T(8,128)(2,1)S(1)} collective-permute-done((bf16[5,34,256]{2,1,0:T(8,128)(2,1)S(1)}, bf16[5,34,256]{2,1,0:T(8,128)(2,1)S(1)}, u32[]{:S(2)}, u32[]{:S(2)}) %collective-permute-start.13) | collective-permute-done | bytes 87072 | tf_op jit(solution)/shard_map/ppermute | solution.py:469
  127.1 14.4 %force.1 = f32[2,3,32,32,256]{4,3,2,1,0:T(8,128)} custom-call(bf16[64,32,256]{2,1,0:T(8,128)(2,1)S(1)} %pick_own.1.own, bf16[32,32,256]{2,1,0:T(8,128)(2,1)} %collective-permute-done.6.la, bf16[32,32,256]{2,1,0:T(8,128)(2,1)} %collective-permute-done.7.ra, bf16[32,32,256]{2,1,0:T(8,128)(2,1)} %collective-permute-done.8.lb, ...), custom_call_target="tpu_custom_call" | custom-call | tf_op jit(solution)/shard_map/force/pallas_call | solution.py:451
  (39 shorter events, 15.9 us)
Async XLA Ops:
  0.0 34.8 %copy-start = (bf16[2,3,32,32,256]{4,3,2,1,0:T(8,128)(2,1)S(1)}, bf16[2,3,32,32,256]{4,3,2,1,0:T(8,128)(2,1)}, u32[]{:S(2)}) copy-start(bf16[2,3,32,32,256]{4,3,2,1,0:T(8,128)(2,1)} %vel.1) | copy-start | bytes 9437188
  0.0 23.5 %copy-start.7 = (s32[2,1,1,8]{3,2,1,0:T(1,128)S(1)}, s32[2,1,1,8]{3,2,1,0:T(1,128)}, u32[]{:S(2)}) copy-start(s32[2,1,1,8]{3,2,1,0:T(1,128)} %param.7) | copy-start | bytes 196
  1.9 51.5 %collective-permute-start.1 = (bf16[32,32,256]{2,1,0:T(8,128)(2,1)}, bf16[32,32,256]{2,1,0:T(8,128)(2,1)}, u32[]{:S(2)}, u32[]{:S(2)}) collective-permute-start(bf16[32,32,256]{2,1,0:T(8,128)(2,1)} %t_own.3), channel_id=1, source_target_pairs={{16,0},{32,16},{48,32},{64,48},{80,64},{96,80},{112,96},{128,112},... | collective-permute-start | bytes 1572872 | tf_op jit(solution)/shard_map/ppermute | solution.py:469
  10.7 42.8 %collective-permute-start = (bf16[32,32,256]{2,1,0:T(8,128)(2,1)}, bf16[32,32,256]{2,1,0:T(8,128)(2,1)}, u32[]{:S(2)}, u32[]{:S(2)}) collective-permute-start(bf16[32,32,256]{2,1,0:T(8,128)(2,1)} %t_own.3), channel_id=1, source_target_pairs={{0,16},{16,32},{32,48},{48,64},{64,80},{80,96},{96,112},{112,128},... | collective-permute-start | bytes 1572872 | tf_op jit(solution)/shard_map/ppermute | solution.py:464
  12.6 22.2 %collective-permute-start.3 = (bf16[7,32,256]{2,1,0:T(8,128)(2,1)S(1)}, bf16[7,32,256]{2,1,0:T(8,128)(2,1)S(1)}, u32[]{:S(2)}, u32[]{:S(2)}) collective-permute-start(bf16[7,32,256]{2,1,0:T(8,128)(2,1)S(1)} %get-tuple-element.35), channel_id=1, source_target_pairs={{16,0},{32,16},{48,32},{64,48},{80,64},{96,80},{112,96},{128,112},... | collective-permute-start | bytes 344072 | tf_op jit(solution)/shard_map/ppermute | solution.py:469
  21.1 13.7 %collective-permute-start.2 = (bf16[7,32,256]{2,1,0:T(8,128)(2,1)}, bf16[7,32,256]{2,1,0:T(8,128)(2,1)S(1)}, u32[]{:S(2)}, u32[]{:S(2)}) collective-permute-start(bf16[7,32,256]{2,1,0:T(8,128)(2,1)} %get-tuple-element.37), channel_id=1, source_target_pairs={{0,16},{16,32},{32,48},{48,64},{64,80},{80,96},{96,112},{112,128},... | collective-permute-start | bytes 344072 | tf_op jit(solution)/shard_map/ppermute | solution.py:464
  34.8 1.9 %copy-start.3 = (bf16[7,32,256]{2,1,0:T(8,128)(2,1)}, bf16[7,32,256]{2,1,0:T(8,128)(2,1)S(1)}, u32[]{:S(2)}) copy-start(bf16[7,32,256]{2,1,0:T(8,128)(2,1)S(1)} %collective-permute-done.2.hxl) | copy-start | bytes 344068
  34.8 1.3 copy-start.1
  36.7 12.8 %collective-permute-start.4 = (bf16[7,34,256]{2,1,0:T(8,128)(2,1)S(1)}, bf16[7,34,256]{2,1,0:T(8,128)(2,1)S(1)}, u32[]{:S(2)}, u32[]{:S(2)}) collective-permute-start(bf16[7,34,256]{2,1,0:T(8,128)(2,1)S(1)} %get-tuple-element.38), channel_id=1, source_target_pairs={{0,1},{1,2},{2,3},{3,4},{4,5},{5,6},{6,7},{7,8},{8,9},{9,10},{10,1... | collective-permute-start | bytes 365576 | tf_op jit(solution)/shard_map/ppermute | solution.py:464
  45.3 7.0 %collective-permute-start.5 = (bf16[7,34,256]{2,1,0:T(8,128)(2,1)S(1)}, bf16[7,34,256]{2,1,0:T(8,128)(2,1)S(1)}, u32[]{:S(2)}, u32[]{:S(2)}) collective-permute-start(bf16[7,34,256]{2,1,0:T(8,128)(2,1)S(1)} %get-tuple-element.39), channel_id=1, source_target_pairs={{1,0},{2,1},{3,2},{4,3},{5,4},{6,5},{7,6},{8,7},{9,8},{10,9},{11,1... | collective-permute-start | bytes 365576 | tf_op jit(solution)/shard_map/ppermute | solution.py:469
  53.5 15.1 %copy-start.5 = (bf16[1,768,512]{2,1,0:T(8,128)(2,1)}, bf16[1,768,512]{2,1,0:T(8,128)(2,1)S(1)}, u32[]{:S(2)}) copy-start(bf16[1,768,512]{2,1,0:T(8,128)(2,1)S(1)} %get-tuple-element.47.q_ref) | copy-start | bytes 2359300
  56.9 35.2 %collective-permute-start.6 = (bf16[32,32,256]{2,1,0:T(8,128)(2,1)}, bf16[32,32,256]{2,1,0:T(8,128)(2,1)}, u32[]{:S(2)}, u32[]{:S(2)}) collective-permute-start(bf16[32,32,256]{2,1,0:T(8,128)(2,1)} %get-tuple-element.48), channel_id=1, source_target_pairs={{0,1},{1,2},{2,3},{3,4},{4,5},{5,6},{6,7},{7,8},{8,9},{9,10},{10,1... | collective-permute-start | bytes 1572872 | tf_op jit(solution)/shard_map/ppermute | solution.py:464
  59.7 32.4 %collective-permute-start.7 = (bf16[32,32,256]{2,1,0:T(8,128)(2,1)}, bf16[32,32,256]{2,1,0:T(8,128)(2,1)}, u32[]{:S(2)}, u32[]{:S(2)}) collective-permute-start(bf16[32,32,256]{2,1,0:T(8,128)(2,1)} %get-tuple-element.41), channel_id=1, source_target_pairs={{1,0},{2,1},{3,2},{4,3},{5,4},{6,5},{7,6},{8,7},{9,8},{10,9},{11,1... | collective-permute-start | bytes 1572872 | tf_op jit(solution)/shard_map/ppermute | solution.py:469
  68.6 35.1 %collective-permute-start.8 = (bf16[32,32,256]{2,1,0:T(8,128)(2,1)}, bf16[32,32,256]{2,1,0:T(8,128)(2,1)}, u32[]{:S(2)}, u32[]{:S(2)}) collective-permute-start(bf16[32,32,256]{2,1,0:T(8,128)(2,1)} %get-tuple-element.49), channel_id=1, source_target_pairs={{0,1},{1,2},{2,3},{3,4},{4,5},{5,6},{6,7},{7,8},{8,9},{9,10},{10,1... | collective-permute-start | bytes 1572872 | tf_op jit(solution)/shard_map/ppermute | solution.py:464
  70.5 38.0 %collective-permute-start.9 = (bf16[32,32,256]{2,1,0:T(8,128)(2,1)}, bf16[32,32,256]{2,1,0:T(8,128)(2,1)}, u32[]{:S(2)}, u32[]{:S(2)}) collective-permute-start(bf16[32,32,256]{2,1,0:T(8,128)(2,1)} %get-tuple-element.46), channel_id=1, source_target_pairs={{1,0},{2,1},{3,2},{4,3},{5,4},{6,5},{7,6},{8,7},{9,8},{10,9},{11,1... | collective-permute-start | bytes 1572872 | tf_op jit(solution)/shard_map/ppermute | solution.py:469
  77.2 3.7 %copy-start.2 = (f32[32,32,256]{2,1,0:T(8,128)S(1)}, f32[32,32,256]{2,1,0:T(8,128)}, u32[]{:S(2)}) copy-start(f32[32,32,256]{2,1,0:T(8,128)} %p_ref.2) | copy-start | bytes 3145732
  77.2 3.6 %copy-start.4 = (bf16[7,32,256]{2,1,0:T(8,128)(2,1)S(1)}, bf16[7,32,256]{2,1,0:T(8,128)(2,1)}, u32[]{:S(2)}) copy-start(bf16[7,32,256]{2,1,0:T(8,128)(2,1)} %copy-done.3) | copy-start | bytes 344068
  77.3 1.2 copy-start.6
  93.3 18.2 %collective-permute-start.10 = (bf16[5,32,256]{2,1,0:T(8,128)(2,1)S(1)}, bf16[5,32,256]{2,1,0:T(8,128)(2,1)S(1)}, u32[]{:S(2)}, u32[]{:S(2)}) collective-permute-start(bf16[5,32,256]{2,1,0:T(8,128)(2,1)S(1)} %get-tuple-element.58), channel_id=1, source_target_pairs={{0,16},{16,32},{32,48},{48,64},{64,80},{80,96},{96,112},{112,128},... | collective-permute-start | bytes 245768 | tf_op jit(solution)/shard_map/ppermute | solution.py:464
  95.3 16.3 %collective-permute-start.11 = (bf16[5,32,256]{2,1,0:T(8,128)(2,1)S(1)}, bf16[5,32,256]{2,1,0:T(8,128)(2,1)S(1)}, u32[]{:S(2)}, u32[]{:S(2)}) collective-permute-start(bf16[5,32,256]{2,1,0:T(8,128)(2,1)S(1)} %get-tuple-element.59), channel_id=1, source_target_pairs={{16,0},{32,16},{48,32},{64,48},{80,64},{96,80},{112,96},{128,112},... | collective-permute-start | bytes 245768 | tf_op jit(solution)/shard_map/ppermute | solution.py:469
  113.7 10.1 %collective-permute-start.12 = (bf16[5,34,256]{2,1,0:T(8,128)(2,1)S(1)}, bf16[5,34,256]{2,1,0:T(8,128)(2,1)S(1)}, u32[]{:S(2)}, u32[]{:S(2)}) collective-permute-start(bf16[5,34,256]{2,1,0:T(8,128)(2,1)S(1)} %get-tuple-element.62), channel_id=1, source_target_pairs={{0,1},{1,2},{2,3},{3,4},{4,5},{5,6},{6,7},{7,8},{8,9},{9,10},{10,1... | collective-permute-start | bytes 261128 | tf_op jit(solution)/shard_map/ppermute | solution.py:464
  120.1 7.0 %collective-permute-start.13 = (bf16[5,34,256]{2,1,0:T(8,128)(2,1)S(1)}, bf16[5,34,256]{2,1,0:T(8,128)(2,1)S(1)}, u32[]{:S(2)}, u32[]{:S(2)}) collective-permute-start(bf16[5,34,256]{2,1,0:T(8,128)(2,1)S(1)} %get-tuple-element.63), channel_id=1, source_target_pairs={{1,0},{2,1},{3,2},{4,3},{5,4},{6,5},{7,6},{8,7},{9,8},{10,9},{11,1... | collective-permute-start | bytes 261128 | tf_op jit(solution)/shard_map/ppermute | solution.py:469

commit v5 on v4

--- a/solution.py
+++ b/solution.py
@@ -16,11 +16,11 @@
     return pl.BlockSpec(shape, lambda *_: (0,) * len(shape))
 
 
-def call(kernel, outs, scratch, name, in_specs, out_specs=None, steps=1):
+def call(kernel, outs, scratch, name, in_specs, out_specs=None, steps=(1,)):
     return pl.pallas_call(
         kernel,
         name=name,
-        grid=(steps,),
+        grid=steps,
         in_specs=in_specs,
         out_specs=out_specs or [whole(o.shape) for o in outs],
         out_shape=outs,
@@ -321,7 +321,7 @@
                 visit(x, own[k * nx + x] + lefts[x + shift] + rights[x + shift])
                 return carry
 
-            lax.fori_loop(a, b, step, 0)
+            lax.fori_loop(a, b, step, 0, unroll=8)
             at += b - a
 
 
@@ -352,6 +352,8 @@
     out, img, packed, frc, s_ylo, s_yhi, s_c0, s_c1, s_fl, s_fh, s_al, s_ah,
 ):
     k = pl.program_id(0)
+    chunk = pl.program_id(1)
+    deep = out.shape[2]
     nx, ny, nz = adj0.shape
     rows = lax.broadcasted_iota(jnp.int32, (ny, nz), 0)
     lanes = lax.broadcasted_iota(jnp.int32, (ny, nz), 1)
@@ -360,61 +362,64 @@
     def this(zero, one):
         return jnp.where(first_image, zero.astype(F32), one.astype(F32))
 
-    for h in range(2):
-        img[h] = xlo[2 * k + h].astype(F32)
-        img[nx + 2 + h] = xhi[2 * k + h].astype(F32)
-
-    def fill(x, cells):
-        packed[x] = cells
-        cells = cells.astype(F32)
-        img[x + 2] = cells
-        s_c0[pl.ds(x, 1), :] = cells[0:1]
-        s_c1[pl.ds(x, 1), :] = cells[ny - 1 : ny]
-
-    each_plane(groups, (own, la, ra, lb, rb), 0, fill)
-    every = packed[...].reshape(nx * ny, nz)
-    frc[2, 1 : nx + 1] = jnp.dot(every, band[...], preferred_element_type=F32).reshape(nx, ny, nz)
-    for h in range(2):
-        s_ylo[h] = ylo[2 * k + h].astype(F32)
-        s_yhi[h] = yhi[2 * k + h].astype(F32)
-    s_al[...] = this(ylo[4, 0:nx], byl[...])
-    s_ah[...] = this(yhi[4, 0:nx], byh[...])
-
     def along_z(cells, index, length):
         following = jnp.where(index == length - 1, 0.0, pltpu.roll(cells, length - 1, 1))
         before = jnp.where(index == 0, 0.0, pltpu.roll(cells, 1, 1))
         return following, before
 
-    def forces(x, half, slope_z):
-        cells = img[x + 2]
-        at = pl.ds(x + 1, 1)
-        frc[0, x + 1] = half * (img[x + 3] - img[x + 1])
-        up = jnp.where(rows == ny - 1, s_yhi[0, at, :], pltpu.roll(cells, ny - 1, 0))
-        down = jnp.where(rows == 0, s_ylo[1, at, :], pltpu.roll(cells, 1, 0))
-        frc[1, x + 1] = half * (up - down)
-        frc[2, x + 1] = half * slope_z
-
-    for x, half in ((-1, 0.5 * this(xlo[4], bxl[...])), (nx, 0.5 * this(xhi[4], bxh[...]))):
-        following, before = along_z(img[x + 2], lanes, nz)
-        forces(x, half, following - before)
-
-    def force_step(x, carry):
-        forces(x, 0.5 * this(adj0[x], adj1[x]), frc[2, x + 1])
-        return carry
-
-    lax.fori_loop(0, nx, force_step, 0)
-    lines = lax.broadcasted_iota(jnp.int32, (nx, nz), 1)
-    for cols, near, far, beside, half, dest, sign in (
-        (s_ylo, 1, 0, s_c0, s_al, s_fl, 1.0),
-        (s_yhi, 0, 1, s_c1, s_ah, s_fh, -1.0),
-    ):
-        weight = 0.5 * half[...]
-        dest[0] = weight * (cols[near, 2 : nx + 2, :] - cols[near, 0:nx, :])
-        dest[1] = (sign * weight) * (beside[...] - cols[far, 1 : nx + 1, :])
-        following, before = along_z(cols[near, 1 : nx + 1, :], lines, nz)
-        dest[2] = weight * (following - before)
-
-    def smooth_step(x, carry):
+    @pl.when(chunk == 0)
+    def _():
+        for h in range(2):
+            img[h] = xlo[2 * k + h].astype(F32)
+            img[nx + 2 + h] = xhi[2 * k + h].astype(F32)
+
+        def fill(x, cells):
+            packed[x] = cells
+            cells = cells.astype(F32)
+            img[x + 2] = cells
+            s_c0[pl.ds(x, 1), :] = cells[0:1]
+            s_c1[pl.ds(x, 1), :] = cells[ny - 1 : ny]
+
+        each_plane(groups, (own, la, ra, lb, rb), 0, fill)
+        every = packed[...].reshape(nx * ny, nz)
+        frc[2, 1 : nx + 1] = jnp.dot(every, band[...], preferred_element_type=F32).reshape(nx, ny, nz)
+        for h in range(2):
+            s_ylo[h] = ylo[2 * k + h].astype(F32)
+            s_yhi[h] = yhi[2 * k + h].astype(F32)
+        s_al[...] = this(ylo[4, 0:nx], byl[...])
+        s_ah[...] = this(yhi[4, 0:nx], byh[...])
+
+        def forces(x, half, slope_z):
+            cells = img[x + 2]
+            at = pl.ds(x + 1, 1)
+            frc[0, x + 1] = half * (img[x + 3] - img[x + 1])
+            up = jnp.where(rows == ny - 1, s_yhi[0, at, :], pltpu.roll(cells, ny - 1, 0))
+            down = jnp.where(rows == 0, s_ylo[1, at, :], pltpu.roll(cells, 1, 0))
+            frc[1, x + 1] = half * (up - down)
+            frc[2, x + 1] = half * slope_z
+
+        for x, half in ((-1, 0.5 * this(xlo[4], bxl[...])), (nx, 0.5 * this(xhi[4], bxh[...]))):
+            following, before = along_z(img[x + 2], lanes, nz)
+            forces(x, half, following - before)
+
+        def force_step(x, carry):
+            forces(x, 0.5 * this(adj0[x], adj1[x]), frc[2, x + 1])
+            return carry
+
+        lax.fori_loop(0, nx, force_step, 0, unroll=8)
+        lines = lax.broadcasted_iota(jnp.int32, (nx, nz), 1)
+        for cols, near, far, beside, half, dest, sign in (
+            (s_ylo, 1, 0, s_c0, s_al, s_fl, 1.0),
+            (s_yhi, 0, 1, s_c1, s_ah, s_fh, -1.0),
+        ):
+            weight = 0.5 * half[...]
+            dest[0] = weight * (cols[near, 2 : nx + 2, :] - cols[near, 0:nx, :])
+            dest[1] = (sign * weight) * (beside[...] - cols[far, 1 : nx + 1, :])
+            following, before = along_z(cols[near, 1 : nx + 1, :], lines, nz)
+            dest[2] = weight * (following - before)
+
+    def smooth_step(i, carry):
+        x = chunk * deep + i
         at = pl.ds(x, 1)
         for c in range(3):
             f = frc[c, x + 1]
@@ -422,18 +427,19 @@
             down = jnp.where(rows == 0, s_fl[c, at, :], pltpu.roll(f, 1, 0))
             following, before = along_z(f, lanes, nz)
             beside = (frc[c, x] + frc[c, x + 2]) + (up + down) + (following + before)
-            out[0, c, x] = vel[0, c, x].astype(F32) + (0.25 * f + 0.125 * beside)
+            out[0, c, i] = vel[0, c, i].astype(F32) + (0.25 * f + 0.125 * beside)
         return carry
 
-    lax.fori_loop(0, nx, smooth_step, 0)
+    lax.fori_loop(0, deep, smooth_step, 0, unroll=8)
 
 
 def force(groups, images, band, x_lo, x_hi, y_lo, y_hi, adj_zero, adj_one, halo_one, velocity):
     nx, ny, nz = adj_zero.shape
-    block = pl.BlockSpec((1, 3, nx, ny, nz), lambda k: (k, 0, 0, 0, 0))
+    deep = nx // 2
+    block = pl.BlockSpec((1, 3, deep, ny, nz), lambda k, i: (k, 0, i, 0, 0))
     middle = [band, x_lo, x_hi, y_lo, y_hi, adj_zero, adj_one, *halo_one]
     counts = [nx] + [sum(b - a for a, b in planes) for planes in groups for _ in range(2)]
-    in_specs = [pl.BlockSpec((count, ny, nz), lambda k: (k, 0, 0)) for count in counts]
+    in_specs = [pl.BlockSpec((count, ny, nz), lambda k, i: (k, 0, 0)) for count in counts]
     in_specs += [whole(a.shape) for a in middle] + [block]
     scratch = [
         pltpu.VMEM((nx + 4, ny, nz), F32),
@@ -455,7 +461,7 @@
         "force",
         in_specs,
         block,
-        2,
+        (2, 2),
     )(*images, *middle, velocity)
 
 

time: 142 us -> 137 us (0.965)
  Pallas kernels: 41.5 us -> 36.8 us
    pallas_call x1, Pallas kernels: 14.4 us -> 10.1 us  [force(): call(functools.partial(force_kernel, groups), struct((2, 3, nx, ny, nz),...]
where the time goes in v5:
time: 137 us; the launch traced here: 136 us
  starting transfers between devices  67.6 us (49%)
  Pallas kernels  36.8 us (27%)
  waiting for transfers between devices  27.9 us (20%)
  local copies, waits for them, and re-layouts  3.11 us (2%)
    ppermute x7, starting transfers between devices, backward(): return lax.ppermute(value, axis, [(i + 1, i) for i in range(ends)])  42 us
    ppermute x7, starting transfers between devices, forward(): return lax.ppermute(value, axis, [(i, i + 1) for i in range(ends)])  25.5 us
    ppermute x7, waiting for transfers between devices, forward(): return lax.ppermute(value, axis, [(i, i + 1) for i in range(ends)])  17.5 us
    ppermute x7, waiting for transfers between devices, backward(): return lax.ppermute(value, axis, [(i + 1, i) for i in range(ends)])  10.3 us
    pallas_call x1, Pallas kernels, force(): call(functools.partial(force_kernel, groups), struct((2, 3, nx, ny, nz),...  10.1 us
    pallas_call x3, Pallas kernels, pick(): call(functools.partial(pick_kernel, planes), outs, [], name, in_specs)(*ins)  8.88 us
    pallas_call x1, Pallas kernels, upwind_one(): call(upwind_one_kernel, outs, scratch, 'upwind_one', in_specs)  6.1 us
    pallas_call x1, Pallas kernels, upwind_zero(): call(upwind_zero_kernel, outs, scratch, 'upwind_zero', in_specs)  5.15 us
  transfers between devices with their start and end apart: 14, of which 7 were waited for; matrix products, arithmetic and copies ran while one was open for 1% of the time, Pallas kernels for 14%

profile of v5, /device:TPU:26, one launch (start us, length us, event | category | flops | bytes accessed | tf_op | source)
XLA Modules:
  0.0 136.4 jit_solution(4061828784700774486)
XLA Ops:
  0.0 1.9 %columns.1 = (bf16[7,32,256]{2,1,0:T(8,128)(2,1)S(1)}, bf16[7,32,256]{2,1,0:T(8,128)(2,1)}) custom-call(f32[32,32,256]{2,1,0:T(8,128)} %p_ref.2, bf16[2,3,32,32,256]{4,3,2,1,0:T(8,128)(2,1)} %vel.1), custom_call_target="tpu_custom_call" | custom-call | tf_op jit(solution)/shard_map/columns/pallas_call | solution.py:92
  1.9 8.7 %collective-permute-start.1 = (bf16[32,32,256]{2,1,0:T(8,128)(2,1)}, bf16[32,32,256]{2,1,0:T(8,128)(2,1)}, u32[]{:S(2)}, u32[]{:S(2)}) collective-permute-start(bf16[32,32,256]{2,1,0:T(8,128)(2,1)} %t_own.3), channel_id=1, source_target_pairs={{16,0},{32,16},{48,32},{64,48},{80,64},{96,80},{112,96},{128,112},... | collective-permute-start | bytes 1572872 | tf_op jit(solution)/shard_map/ppermute | solution.py:475
  10.7 1.9 %collective-permute-start = (bf16[32,32,256]{2,1,0:T(8,128)(2,1)}, bf16[32,32,256]{2,1,0:T(8,128)(2,1)}, u32[]{:S(2)}, u32[]{:S(2)}) collective-permute-start(bf16[32,32,256]{2,1,0:T(8,128)(2,1)} %t_own.3), channel_id=1, source_target_pairs={{0,16},{16,32},{32,48},{48,64},{64,80},{80,96},{96,112},{112,128},... | collective-permute-start | bytes 1572872 | tf_op jit(solution)/shard_map/ppermute | solution.py:470
  12.6 8.4 %collective-permute-start.3 = (bf16[7,32,256]{2,1,0:T(8,128)(2,1)S(1)}, bf16[7,32,256]{2,1,0:T(8,128)(2,1)S(1)}, u32[]{:S(2)}, u32[]{:S(2)}) collective-permute-start(bf16[7,32,256]{2,1,0:T(8,128)(2,1)S(1)} %get-tuple-element.35), channel_id=1, source_target_pairs={{16,0},{32,16},{48,32},{64,48},{80,64},{96,80},{112,96},{128,112},... | collective-permute-start | bytes 344072 | tf_op jit(solution)/shard_map/ppermute | solution.py:475
  24.2 10.6 %collective-permute-done.2.hxl = bf16[7,32,256]{2,1,0:T(8,128)(2,1)S(1)} collective-permute-done((bf16[7,32,256]{2,1,0:T(8,128)(2,1)}, bf16[7,32,256]{2,1,0:T(8,128)(2,1)S(1)}, u32[]{:S(2)}, u32[]{:S(2)}) %collective-permute-start.2) | collective-permute-done | bytes 114720 | tf_op jit(solution)/shard_map/ppermute | solution.py:470
  36.7 8.7 %collective-permute-start.4 = (bf16[7,34,256]{2,1,0:T(8,128)(2,1)S(1)}, bf16[7,34,256]{2,1,0:T(8,128)(2,1)S(1)}, u32[]{:S(2)}, u32[]{:S(2)}) collective-permute-start(bf16[7,34,256]{2,1,0:T(8,128)(2,1)S(1)} %get-tuple-element.38), channel_id=1, source_target_pairs={{0,1},{1,2},{2,3},{3,4},{4,5},{5,6},{6,7},{7,8},{8,9},{9,10},{10,1... | collective-permute-start | bytes 365576 | tf_op jit(solution)/shard_map/ppermute | solution.py:470
  45.3 1.9 %collective-permute-start.5 = (bf16[7,34,256]{2,1,0:T(8,128)(2,1)S(1)}, bf16[7,34,256]{2,1,0:T(8,128)(2,1)S(1)}, u32[]{:S(2)}, u32[]{:S(2)}) collective-permute-start(bf16[7,34,256]{2,1,0:T(8,128)(2,1)S(1)} %get-tuple-element.39), channel_id=1, source_target_pairs={{1,0},{2,1},{3,2},{4,3},{5,4},{6,5},{7,6},{8,7},{9,8},{10,9},{11,1... | collective-permute-start | bytes 365576 | tf_op jit(solution)/shard_map/ppermute | solution.py:475
  47.3 2.2 %collective-permute-done.4.left.hyl = bf16[7,34,256]{2,1,0:T(8,128)(2,1)S(1)} collective-permute-done((bf16[7,34,256]{2,1,0:T(8,128)(2,1)S(1)}, bf16[7,34,256]{2,1,0:T(8,128)(2,1)S(1)}, u32[]{:S(2)}, u32[]{:S(2)}) %collective-permute-start.4) | collective-permute-done | bytes 121888 | tf_op jit(solution)/shard_map/ppermute | solution.py:470
  49.5 2.9 %collective-permute-done.5.right.hyh = bf16[7,34,256]{2,1,0:T(8,128)(2,1)S(1)} collective-permute-done((bf16[7,34,256]{2,1,0:T(8,128)(2,1)S(1)}, bf16[7,34,256]{2,1,0:T(8,128)(2,1)S(1)}, u32[]{:S(2)}, u32[]{:S(2)}) %collective-permute-start.5) | collective-permute-done | bytes 121888 | tf_op jit(solution)/shard_map/ppermute | solution.py:475
  53.5 3.4 %pick_outer.1 = (bf16[32,32,256]{2,1,0:T(8,128)(2,1)}, bf16[32,32,256]{2,1,0:T(8,128)(2,1)}) custom-call(bf16[32,32,256]{2,1,0:T(8,128)(2,1)} %collective-permute-done.t_lo, bf16[32,32,256]{2,1,0:T(8,128)(2,1)} %t_own.3, bf16[32,32,256]{2,1,0:T(8,128)(2,1)} %collective-permute-done.1.t_hi, bf16[2,768,512]{2,1,0:T(8,128)(2,1)S(1)} %get-tuple-element.40.q_ref), custom_call_target="tpu_custom_call" | custom-call | tf_op jit(solution)/shard_map/pick_outer/pallas_call | solution.py:299
  56.9 2.8 %collective-permute-start.6 = (bf16[32,32,256]{2,1,0:T(8,128)(2,1)}, bf16[32,32,256]{2,1,0:T(8,128)(2,1)}, u32[]{:S(2)}, u32[]{:S(2)}) collective-permute-start(bf16[32,32,256]{2,1,0:T(8,128)(2,1)} %get-tuple-element.48), channel_id=1, source_target_pairs={{0,1},{1,2},{2,3},{3,4},{4,5},{5,6},{6,7},{7,8},{8,9},{9,10},{10,1... | collective-permute-start | bytes 1572872 | tf_op jit(solution)/shard_map/ppermute | solution.py:470
  59.7 5.7 %collective-permute-start.7 = (bf16[32,32,256]{2,1,0:T(8,128)(2,1)}, bf16[32,32,256]{2,1,0:T(8,128)(2,1)}, u32[]{:S(2)}, u32[]{:S(2)}) collective-permute-start(bf16[32,32,256]{2,1,0:T(8,128)(2,1)} %get-tuple-element.41), channel_id=1, source_target_pairs={{1,0},{2,1},{3,2},{4,3},{5,4},{6,5},{7,6},{8,7},{9,8},{10,9},{11,1... | collective-permute-start | bytes 1572872 | tf_op jit(solution)/shard_map/ppermute | solution.py:475
  65.4 3.1 %pick_inner.1 = (bf16[32,32,256]{2,1,0:T(8,128)(2,1)}, bf16[32,32,256]{2,1,0:T(8,128)(2,1)}) custom-call(bf16[32,32,256]{2,1,0:T(8,128)(2,1)} %collective-permute-done.t_lo, bf16[32,32,256]{2,1,0:T(8,128)(2,1)} %t_own.3, bf16[32,32,256]{2,1,0:T(8,128)(2,1)} %collective-permute-done.1.t_hi, bf16[2,768,512]{2,1,0:T(8,128)(2,1)S(1)} %get-tuple-element.40.q_ref), custom_call_target="tpu_custom_call" | custom-call | tf_op jit(solution)/shard_map/pick_inner/pallas_call | solution.py:299
  70.5 6.6 %collective-permute-start.9 = (bf16[32,32,256]{2,1,0:T(8,128)(2,1)}, bf16[32,32,256]{2,1,0:T(8,128)(2,1)}, u32[]{:S(2)}, u32[]{:S(2)}) collective-permute-start(bf16[32,32,256]{2,1,0:T(8,128)(2,1)} %get-tuple-element.46), channel_id=1, source_target_pairs={{1,0},{2,1},{3,2},{4,3},{5,4},{6,5},{7,6},{8,7},{9,8},{10,9},{11,1... | collective-permute-start | bytes 1572872 | tf_op jit(solution)/shard_map/ppermute | solution.py:475
  78.5 2.3 %pick_own.1.own = bf16[64,32,256]{2,1,0:T(8,128)(2,1)S(1)} custom-call(bf16[32,32,256]{2,1,0:T(8,128)(2,1)} %collective-permute-done.t_lo, bf16[32,32,256]{2,1,0:T(8,128)(2,1)} %t_own.3, bf16[32,32,256]{2,1,0:T(8,128)(2,1)} %collective-permute-done.1.t_hi, bf16[1,768,512]{2,1,0:T(8,128)(2,1)S(1)} %copy-done.6), custom_call_target="tpu_custom_call" | custom-call | tf_op jit(solution)/shard_map/pick_own/pallas_call | solution.py:299
  80.8 6.1 %upwind_one.1 = (f32[32,32,256]{2,1,0:T(8,128)S(1)}, f32[32,256]{1,0:T(8,128)S(1)}, f32[32,256]{1,0:T(8,128)S(1)}, f32[32,256]{1,0:T(8,128)S(1)}, f32[32,256]{1,0:T(8,128)S(1)}) custom-call(f32[4]{0:T(128)S(1)} %add_convert_fusion.inside, f32[32,32,256]{2,1,0:T(8,128)S(1)} %copy-done.2, bf16[2,3,32,32,256]{4,3,2,1,0:T(8,128)(2,1)S(1)} %copy-done, ...), custom_call_target="tpu_custom_call" | custom-call | tf_op jit(solution)/shard_map/upwind_one/pallas_call | solution.py:237
  86.9 5.2 %upwind_zero.1 = (f32[32,32,256]{2,1,0:T(8,128)S(1)}, bf16[1,32,256]{2,1,0:T(8,128)(2,1)S(1)}, bf16[1,32,256]{2,1,0:T(8,128)(2,1)S(1)}, bf16[1,32,256]{2,1,0:T(8,128)(2,1)S(1)}, bf16[1,32,256]{2,1,0:T(8,128)(2,1)S(1)}) custom-call(f32[32,32,256]{2,1,0:T(8,128)S(1)} %get-tuple-element.51.p_ref.adj1, bf16[2,3,32,32,256]{4,3,2,1,0:T(8,128)(2,1)S(1)} %copy-done, ...), custom_call_target="tpu_custom_call" | custom-call | tf_op jit(solution)/shard_map/upwind_zero/pallas_call | solution.py:246
  95.3 8.4 %collective-permute-start.11 = (bf16[5,32,256]{2,1,0:T(8,128)(2,1)S(1)}, bf16[5,32,256]{2,1,0:T(8,128)(2,1)S(1)}, u32[]{:S(2)}, u32[]{:S(2)}) collective-permute-start(bf16[5,32,256]{2,1,0:T(8,128)(2,1)S(1)} %get-tuple-element.59), channel_id=1, source_target_pairs={{16,0},{32,16},{48,32},{64,48},{80,64},{96,80},{112,96},{128,112},... | collective-permute-start | bytes 245768 | tf_op jit(solution)/shard_map/ppermute | solution.py:475
  103.7 4.7 %collective-permute-done.9.rb = bf16[32,32,256]{2,1,0:T(8,128)(2,1)} collective-permute-done((bf16[32,32,256]{2,1,0:T(8,128)(2,1)}, bf16[32,32,256]{2,1,0:T(8,128)(2,1)}, u32[]{:S(2)}, u32[]{:S(2)}) %collective-permute-start.9) | collective-permute-done | bytes 524320 | tf_op jit(solution)/shard_map/ppermute | solution.py:475
  108.5 3.1 %collective-permute-done.10.xlo = bf16[5,32,256]{2,1,0:T(8,128)(2,1)S(1)} collective-permute-done((bf16[5,32,256]{2,1,0:T(8,128)(2,1)S(1)}, bf16[5,32,256]{2,1,0:T(8,128)(2,1)S(1)}, u32[]{:S(2)}, u32[]{:S(2)}) %collective-permute-start.10) | collective-permute-done | bytes 81952 | tf_op jit(solution)/shard_map/ppermute | solution.py:470
  113.3 6.4 %collective-permute-start.12 = (bf16[5,34,256]{2,1,0:T(8,128)(2,1)S(1)}, bf16[5,34,256]{2,1,0:T(8,128)(2,1)S(1)}, u32[]{:S(2)}, u32[]{:S(2)}) collective-permute-start(bf16[5,34,256]{2,1,0:T(8,128)(2,1)S(1)} %get-tuple-element.62), channel_id=1, source_target_pairs={{0,1},{1,2},{2,3},{3,4},{4,5},{5,6},{6,7},{7,8},{8,9},{9,10},{10,1... | collective-permute-start | bytes 261128 | tf_op jit(solution)/shard_map/ppermute | solution.py:470
  119.7 2.1 %collective-permute-start.13 = (bf16[5,34,256]{2,1,0:T(8,128)(2,1)S(1)}, bf16[5,34,256]{2,1,0:T(8,128)(2,1)S(1)}, u32[]{:S(2)}, u32[]{:S(2)}) collective-permute-start(bf16[5,34,256]{2,1,0:T(8,128)(2,1)S(1)} %get-tuple-element.63), channel_id=1, source_target_pairs={{1,0},{2,1},{3,2},{4,3},{5,4},{6,5},{7,6},{8,7},{9,8},{10,9},{11,1... | collective-permute-start | bytes 261128 | tf_op jit(solution)/shard_map/ppermute | solution.py:475
  123.6 2.7 %collective-permute-done.13.yhi = bf16[5,34,256]{2,1,0:T(8,128)(2,1)S(1)} collective-permute-done((bf16[5,34,256]{2,1,0:T(8,128)(2,1)S(1)}, bf16[5,34,256]{2,1,0:T(8,128)(2,1)S(1)}, u32[]{:S(2)}, u32[]{:S(2)}) %collective-permute-start.13) | collective-permute-done | bytes 87072 | tf_op jit(solution)/shard_map/ppermute | solution.py:475
  126.3 10.1 %force.1 = f32[2,3,32,32,256]{4,3,2,1,0:T(8,128)} custom-call(bf16[64,32,256]{2,1,0:T(8,128)(2,1)S(1)} %pick_own.1.own, bf16[32,32,256]{2,1,0:T(8,128)(2,1)} %collective-permute-done.6.la, bf16[32,32,256]{2,1,0:T(8,128)(2,1)} %collective-permute-done.7.ra, bf16[32,32,256]{2,1,0:T(8,128)(2,1)} %collective-permute-done.8.lb, ...), custom_call_target="tpu_custom_call" | custom-call | tf_op jit(solution)/shard_map/force/pallas_call | solution.py:457
  (39 shorter events, 16.0 us)
Async XLA Ops:
  0.0 34.8 %copy-start = (bf16[2,3,32,32,256]{4,3,2,1,0:T(8,128)(2,1)S(1)}, bf16[2,3,32,32,256]{4,3,2,1,0:T(8,128)(2,1)}, u32[]{:S(2)}) copy-start(bf16[2,3,32,32,256]{4,3,2,1,0:T(8,128)(2,1)} %vel.1) | copy-start | bytes 9437188
  0.0 23.5 %copy-start.7 = (s32[2,1,1,8]{3,2,1,0:T(1,128)S(1)}, s32[2,1,1,8]{3,2,1,0:T(1,128)}, u32[]{:S(2)}) copy-start(s32[2,1,1,8]{3,2,1,0:T(1,128)} %param.7) | copy-start | bytes 196
  1.9 51.5 %collective-permute-start.1 = (bf16[32,32,256]{2,1,0:T(8,128)(2,1)}, bf16[32,32,256]{2,1,0:T(8,128)(2,1)}, u32[]{:S(2)}, u32[]{:S(2)}) collective-permute-start(bf16[32,32,256]{2,1,0:T(8,128)(2,1)} %t_own.3), channel_id=1, source_target_pairs={{16,0},{32,16},{48,32},{64,48},{80,64},{96,80},{112,96},{128,112},... | collective-permute-start | bytes 1572872 | tf_op jit(solution)/shard_map/ppermute | solution.py:475
  10.7 42.8 %collective-permute-start = (bf16[32,32,256]{2,1,0:T(8,128)(2,1)}, bf16[32,32,256]{2,1,0:T(8,128)(2,1)}, u32[]{:S(2)}, u32[]{:S(2)}) collective-permute-start(bf16[32,32,256]{2,1,0:T(8,128)(2,1)} %t_own.3), channel_id=1, source_target_pairs={{0,16},{16,32},{32,48},{48,64},{64,80},{80,96},{96,112},{112,128},... | collective-permute-start | bytes 1572872 | tf_op jit(solution)/shard_map/ppermute | solution.py:470
  12.6 22.2 %collective-permute-start.3 = (bf16[7,32,256]{2,1,0:T(8,128)(2,1)S(1)}, bf16[7,32,256]{2,1,0:T(8,128)(2,1)S(1)}, u32[]{:S(2)}, u32[]{:S(2)}) collective-permute-start(bf16[7,32,256]{2,1,0:T(8,128)(2,1)S(1)} %get-tuple-element.35), channel_id=1, source_target_pairs={{16,0},{32,16},{48,32},{64,48},{80,64},{96,80},{112,96},{128,112},... | collective-permute-start | bytes 344072 | tf_op jit(solution)/shard_map/ppermute | solution.py:475
  21.1 13.7 %collective-permute-start.2 = (bf16[7,32,256]{2,1,0:T(8,128)(2,1)}, bf16[7,32,256]{2,1,0:T(8,128)(2,1)S(1)}, u32[]{:S(2)}, u32[]{:S(2)}) collective-permute-start(bf16[7,32,256]{2,1,0:T(8,128)(2,1)} %get-tuple-element.37), channel_id=1, source_target_pairs={{0,16},{16,32},{32,48},{48,64},{64,80},{80,96},{96,112},{112,128},... | collective-permute-start | bytes 344072 | tf_op jit(solution)/shard_map/ppermute | solution.py:470
  34.8 1.9 %copy-start.3 = (bf16[7,32,256]{2,1,0:T(8,128)(2,1)}, bf16[7,32,256]{2,1,0:T(8,128)(2,1)S(1)}, u32[]{:S(2)}) copy-start(bf16[7,32,256]{2,1,0:T(8,128)(2,1)S(1)} %collective-permute-done.2.hxl) | copy-start | bytes 344068
  34.8 1.3 copy-start.1
  36.7 12.8 %collective-permute-start.4 = (bf16[7,34,256]{2,1,0:T(8,128)(2,1)S(1)}, bf16[7,34,256]{2,1,0:T(8,128)(2,1)S(1)}, u32[]{:S(2)}, u32[]{:S(2)}) collective-permute-start(bf16[7,34,256]{2,1,0:T(8,128)(2,1)S(1)} %get-tuple-element.38), channel_id=1, source_target_pairs={{0,1},{1,2},{2,3},{3,4},{4,5},{5,6},{6,7},{7,8},{8,9},{9,10},{10,1... | collective-permute-start | bytes 365576 | tf_op jit(solution)/shard_map/ppermute | solution.py:470
  45.3 7.0 %collective-permute-start.5 = (bf16[7,34,256]{2,1,0:T(8,128)(2,1)S(1)}, bf16[7,34,256]{2,1,0:T(8,128)(2,1)S(1)}, u32[]{:S(2)}, u32[]{:S(2)}) collective-permute-start(bf16[7,34,256]{2,1,0:T(8,128)(2,1)S(1)} %get-tuple-element.39), channel_id=1, source_target_pairs={{1,0},{2,1},{3,2},{4,3},{5,4},{6,5},{7,6},{8,7},{9,8},{10,9},{11,1... | collective-permute-start | bytes 365576 | tf_op jit(solution)/shard_map/ppermute | solution.py:475
  53.5 15.1 %copy-start.5 = (bf16[1,768,512]{2,1,0:T(8,128)(2,1)}, bf16[1,768,512]{2,1,0:T(8,128)(2,1)S(1)}, u32[]{:S(2)}) copy-start(bf16[1,768,512]{2,1,0:T(8,128)(2,1)S(1)} %get-tuple-element.47.q_ref) | copy-start | bytes 2359300
  56.9 35.2 %collective-permute-start.6 = (bf16[32,32,256]{2,1,0:T(8,128)(2,1)}, bf16[32,32,256]{2,1,0:T(8,128)(2,1)}, u32[]{:S(2)}, u32[]{:S(2)}) collective-permute-start(bf16[32,32,256]{2,1,0:T(8,128)(2,1)} %get-tuple-element.48), channel_id=1, source_target_pairs={{0,1},{1,2},{2,3},{3,4},{4,5},{5,6},{6,7},{7,8},{8,9},{9,10},{10,1... | collective-permute-start | bytes 1572872 | tf_op jit(solution)/shard_map/ppermute | solution.py:470
  59.7 32.4 %collective-permute-start.7 = (bf16[32,32,256]{2,1,0:T(8,128)(2,1)}, bf16[32,32,256]{2,1,0:T(8,128)(2,1)}, u32[]{:S(2)}, u32[]{:S(2)}) collective-permute-start(bf16[32,32,256]{2,1,0:T(8,128)(2,1)} %get-tuple-element.41), channel_id=1, source_target_pairs={{1,0},{2,1},{3,2},{4,3},{5,4},{6,5},{7,6},{8,7},{9,8},{10,9},{11,1... | collective-permute-start | bytes 1572872 | tf_op jit(solution)/shard_map/ppermute | solution.py:475
  68.6 35.1 %collective-permute-start.8 = (bf16[32,32,256]{2,1,0:T(8,128)(2,1)}, bf16[32,32,256]{2,1,0:T(8,128)(2,1)}, u32[]{:S(2)}, u32[]{:S(2)}) collective-permute-start(bf16[32,32,256]{2,1,0:T(8,128)(2,1)} %get-tuple-element.49), channel_id=1, source_target_pairs={{0,1},{1,2},{2,3},{3,4},{4,5},{5,6},{6,7},{7,8},{8,9},{9,10},{10,1... | collective-permute-start | bytes 1572872 | tf_op jit(solution)/shard_map/ppermute | solution.py:470
  70.5 38.0 %collective-permute-start.9 = (bf16[32,32,256]{2,1,0:T(8,128)(2,1)}, bf16[32,32,256]{2,1,0:T(8,128)(2,1)}, u32[]{:S(2)}, u32[]{:S(2)}) collective-permute-start(bf16[32,32,256]{2,1,0:T(8,128)(2,1)} %get-tuple-element.46), channel_id=1, source_target_pairs={{1,0},{2,1},{3,2},{4,3},{5,4},{6,5},{7,6},{8,7},{9,8},{10,9},{11,1... | collective-permute-start | bytes 1572872 | tf_op jit(solution)/shard_map/ppermute | solution.py:475
  77.2 3.7 %copy-start.2 = (f32[32,32,256]{2,1,0:T(8,128)S(1)}, f32[32,32,256]{2,1,0:T(8,128)}, u32[]{:S(2)}) copy-start(f32[32,32,256]{2,1,0:T(8,128)} %p_ref.2) | copy-start | bytes 3145732
  77.2 3.6 %copy-start.4 = (bf16[7,32,256]{2,1,0:T(8,128)(2,1)S(1)}, bf16[7,32,256]{2,1,0:T(8,128)(2,1)}, u32[]{:S(2)}) copy-start(bf16[7,32,256]{2,1,0:T(8,128)(2,1)} %copy-done.3) | copy-start | bytes 344068
  77.3 1.2 copy-start.6
  93.3 18.2 %collective-permute-start.10 = (bf16[5,32,256]{2,1,0:T(8,128)(2,1)S(1)}, bf16[5,32,256]{2,1,0:T(8,128)(2,1)S(1)}, u32[]{:S(2)}, u32[]{:S(2)}) collective-permute-start(bf16[5,32,256]{2,1,0:T(8,128)(2,1)S(1)} %get-tuple-element.58), channel_id=1, source_target_pairs={{0,16},{16,32},{32,48},{48,64},{64,80},{80,96},{96,112},{112,128},... | collective-permute-start | bytes 245768 | tf_op jit(solution)/shard_map/ppermute | solution.py:470
  95.3 16.3 %collective-permute-start.11 = (bf16[5,32,256]{2,1,0:T(8,128)(2,1)S(1)}, bf16[5,32,256]{2,1,0:T(8,128)(2,1)S(1)}, u32[]{:S(2)}, u32[]{:S(2)}) collective-permute-start(bf16[5,32,256]{2,1,0:T(8,128)(2,1)S(1)} %get-tuple-element.59), channel_id=1, source_target_pairs={{16,0},{32,16},{48,32},{64,48},{80,64},{96,80},{112,96},{128,112},... | collective-permute-start | bytes 245768 | tf_op jit(solution)/shard_map/ppermute | solution.py:475
  113.3 10.3 %collective-permute-start.12 = (bf16[5,34,256]{2,1,0:T(8,128)(2,1)S(1)}, bf16[5,34,256]{2,1,0:T(8,128)(2,1)S(1)}, u32[]{:S(2)}, u32[]{:S(2)}) collective-permute-start(bf16[5,34,256]{2,1,0:T(8,128)(2,1)S(1)} %get-tuple-element.62), channel_id=1, source_target_pairs={{0,1},{1,2},{2,3},{3,4},{4,5},{5,6},{6,7},{7,8},{8,9},{9,10},{10,1... | collective-permute-start | bytes 261128 | tf_op jit(solution)/shard_map/ppermute | solution.py:470
  119.7 6.6 %collective-permute-start.13 = (bf16[5,34,256]{2,1,0:T(8,128)(2,1)S(1)}, bf16[5,34,256]{2,1,0:T(8,128)(2,1)S(1)}, u32[]{:S(2)}, u32[]{:S(2)}) collective-permute-start(bf16[5,34,256]{2,1,0:T(8,128)(2,1)S(1)} %get-tuple-element.63), channel_id=1, source_target_pairs={{1,0},{2,1},{3,2},{4,3},{5,4},{6,5},{7,6},{8,7},{9,8},{10,9},{11,1... | collective-permute-start | bytes 261128 | tf_op jit(solution)/shard_map/ppermute | solution.py:475

commit v6 on v3

--- a/solution.py
+++ b/solution.py
@@ -16,11 +16,11 @@
     return pl.BlockSpec(shape, lambda *_: (0,) * len(shape))
 
 
-def call(kernel, outs, scratch, name, in_specs, out_specs=None, steps=1):
+def call(kernel, outs, scratch, name, in_specs, out_specs=None, steps=(1,)):
     return pl.pallas_call(
         kernel,
         name=name,
-        grid=(steps,),
+        grid=steps,
         in_specs=in_specs,
         out_specs=out_specs or [whole(o.shape) for o in outs],
         out_shape=outs,
@@ -63,7 +63,16 @@
 NEAR_P, FAR_P, NEAR_N, FAR_N, NEAR_T, NEAR_Z, NEAR_EARLY = range(7)
 
 
-def column_kernel(p_lo, p_hi, v_lo, v_hi, low, high):
+def column_kernel(p_any, v_any, low, high, p_lo, p_hi, v_lo, v_hi, sem):
+    nx = p_any.shape[0]
+    copies = []
+    for at, (p, v, x) in enumerate(((p_lo, v_lo, 0), (p_hi, v_hi, nx - 2))):
+        copies.append(pltpu.make_async_copy(p_any.at[pl.ds(x, 2)], p, sem.at[2 * at]))
+        copies.append(pltpu.make_async_copy(v_any.at[:, :, pl.ds(x, 2)], v, sem.at[2 * at + 1]))
+    for copy in copies:
+        copy.start()
+    for copy in copies:
+        copy.wait()
     for msg, p, v, near, far in ((low, p_lo, v_lo, 0, 1), (high, p_hi, v_hi, 1, 0)):
         msg[NEAR_P] = p[near].astype(BF16)
         msg[FAR_P] = p[far].astype(BF16)
@@ -76,14 +85,11 @@
 
 def column_messages(field, velocity):
     nx, ny, nz = field.shape
-    in_specs = [pl.BlockSpec((2, ny, nz), lambda *_, b=b: (b, 0, 0)) for b in (0, nx // 2 - 1)]
-    in_specs += [
-        pl.BlockSpec((2, 3, 2, ny, nz), lambda *_, b=b: (0, 0, b, 0, 0)) for b in (0, nx // 2 - 1)
-    ]
     outs = [struct((7, ny, nz), BF16)] * 2
-    return call(column_kernel, outs, [], "columns", in_specs)(
-        field, field, velocity, velocity
-    )
+    scratch = [pltpu.VMEM((2, ny, nz), F32)] * 2
+    scratch += [pltpu.VMEM((2, 3, 2, ny, nz), BF16)] * 2 + [pltpu.SemaphoreType.DMA((4,))]
+    in_specs = [pl.BlockSpec(memory_space=pltpu.HBM)] * 2
+    return call(column_kernel, outs, scratch, "columns", in_specs)(field, velocity)
 
 
 def rows_kernel(p_ref, v_ref, lo, hi):
@@ -316,13 +322,15 @@
     return call(functools.partial(pick_kernel, planes), outs, [], name, in_specs)(*ins)
 
 
-def outer_kernel(nx, count, own, la, ra, low, high):
+def outer_kernel(nx, count, own, la, ra, face_lo, face_hi, low, high):
     for k in range(2):
         for c in range(2):
             x, a = k * nx + c, k * count + c
             low[2 * k + c] = own[x] + la[a] + ra[a]
             x, a = (k + 1) * nx - 2 + c, (k + 1) * count - 2 + c
             high[2 * k + c] = own[x] + la[a] + ra[a]
+    low[4] = face_lo[0]
+    high[4] = face_hi[0]
 
 
 def each_plane(groups, images, k, visit):
@@ -336,7 +344,7 @@
                 visit(x, own[k * nx + x] + lefts[x + shift] + rights[x + shift])
                 return carry
 
-            lax.fori_loop(a, b, step, 0)
+            lax.fori_loop(a, b, step, 0, unroll=8)
             at += b - a
 
 
@@ -363,10 +371,12 @@
 
 
 def force_kernel(
-    groups, own, la, ra, lb, rb, band, xlo, xhi, zxl, zxh, ylo, yhi, adj0, adj1, bxl, bxh, byl, byh, vel,
+    groups, own, la, ra, lb, rb, band, xlo, xhi, ylo, yhi, adj0, adj1, bxl, bxh, byl, byh, vel,
     out, img, packed, frc, s_ylo, s_yhi, s_c0, s_c1, s_fl, s_fh, s_al, s_ah,
 ):
     k = pl.program_id(0)
+    chunk = pl.program_id(1)
+    deep = out.shape[2]
     nx, ny, nz = adj0.shape
     rows = lax.broadcasted_iota(jnp.int32, (ny, nz), 0)
     lanes = lax.broadcasted_iota(jnp.int32, (ny, nz), 1)
@@ -375,61 +385,64 @@
     def this(zero, one):
         return jnp.where(first_image, zero.astype(F32), one.astype(F32))
 
-    for h in range(2):
-        img[h] = xlo[2 * k + h].astype(F32)
-        img[nx + 2 + h] = xhi[2 * k + h].astype(F32)
-
-    def fill(x, cells):
-        packed[x] = cells
-        cells = cells.astype(F32)
-        img[x + 2] = cells
-        s_c0[pl.ds(x, 1), :] = cells[0:1]
-        s_c1[pl.ds(x, 1), :] = cells[ny - 1 : ny]
-
-    each_plane(groups, (own, la, ra, lb, rb), 0, fill)
-    every = packed[...].reshape(nx * ny, nz)
-    frc[2, 1 : nx + 1] = jnp.dot(every, band[...], preferred_element_type=F32).reshape(nx, ny, nz)
-    for h in range(2):
-        s_ylo[h] = ylo[2 * k + h].astype(F32)
-        s_yhi[h] = yhi[2 * k + h].astype(F32)
-    s_al[...] = this(ylo[4, 0:nx], byl[...])
-    s_ah[...] = this(yhi[4, 0:nx], byh[...])
-
     def along_z(cells, index, length):
         following = jnp.where(index == length - 1, 0.0, pltpu.roll(cells, length - 1, 1))
         before = jnp.where(index == 0, 0.0, pltpu.roll(cells, 1, 1))
         return following, before
 
-    def forces(x, half, slope_z):
-        cells = img[x + 2]
-        at = pl.ds(x + 1, 1)
-        frc[0, x + 1] = half * (img[x + 3] - img[x + 1])
-        up = jnp.where(rows == ny - 1, s_yhi[0, at, :], pltpu.roll(cells, ny - 1, 0))
-        down = jnp.where(rows == 0, s_ylo[1, at, :], pltpu.roll(cells, 1, 0))
-        frc[1, x + 1] = half * (up - down)
-        frc[2, x + 1] = half * slope_z
-
-    for x, half in ((-1, 0.5 * this(zxl[0], bxl[...])), (nx, 0.5 * this(zxh[0], bxh[...]))):
-        following, before = along_z(img[x + 2], lanes, nz)
-        forces(x, half, following - before)
-
-    def force_step(x, carry):
-        forces(x, 0.5 * this(adj0[x], adj1[x]), frc[2, x + 1])
-        return carry
-
-    lax.fori_loop(0, nx, force_step, 0)
-    lines = lax.broadcasted_iota(jnp.int32, (nx, nz), 1)
-    for cols, near, far, beside, half, dest, sign in (
-        (s_ylo, 1, 0, s_c0, s_al, s_fl, 1.0),
-        (s_yhi, 0, 1, s_c1, s_ah, s_fh, -1.0),
-    ):
-        weight = 0.5 * half[...]
-        dest[0] = weight * (cols[near, 2 : nx + 2, :] - cols[near, 0:nx, :])
-        dest[1] = (sign * weight) * (beside[...] - cols[far, 1 : nx + 1, :])
-        following, before = along_z(cols[near, 1 : nx + 1, :], lines, nz)
-        dest[2] = weight * (following - before)
-
-    def smooth_step(x, carry):
+    @pl.when(chunk == 0)
+    def _():
+        for h in range(2):
+            img[h] = xlo[2 * k + h].astype(F32)
+            img[nx + 2 + h] = xhi[2 * k + h].astype(F32)
+
+        def fill(x, cells):
+            packed[x] = cells
+            cells = cells.astype(F32)
+            img[x + 2] = cells
+            s_c0[pl.ds(x, 1), :] = cells[0:1]
+            s_c1[pl.ds(x, 1), :] = cells[ny - 1 : ny]
+
+        each_plane(groups, (own, la, ra, lb, rb), 0, fill)
+        every = packed[...].reshape(nx * ny, nz)
+        frc[2, 1 : nx + 1] = jnp.dot(every, band[...], preferred_element_type=F32).reshape(nx, ny, nz)
+        for h in range(2):
+            s_ylo[h] = ylo[2 * k + h].astype(F32)
+            s_yhi[h] = yhi[2 * k + h].astype(F32)
+        s_al[...] = this(ylo[4, 0:nx], byl[...])
+        s_ah[...] = this(yhi[4, 0:nx], byh[...])
+
+        def forces(x, half, slope_z):
+            cells = img[x + 2]
+            at = pl.ds(x + 1, 1)
+            frc[0, x + 1] = half * (img[x + 3] - img[x + 1])
+            up = jnp.where(rows == ny - 1, s_yhi[0, at, :], pltpu.roll(cells, ny - 1, 0))
+            down = jnp.where(rows == 0, s_ylo[1, at, :], pltpu.roll(cells, 1, 0))
+            frc[1, x + 1] = half * (up - down)
+            frc[2, x + 1] = half * slope_z
+
+        for x, half in ((-1, 0.5 * this(xlo[4], bxl[...])), (nx, 0.5 * this(xhi[4], bxh[...]))):
+            following, before = along_z(img[x + 2], lanes, nz)
+            forces(x, half, following - before)
+
+        def force_step(x, carry):
+            forces(x, 0.5 * this(adj0[x], adj1[x]), frc[2, x + 1])
+            return carry
+
+        lax.fori_loop(0, nx, force_step, 0, unroll=8)
+        lines = lax.broadcasted_iota(jnp.int32, (nx, nz), 1)
+        for cols, near, far, beside, half, dest, sign in (
+            (s_ylo, 1, 0, s_c0, s_al, s_fl, 1.0),
+            (s_yhi, 0, 1, s_c1, s_ah, s_fh, -1.0),
+        ):
+            weight = 0.5 * half[...]
+            dest[0] = weight * (cols[near, 2 : nx + 2, :] - cols[near, 0:nx, :])
+            dest[1] = (sign * weight) * (beside[...] - cols[far, 1 : nx + 1, :])
+            following, before = along_z(cols[near, 1 : nx + 1, :], lines, nz)
+            dest[2] = weight * (following - before)
+
+    def smooth_step(i, carry):
+        x = chunk * deep + i
         at = pl.ds(x, 1)
         for c in range(3):
             f = frc[c, x + 1]
@@ -437,18 +450,19 @@
             down = jnp.where(rows == 0, s_fl[c, at, :], pltpu.roll(f, 1, 0))
             following, before = along_z(f, lanes, nz)
             beside = (frc[c, x] + frc[c, x + 2]) + (up + down) + (following + before)
-            out[0, c, x] = vel[0, c, x].astype(F32) + (0.25 * f + 0.125 * beside)
+            out[0, c, i] = vel[0, c, i].astype(F32) + (0.25 * f + 0.125 * beside)
         return carry
 
-    lax.fori_loop(0, nx, smooth_step, 0)
-
-
-def force(groups, images, band, x_lo, x_hi, face_lo, face_hi, y_lo, y_hi, adj_zero, adj_one, halo_one, velocity):
+    lax.fori_loop(0, deep, smooth_step, 0, unroll=8)
+
+
+def force(groups, images, band, x_lo, x_hi, y_lo, y_hi, adj_zero, adj_one, halo_one, velocity):
     nx, ny, nz = adj_zero.shape
-    block = pl.BlockSpec((1, 3, nx, ny, nz), lambda k: (k, 0, 0, 0, 0))
-    middle = [band, x_lo, x_hi, face_lo, face_hi, y_lo, y_hi, adj_zero, adj_one, *halo_one]
+    deep = nx // 2
+    block = pl.BlockSpec((1, 3, deep, ny, nz), lambda k, i: (k, 0, i, 0, 0))
+    middle = [band, x_lo, x_hi, y_lo, y_hi, adj_zero, adj_one, *halo_one]
     counts = [nx] + [sum(b - a for a, b in planes) for planes in groups for _ in range(2)]
-    in_specs = [pl.BlockSpec((count, ny, nz), lambda k: (k, 0, 0)) for count in counts]
+    in_specs = [pl.BlockSpec((count, ny, nz), lambda k, i: (k, 0, 0)) for count in counts]
     in_specs += [whole(a.shape) for a in middle] + [block]
     scratch = [
         pltpu.VMEM((nx + 4, ny, nz), F32),
@@ -470,7 +484,7 @@
         "force",
         in_specs,
         block,
-        2,
+        (2, 2),
     )(*images, *middle, velocity)
 
 
@@ -496,10 +510,6 @@
 
     t_lo = forward(template, "gx")
     t_hi = backward(template, "gx")
-    low, high = column_messages(mismatch, velocity)
-    halo_xl = forward(high, "gx")
-    halo_xh = backward(low, "gx")
-
     ids = src_ids.reshape(slots)
     first_block = ids // (count_second * depth_blocks)
     second_block = ids // depth_blocks % count_second
@@ -508,13 +518,22 @@
     code = (side * (3 * depth_blocks) + start).astype(BF16).reshape(1, slots)
     left_code = forward(code, "gy")
     right_code = backward(code, "gy")
+    left_code, right_code, late_mismatch, late_velocity = lax.optimization_barrier(
+        (left_code, right_code, mismatch, velocity)
+    )
+    low, high = column_messages(
+        pltpu.with_memory_space_constraint(late_mismatch, pltpu.HBM),
+        pltpu.with_memory_space_constraint(late_velocity, pltpu.HBM),
+    )
+    halo_xl = forward(high, "gx")
+    halo_xh = backward(low, "gx")
     lines = call(
         rows_kernel,
         [struct((8 * ny, nz), F32)] * 2,
         [],
         "rows",
         [whole(a.shape) for a in (mismatch, velocity)],
-    )(mismatch, velocity)
+    )(late_mismatch, late_velocity)
 
     send_choice, own_choice = choices(left_code, right_code, code, edge, nz)
     z = jnp.arange(nz)
@@ -540,15 +559,13 @@
     adj_one, *halo_one = upwind_one(inside, late_mismatch, velocity, halo)
     adj_zero, low_x, high_x, low_y, high_y = upwind_zero(adj_one, velocity, halo_one, halo)
 
-    ins = (own, from_left_a, from_right_a)
+    ins = (own, from_left_a, from_right_a, low_x, high_x)
     low, high = call(
         functools.partial(outer_kernel, nx, 2 * margin),
-        [struct((4, ny, nz), BF16)] * 2, [], "outer", [whole(a.shape) for a in ins]
+        [struct((5, ny, nz), BF16)] * 2, [], "outer", [whole(a.shape) for a in ins]
     )(*ins)
     x_lo = forward(high, "gx")
     x_hi = backward(low, "gx")
-    face_lo = forward(high_x, "gx")
-    face_hi = backward(low_x, "gx")
 
     images = (own, from_left_a, from_right_a, from_left_b, from_right_b)
     ins = (*images, x_lo, x_hi, low_y, high_y)
@@ -562,7 +579,7 @@
     y_lo = forward(final, "gy")
     y_hi = backward(first, "gy")
     return force(
-        groups, images, band, x_lo, x_hi, face_lo, face_hi, y_lo, y_hi, adj_zero, adj_one, halo_one, velocity
+        groups, images, band, x_lo, x_hi, y_lo, y_hi, adj_zero, adj_one, halo_one, velocity
     )
 
 

time: 149 us -> 145 us (0.973)
  the two profiles are of different devices: /device:TPU:26 before, /device:TPU:121 now
where the time goes in v6:
time: 145 us; the launch traced here: 144 us
  starting transfers between devices  54.8 us (38%)
  waiting for transfers between devices  48.7 us (34%)
  Pallas kernels  35.8 us (25%)
  local copies, waits for them, and re-layouts  2.64 us (2%)
  other arithmetic  1.51 us (1%)
    ppermute x7, waiting for transfers between devices, backward(): return lax.ppermute(value, axis, [(i + 1, i) for i in range(ends)])  44.4 us
    ppermute x7, starting transfers between devices, forward(): return lax.ppermute(value, axis, [(i, i + 1) for i in range(ends)])  39.3 us
    ppermute x7, starting transfers between devices, backward(): return lax.ppermute(value, axis, [(i + 1, i) for i in range(ends)])  15.6 us
    pallas_call x1, Pallas kernels, force(): call(functools.partial(force_kernel, groups), struct((2, 3, nx, ny, nz),...  9.6 us
    pallas_call x3, Pallas kernels, pick(): call(functools.partial(pick_kernel, planes), outs, [], name, in_specs)(*ins)  8.43 us
    pallas_call x1, Pallas kernels, upwind_one(): call(upwind_one_kernel, outs, scratch, 'upwind_one', in_specs)  6.98 us
    pallas_call x1, Pallas kernels, upwind_zero(): call(upwind_zero_kernel, outs, scratch, 'upwind_zero', in_specs)  6.64 us
    ppermute x7, waiting for transfers between devices, forward(): return lax.ppermute(value, axis, [(i, i + 1) for i in range(ends)])  4.31 us
  transfers between devices with their start and end apart: 14, of which 6 were waited for; matrix products, arithmetic and copies ran while one was open for 1% of the time, Pallas kernels for 15%

profile of v6, /device:TPU:121, one launch (start us, length us, event | category | flops | bytes accessed | tf_op | source)
XLA Modules:
  0.0 143.8 jit_solution(8117596779998754010)
XLA Ops:
  0.0 2.8 %collective-permute-start.1 = (bf16[32,32,256]{2,1,0:T(8,128)(2,1)}, bf16[32,32,256]{2,1,0:T(8,128)(2,1)}, u32[]{:S(2)}, u32[]{:S(2)}) collective-permute-start(bf16[32,32,256]{2,1,0:T(8,128)(2,1)} %t_own.3), channel_id=1, source_target_pairs={{16,0},{32,16},{48,32},{64,48},{80,64},{96,80},{112,96},{128,112},... | collective-permute-start | bytes 1572872 | tf_op jit(solution)/shard_map/ppermute | solution.py:498
  2.8 6.9 %collective-permute-start = (bf16[32,32,256]{2,1,0:T(8,128)(2,1)}, bf16[32,32,256]{2,1,0:T(8,128)(2,1)}, u32[]{:S(2)}, u32[]{:S(2)}) collective-permute-start(bf16[32,32,256]{2,1,0:T(8,128)(2,1)} %t_own.3), channel_id=1, source_target_pairs={{0,16},{16,32},{32,48},{48,64},{64,80},{80,96},{96,112},{112,128},... | collective-permute-start | bytes 1572872 | tf_op jit(solution)/shard_map/ppermute | solution.py:493
  11.7 2.0 %collective-permute-start.3 = (bf16[1,16]{1,0:T(2,128)(2,1)S(1)}, bf16[1,16]{1,0:T(2,128)(2,1)S(1)}, u32[]{:S(2)}, u32[]{:S(2)}) collective-permute-start(bf16[1,16]{1,0:T(2,128)(2,1)S(1)} %fusion.9.own), channel_id=1, source_target_pairs={{1,0},{2,1},{3,2},{4,3},{5,4},{6,5},{7,6},{8,7},{9,8},{10,9},{11,1... | collective-permute-start | bytes 104 | tf_op jit(solution)/shard_map/ppermute | solution.py:498
  13.8 6.1 %collective-permute-start.2 = (bf16[1,16]{1,0:T(2,128)(2,1)S(1)}, bf16[1,16]{1,0:T(2,128)(2,1)S(1)}, u32[]{:S(2)}, u32[]{:S(2)}) collective-permute-start(bf16[1,16]{1,0:T(2,128)(2,1)S(1)} %fusion.9.own), channel_id=1, source_target_pairs={{0,1},{1,2},{2,3},{3,4},{4,5},{5,6},{6,7},{7,8},{8,9},{9,10},{10,1... | collective-permute-start | bytes 104 | tf_op jit(solution)/shard_map/ppermute | solution.py:493
  19.8 7.3 %collective-permute-done.3.right = bf16[1,16]{1,0:T(2,128)(2,1)S(1)} collective-permute-done((bf16[1,16]{1,0:T(2,128)(2,1)S(1)}, bf16[1,16]{1,0:T(2,128)(2,1)S(1)}, u32[]{:S(2)}, u32[]{:S(2)}) %collective-permute-start.3) | collective-permute-done | bytes 64 | tf_op jit(solution)/shard_map/ppermute | solution.py:498
  27.2 4.3 %collective-permute-done.2.left = bf16[1,16]{1,0:T(2,128)(2,1)S(1)} collective-permute-done((bf16[1,16]{1,0:T(2,128)(2,1)S(1)}, bf16[1,16]{1,0:T(2,128)(2,1)S(1)}, u32[]{:S(2)}, u32[]{:S(2)}) %collective-permute-start.2) | collective-permute-done | bytes 64 | tf_op jit(solution)/shard_map/ppermute | solution.py:493
  32.6 2.1 %collective-permute-start.4 = (bf16[7,32,256]{2,1,0:T(8,128)(2,1)S(1)}, bf16[7,32,256]{2,1,0:T(8,128)(2,1)S(1)}, u32[]{:S(2)}, u32[]{:S(2)}) collective-permute-start(bf16[7,32,256]{2,1,0:T(8,128)(2,1)S(1)} %get-tuple-element.45), channel_id=1, source_target_pairs={{0,16},{16,32},{32,48},{48,64},{64,80},{80,96},{96,112},{112,128},... | collective-permute-start | bytes 344072 | tf_op jit(solution)/shard_map/ppermute | solution.py:493
  34.7 2.4 %collective-permute-start.5 = (bf16[7,32,256]{2,1,0:T(8,128)(2,1)S(1)}, bf16[7,32,256]{2,1,0:T(8,128)(2,1)S(1)}, u32[]{:S(2)}, u32[]{:S(2)}) collective-permute-start(bf16[7,32,256]{2,1,0:T(8,128)(2,1)S(1)} %get-tuple-element.46), channel_id=1, source_target_pairs={{16,0},{32,16},{48,32},{64,48},{80,64},{96,80},{112,96},{128,112},... | collective-permute-start | bytes 344072 | tf_op jit(solution)/shard_map/ppermute | solution.py:498
  39.8 6.3 %collective-permute-done.5.rest_3_.hxh = bf16[7,32,256]{2,1,0:T(8,128)(2,1)S(1)} collective-permute-done((bf16[7,32,256]{2,1,0:T(8,128)(2,1)S(1)}, bf16[7,32,256]{2,1,0:T(8,128)(2,1)S(1)}, u32[]{:S(2)}, u32[]{:S(2)}) %collective-permute-start.5) | collective-permute-done | bytes 114720 | tf_op jit(solution)/shard_map/ppermute | solution.py:498
  46.1 3.3 %pick_outer.1 = (bf16[40,32,256]{2,1,0:T(8,128)(2,1)}, bf16[40,32,256]{2,1,0:T(8,128)(2,1)}) custom-call(bf16[32,32,256]{2,1,0:T(8,128)(2,1)} %collective-permute-done.t_lo, bf16[32,32,256]{2,1,0:T(8,128)(2,1)S(1)} %copy-done.3, bf16[32,32,256]{2,1,0:T(8,128)(2,1)} %collective-permute-done.1.t_hi, bf16[2,768,512]{2,1,0:T(8,128)(2,1)S(1)} %get-tuple-element.40.q_ref, ...), custom_call_target="tpu_custom_call" | custom-call | tf_op jit(solution)/shard_map/pick_outer/pallas_call | solution.py:322
  49.4 4.4 %collective-permute-start.6 = (bf16[40,32,256]{2,1,0:T(8,128)(2,1)}, bf16[40,32,256]{2,1,0:T(8,128)(2,1)S(1)}, u32[]{:S(2)}, u32[]{:S(2)}) collective-permute-start(bf16[40,32,256]{2,1,0:T(8,128)(2,1)} %get-tuple-element.54), channel_id=1, source_target_pairs={{0,1},{1,2},{2,3},{3,4},{4,5},{5,6},{6,7},{7,8},{8,9},{9,10},{10,1... | collective-permute-start | bytes 1966088 | tf_op jit(solution)/shard_map/ppermute | solution.py:493
  53.8 2.1 %collective-permute-start.7 = (bf16[40,32,256]{2,1,0:T(8,128)(2,1)}, bf16[40,32,256]{2,1,0:T(8,128)(2,1)S(1)}, u32[]{:S(2)}, u32[]{:S(2)}) collective-permute-start(bf16[40,32,256]{2,1,0:T(8,128)(2,1)} %get-tuple-element.47), channel_id=1, source_target_pairs={{1,0},{2,1},{3,2},{4,3},{5,4},{6,5},{7,6},{8,7},{9,8},{10,9},{11,1... | collective-permute-start | bytes 1966088 | tf_op jit(solution)/shard_map/ppermute | solution.py:498
  55.9 3.0 %pick_inner.1 = (bf16[32,32,256]{2,1,0:T(8,128)(2,1)}, bf16[32,32,256]{2,1,0:T(8,128)(2,1)}) custom-call(bf16[32,32,256]{2,1,0:T(8,128)(2,1)} %collective-permute-done.t_lo, bf16[32,32,256]{2,1,0:T(8,128)(2,1)S(1)} %copy-done.3, bf16[32,32,256]{2,1,0:T(8,128)(2,1)} %collective-permute-done.1.t_hi, bf16[2,768,512]{2,1,0:T(8,128)(2,1)S(1)} %get-tuple-element.40.q_ref), custom_call_target="tpu_custom_call" | custom-call | tf_op jit(solution)/shard_map/pick_inner/pallas_call | solution.py:322
  58.8 9.5 %collective-permute-start.8 = (bf16[32,32,256]{2,1,0:T(8,128)(2,1)}, bf16[32,32,256]{2,1,0:T(8,128)(2,1)S(1)}, u32[]{:S(2)}, u32[]{:S(2)}) collective-permute-start(bf16[32,32,256]{2,1,0:T(8,128)(2,1)} %get-tuple-element.55), channel_id=1, source_target_pairs={{0,1},{1,2},{2,3},{3,4},{4,5},{5,6},{6,7},{7,8},{8,9},{9,10},{10,1... | collective-permute-start | bytes 1572872 | tf_op jit(solution)/shard_map/ppermute | solution.py:493
  68.3 1.9 %collective-permute-start.9 = (bf16[32,32,256]{2,1,0:T(8,128)(2,1)}, bf16[32,32,256]{2,1,0:T(8,128)(2,1)}, u32[]{:S(2)}, u32[]{:S(2)}) collective-permute-start(bf16[32,32,256]{2,1,0:T(8,128)(2,1)} %get-tuple-element.52), channel_id=1, source_target_pairs={{1,0},{2,1},{3,2},{4,3},{5,4},{6,5},{7,6},{8,7},{9,8},{10,9},{11,1... | collective-permute-start | bytes 1572872 | tf_op jit(solution)/shard_map/ppermute | solution.py:498
  71.5 2.2 %pick_own.1.own = bf16[64,32,256]{2,1,0:T(8,128)(2,1)S(1)} custom-call(bf16[32,32,256]{2,1,0:T(8,128)(2,1)} %collective-permute-done.t_lo, bf16[32,32,256]{2,1,0:T(8,128)(2,1)S(1)} %copy-done.4, bf16[32,32,256]{2,1,0:T(8,128)(2,1)} %collective-permute-done.1.t_hi, bf16[1,768,512]{2,1,0:T(8,128)(2,1)S(1)} %copy-done.8), custom_call_target="tpu_custom_call" | custom-call | tf_op jit(solution)/shard_map/pick_own/pallas_call | solution.py:322
  73.7 17.4 %collective-permute-done.7.hyh.ra = bf16[40,32,256]{2,1,0:T(8,128)(2,1)S(1)} collective-permute-done((bf16[40,32,256]{2,1,0:T(8,128)(2,1)}, bf16[40,32,256]{2,1,0:T(8,128)(2,1)S(1)}, u32[]{:S(2)}, u32[]{:S(2)}) %collective-permute-start.7) | collective-permute-done | bytes 655392 | tf_op jit(solution)/shard_map/ppermute | solution.py:498
  91.1 7.0 %upwind_one.1 = (f32[32,32,256]{2,1,0:T(8,128)S(1)}, f32[32,256]{1,0:T(8,128)S(1)}, f32[32,256]{1,0:T(8,128)S(1)}, f32[32,256]{1,0:T(8,128)S(1)}, f32[32,256]{1,0:T(8,128)S(1)}) custom-call(f32[4]{0:T(128)S(1)} %add_convert_fusion.inside, f32[32,32,256]{2,1,0:T(8,128)S(1)} %copy-done.2, bf16[2,3,32,32,256]{4,3,2,1,0:T(8,128)(2,1)} %vel.1, ...), custom_call_target="tpu_custom_call" | custom-call | tf_op jit(solution)/shard_map/upwind_one/pallas_call | solution.py:247
  98.1 6.6 %upwind_zero.1 = (f32[32,32,256]{2,1,0:T(8,128)S(1)}, bf16[1,32,256]{2,1,0:T(8,128)(2,1)S(1)}, bf16[1,32,256]{2,1,0:T(8,128)(2,1)S(1)}, bf16[1,32,256]{2,1,0:T(8,128)(2,1)S(1)}, bf16[1,32,256]{2,1,0:T(8,128)(2,1)S(1)}) custom-call(f32[32,32,256]{2,1,0:T(8,128)S(1)} %get-tuple-element.57.p_ref.adj1, bf16[2,3,32,32,256]{4,3,2,1,0:T(8,128)(2,1)} %vel.1, ...), custom_call_target="tpu_custom_call" | custom-call | tf_op jit(solution)/shard_map/upwind_zero/pallas_call | solution.py:256
  106.7 2.4 %collective-permute-start.11 = (bf16[5,32,256]{2,1,0:T(8,128)(2,1)S(1)}, bf16[5,32,256]{2,1,0:T(8,128)(2,1)S(1)}, u32[]{:S(2)}, u32[]{:S(2)}) collective-permute-start(bf16[5,32,256]{2,1,0:T(8,128)(2,1)S(1)} %get-tuple-element.65), channel_id=1, source_target_pairs={{16,0},{32,16},{48,32},{64,48},{80,64},{96,80},{112,96},{128,112},... | collective-permute-start | bytes 245768 | tf_op jit(solution)/shard_map/ppermute | solution.py:498
  109.1 7.2 %collective-permute-done.11.xhi = bf16[5,32,256]{2,1,0:T(8,128)(2,1)S(1)} collective-permute-done((bf16[5,32,256]{2,1,0:T(8,128)(2,1)S(1)}, bf16[5,32,256]{2,1,0:T(8,128)(2,1)S(1)}, u32[]{:S(2)}, u32[]{:S(2)}) %collective-permute-start.11) | collective-permute-done | bytes 81952 | tf_op jit(solution)/shard_map/ppermute | solution.py:498
  117.6 8.5 %collective-permute-start.12 = (bf16[5,34,256]{2,1,0:T(8,128)(2,1)S(1)}, bf16[5,34,256]{2,1,0:T(8,128)(2,1)S(1)}, u32[]{:S(2)}, u32[]{:S(2)}) collective-permute-start(bf16[5,34,256]{2,1,0:T(8,128)(2,1)S(1)} %get-tuple-element.68), channel_id=1, source_target_pairs={{0,1},{1,2},{2,3},{3,4},{4,5},{5,6},{6,7},{7,8},{8,9},{9,10},{10,1... | collective-permute-start | bytes 261128 | tf_op jit(solution)/shard_map/ppermute | solution.py:493
  128.1 6.1 %collective-permute-done.13.yhi = bf16[5,34,256]{2,1,0:T(8,128)(2,1)S(1)} collective-permute-done((bf16[5,34,256]{2,1,0:T(8,128)(2,1)S(1)}, bf16[5,34,256]{2,1,0:T(8,128)(2,1)S(1)}, u32[]{:S(2)}, u32[]{:S(2)}) %collective-permute-start.13) | collective-permute-done | bytes 87072 | tf_op jit(solution)/shard_map/ppermute | solution.py:498
  134.2 9.6 %force.1 = f32[2,3,32,32,256]{4,3,2,1,0:T(8,128)} custom-call(bf16[64,32,256]{2,1,0:T(8,128)(2,1)S(1)} %pick_own.1.own, bf16[40,32,256]{2,1,0:T(8,128)(2,1)S(1)} %collective-permute-done.6.hyl.la, bf16[40,32,256]{2,1,0:T(8,128)(2,1)S(1)} %collective-permute-done.7.hyh.ra, bf16[32,32,256]{2,1,0:T(8,128)(2,1)S(1)} %collective-permute-done.8.lb, ...), custom_call_target="tpu_custom_call" | custom-call | tf_op jit(solution)/shard_map/force/pallas_call | solution.py:480
  (40 shorter events, 12.2 us)
Async XLA Ops:
  0.0 37.1 %copy-start = (bf16[2,3,32,32,256]{4,3,2,1,0:T(8,128)(2,1)S(1)}, bf16[2,3,32,32,256]{4,3,2,1,0:T(8,128)(2,1)}, u32[]{:S(2)}) copy-start(bf16[2,3,32,32,256]{4,3,2,1,0:T(8,128)(2,1)} %vel.1) | copy-start | bytes 9437188
  0.0 46.1 %collective-permute-start.1 = (bf16[32,32,256]{2,1,0:T(8,128)(2,1)}, bf16[32,32,256]{2,1,0:T(8,128)(2,1)}, u32[]{:S(2)}, u32[]{:S(2)}) collective-permute-start(bf16[32,32,256]{2,1,0:T(8,128)(2,1)} %t_own.3), channel_id=1, source_target_pairs={{16,0},{32,16},{48,32},{64,48},{80,64},{96,80},{112,96},{128,112},... | collective-permute-start | bytes 1572872 | tf_op jit(solution)/shard_map/ppermute | solution.py:498
  2.8 43.2 %collective-permute-start = (bf16[32,32,256]{2,1,0:T(8,128)(2,1)}, bf16[32,32,256]{2,1,0:T(8,128)(2,1)}, u32[]{:S(2)}, u32[]{:S(2)}) collective-permute-start(bf16[32,32,256]{2,1,0:T(8,128)(2,1)} %t_own.3), channel_id=1, source_target_pairs={{0,16},{16,32},{32,48},{48,64},{64,80},{80,96},{96,112},{112,128},... | collective-permute-start | bytes 1572872 | tf_op jit(solution)/shard_map/ppermute | solution.py:493
  11.7 25.4 %copy-start.1 = (f32[32,32,256]{2,1,0:T(8,128)S(1)}, f32[32,32,256]{2,1,0:T(8,128)}, u32[]{:S(2)}) copy-start(f32[32,32,256]{2,1,0:T(8,128)} %p_ref.1) | copy-start | bytes 3145732
  11.7 15.4 %collective-permute-start.3 = (bf16[1,16]{1,0:T(2,128)(2,1)S(1)}, bf16[1,16]{1,0:T(2,128)(2,1)S(1)}, u32[]{:S(2)}, u32[]{:S(2)}) collective-permute-start(bf16[1,16]{1,0:T(2,128)(2,1)S(1)} %fusion.9.own), channel_id=1, source_target_pairs={{1,0},{2,1},{3,2},{4,3},{5,4},{6,5},{7,6},{8,7},{9,8},{10,9},{11,1... | collective-permute-start | bytes 104 | tf_op jit(solution)/shard_map/ppermute | solution.py:498
  13.8 17.7 %collective-permute-start.2 = (bf16[1,16]{1,0:T(2,128)(2,1)S(1)}, bf16[1,16]{1,0:T(2,128)(2,1)S(1)}, u32[]{:S(2)}, u32[]{:S(2)}) collective-permute-start(bf16[1,16]{1,0:T(2,128)(2,1)S(1)} %fusion.9.own), channel_id=1, source_target_pairs={{0,1},{1,2},{2,3},{3,4},{4,5},{5,6},{6,7},{7,8},{8,9},{9,10},{10,1... | collective-permute-start | bytes 104 | tf_op jit(solution)/shard_map/ppermute | solution.py:493
  32.6 13.5 %copy-start.3 = (bf16[32,32,256]{2,1,0:T(8,128)(2,1)S(1)}, bf16[32,32,256]{2,1,0:T(8,128)(2,1)}, u32[]{:S(2)}) copy-start(bf16[32,32,256]{2,1,0:T(8,128)(2,1)} %t_own.3) | copy-start | bytes 1572868
  32.6 7.1 %collective-permute-start.4 = (bf16[7,32,256]{2,1,0:T(8,128)(2,1)S(1)}, bf16[7,32,256]{2,1,0:T(8,128)(2,1)S(1)}, u32[]{:S(2)}, u32[]{:S(2)}) collective-permute-start(bf16[7,32,256]{2,1,0:T(8,128)(2,1)S(1)} %get-tuple-element.45), channel_id=1, source_target_pairs={{0,16},{16,32},{32,48},{48,64},{64,80},{80,96},{96,112},{112,128},... | collective-permute-start | bytes 344072 | tf_op jit(solution)/shard_map/ppermute | solution.py:493
  34.7 11.4 %collective-permute-start.5 = (bf16[7,32,256]{2,1,0:T(8,128)(2,1)S(1)}, bf16[7,32,256]{2,1,0:T(8,128)(2,1)S(1)}, u32[]{:S(2)}, u32[]{:S(2)}) collective-permute-start(bf16[7,32,256]{2,1,0:T(8,128)(2,1)S(1)} %get-tuple-element.46), channel_id=1, source_target_pairs={{16,0},{32,16},{48,32},{64,48},{80,64},{96,80},{112,96},{128,112},... | collective-permute-start | bytes 344072 | tf_op jit(solution)/shard_map/ppermute | solution.py:498
  38.9 0.9 copy-start.7
  46.1 7.7 %copy-start.5 = (bf16[7,32,256]{2,1,0:T(8,128)(2,1)}, bf16[7,32,256]{2,1,0:T(8,128)(2,1)S(1)}, u32[]{:S(2)}) copy-start(bf16[7,32,256]{2,1,0:T(8,128)(2,1)S(1)} %collective-permute-done.5.rest_3_.hxh) | copy-start | bytes 344068
  46.1 24.2 %copy-start.4 = (bf16[32,32,256]{2,1,0:T(8,128)(2,1)S(1)}, bf16[32,32,256]{2,1,0:T(8,128)(2,1)}, u32[]{:S(2)}) copy-start(bf16[32,32,256]{2,1,0:T(8,128)(2,1)} %t_own.3) | copy-start | bytes 1572868
  49.4 24.3 %collective-permute-start.6 = (bf16[40,32,256]{2,1,0:T(8,128)(2,1)}, bf16[40,32,256]{2,1,0:T(8,128)(2,1)S(1)}, u32[]{:S(2)}, u32[]{:S(2)}) collective-permute-start(bf16[40,32,256]{2,1,0:T(8,128)(2,1)} %get-tuple-element.54), channel_id=1, source_target_pairs={{0,1},{1,2},{2,3},{3,4},{4,5},{5,6},{6,7},{7,8},{8,9},{9,10},{10,1... | collective-permute-start | bytes 1966088 | tf_op jit(solution)/shard_map/ppermute | solution.py:493
  53.8 37.3 %copy-start.2 = (f32[32,32,256]{2,1,0:T(8,128)S(1)}, f32[32,32,256]{2,1,0:T(8,128)}, u32[]{:S(2)}) copy-start(f32[32,32,256]{2,1,0:T(8,128)} %p_ref.1) | copy-start | bytes 3145732
  53.8 37.3 %collective-permute-start.7 = (bf16[40,32,256]{2,1,0:T(8,128)(2,1)}, bf16[40,32,256]{2,1,0:T(8,128)(2,1)S(1)}, u32[]{:S(2)}, u32[]{:S(2)}) collective-permute-start(bf16[40,32,256]{2,1,0:T(8,128)(2,1)} %get-tuple-element.47), channel_id=1, source_target_pairs={{1,0},{2,1},{3,2},{4,3},{5,4},{6,5},{7,6},{8,7},{9,8},{10,9},{11,1... | collective-permute-start | bytes 1966088 | tf_op jit(solution)/shard_map/ppermute | solution.py:498
  58.8 50.3 %collective-permute-start.8 = (bf16[32,32,256]{2,1,0:T(8,128)(2,1)}, bf16[32,32,256]{2,1,0:T(8,128)(2,1)S(1)}, u32[]{:S(2)}, u32[]{:S(2)}) collective-permute-start(bf16[32,32,256]{2,1,0:T(8,128)(2,1)} %get-tuple-element.55), channel_id=1, source_target_pairs={{0,1},{1,2},{2,3},{3,4},{4,5},{5,6},{6,7},{7,8},{8,9},{9,10},{10,1... | collective-permute-start | bytes 1572872 | tf_op jit(solution)/shard_map/ppermute | solution.py:493
  68.3 40.8 %collective-permute-start.9 = (bf16[32,32,256]{2,1,0:T(8,128)(2,1)}, bf16[32,32,256]{2,1,0:T(8,128)(2,1)}, u32[]{:S(2)}, u32[]{:S(2)}) collective-permute-start(bf16[32,32,256]{2,1,0:T(8,128)(2,1)} %get-tuple-element.52), channel_id=1, source_target_pairs={{1,0},{2,1},{3,2},{4,3},{5,4},{6,5},{7,6},{8,7},{9,8},{10,9},{11,1... | collective-permute-start | bytes 1572872 | tf_op jit(solution)/shard_map/ppermute | solution.py:498
  70.3 20.8 %copy-start.6 = (bf16[7,32,256]{2,1,0:T(8,128)(2,1)S(1)}, bf16[7,32,256]{2,1,0:T(8,128)(2,1)}, u32[]{:S(2)}) copy-start(bf16[7,32,256]{2,1,0:T(8,128)(2,1)} %copy-done.5) | copy-start | bytes 344068
  70.3 1.1 copy-start.8
  104.7 4.4 %collective-permute-start.10 = (bf16[5,32,256]{2,1,0:T(8,128)(2,1)S(1)}, bf16[5,32,256]{2,1,0:T(8,128)(2,1)S(1)}, u32[]{:S(2)}, u32[]{:S(2)}) collective-permute-start(bf16[5,32,256]{2,1,0:T(8,128)(2,1)S(1)} %get-tuple-element.64), channel_id=1, source_target_pairs={{0,16},{16,32},{32,48},{48,64},{64,80},{80,96},{96,112},{112,128},... | collective-permute-start | bytes 245768 | tf_op jit(solution)/shard_map/ppermute | solution.py:493
  106.7 9.7 %collective-permute-start.11 = (bf16[5,32,256]{2,1,0:T(8,128)(2,1)S(1)}, bf16[5,32,256]{2,1,0:T(8,128)(2,1)S(1)}, u32[]{:S(2)}, u32[]{:S(2)}) collective-permute-start(bf16[5,32,256]{2,1,0:T(8,128)(2,1)S(1)} %get-tuple-element.65), channel_id=1, source_target_pairs={{16,0},{32,16},{48,32},{64,48},{80,64},{96,80},{112,96},{128,112},... | collective-permute-start | bytes 245768 | tf_op jit(solution)/shard_map/ppermute | solution.py:498
  117.6 10.5 %collective-permute-start.12 = (bf16[5,34,256]{2,1,0:T(8,128)(2,1)S(1)}, bf16[5,34,256]{2,1,0:T(8,128)(2,1)S(1)}, u32[]{:S(2)}, u32[]{:S(2)}) collective-permute-start(bf16[5,34,256]{2,1,0:T(8,128)(2,1)S(1)} %get-tuple-element.68), channel_id=1, source_target_pairs={{0,1},{1,2},{2,3},{3,4},{4,5},{5,6},{6,7},{7,8},{8,9},{9,10},{10,1... | collective-permute-start | bytes 261128 | tf_op jit(solution)/shard_map/ppermute | solution.py:493
  126.1 8.1 %collective-permute-start.13 = (bf16[5,34,256]{2,1,0:T(8,128)(2,1)S(1)}, bf16[5,34,256]{2,1,0:T(8,128)(2,1)S(1)}, u32[]{:S(2)}, u32[]{:S(2)}) collective-permute-start(bf16[5,34,256]{2,1,0:T(8,128)(2,1)S(1)} %get-tuple-element.69), channel_id=1, source_target_pairs={{1,0},{2,1},{3,2},{4,3},{5,4},{6,5},{7,6},{8,7},{9,8},{10,9},{11,1... | collective-permute-start | bytes 261128 | tf_op jit(solution)/shard_map/ppermute | solution.py:498

commit v7 on v5

--- a/solution.py
+++ b/solution.py
@@ -163,7 +163,11 @@
         s_v1[at, :] = vy[ny - 1 : ny]
         return flux
 
-    flux = lax.fori_loop(0, nx - 1, lambda x, f: inner(x, f, p_ref[x + 1], speed(0, x + 1)), flux)
+    def inner_step(x, f):
+        return inner(x, f, p_ref[x + 1], speed(0, x + 1))
+
+    flux = lax.fori_loop(0, nx - 2, inner_step, flux, unroll=5)
+    flux = inner_step(nx - 2, flux)
     flux = inner(nx - 1, flux, p_high, vx_high)
     got, _ = plane(nx, flux, p_high, (vx_high, vy_high, vz_high), p_far, vx_far)
     oxh[...] = got * inside[1]
@@ -214,7 +218,11 @@
         return flux_above
 
     flux = face_flux(pxl[...], p_ref[0], hxl[NEAR_EARLY].astype(F32), speed(0, 0))
-    flux = lax.fori_loop(0, nx - 1, lambda x, f: plane(x, f, p_ref[x + 1], speed(0, x + 1)), flux)
+    def plane_step(x, f):
+        return plane(x, f, p_ref[x + 1], speed(0, x + 1))
+
+    flux = lax.fori_loop(0, nx - 2, plane_step, flux, unroll=5)
+    flux = plane_step(nx - 2, flux)
     plane(nx - 1, flux, pxh[...], hxh[NEAR_EARLY].astype(F32))
     fxl[0] = out[0].astype(BF16)
     fxh[0] = out[nx - 1].astype(BF16)

time: 137 us -> 137 us (level)
  Pallas kernels: 36.8 us -> 30.8 us
  waiting for transfers between devices: 27.9 us -> 33.8 us
    ppermute x7, waiting for transfers between devices: 10.3 us -> 17.3 us  [backward(): return lax.ppermute(value, axis, [(i + 1, i) for i in range(ends)])]
    pallas_call x1, Pallas kernels: 6.1 us -> 3.03 us  [upwind_one(): call(upwind_one_kernel, outs, scratch, 'upwind_one', in_specs)]
    pallas_call x1, Pallas kernels: 5.15 us -> 2.21 us  [upwind_zero(): call(upwind_zero_kernel, outs, scratch, 'upwind_zero', in_specs)]
  transfers between devices with their start and end apart: 14 -> 14, of which waited for: 7 -> 8; matrix products, arithmetic and copies ran while one was open for 1% -> 1% of each run, Pallas kernels for 14% -> 10%
where the time goes in v7:
time: 137 us; the launch traced here: 136 us
  starting transfers between devices  67.6 us (49%)
  waiting for transfers between devices  33.8 us (25%)
  Pallas kernels  30.8 us (22%)
  local copies, waits for them, and re-layouts  3.11 us (2%)
    ppermute x7, starting transfers between devices, backward(): return lax.ppermute(value, axis, [(i + 1, i) for i in range(ends)])  42 us
    ppermute x7, starting transfers between devices, forward(): return lax.ppermute(value, axis, [(i, i + 1) for i in range(ends)])  25.5 us
    ppermute x7, waiting for transfers between devices, backward(): return lax.ppermute(value, axis, [(i + 1, i) for i in range(ends)])  17.3 us
    ppermute x7, waiting for transfers between devices, forward(): return lax.ppermute(value, axis, [(i, i + 1) for i in range(ends)])  16.5 us
    pallas_call x1, Pallas kernels, force(): call(functools.partial(force_kernel, groups), struct((2, 3, nx, ny, nz),...  10.1 us
    pallas_call x3, Pallas kernels, pick(): call(functools.partial(pick_kernel, planes), outs, [], name, in_specs)(*ins)  8.88 us
    pallas_call x1, Pallas kernels, upwind_one(): call(upwind_one_kernel, outs, scratch, 'upwind_one', in_specs)  3.03 us
    unnamed x17, local copies, waits for them, and re-layouts  3.01 us
  transfers between devices with their start and end apart: 14, of which 8 were waited for; matrix products, arithmetic and copies ran while one was open for 1% of the time, Pallas kernels for 10%

profile of v7, /device:TPU:26, one launch (start us, length us, event | category | flops | bytes accessed | tf_op | source)
XLA Modules:
  0.0 136.3 jit_solution(330416417309539414)
XLA Ops:
  0.0 1.9 %columns.1 = (bf16[7,32,256]{2,1,0:T(8,128)(2,1)S(1)}, bf16[7,32,256]{2,1,0:T(8,128)(2,1)}) custom-call(f32[32,32,256]{2,1,0:T(8,128)} %p_ref.2, bf16[2,3,32,32,256]{4,3,2,1,0:T(8,128)(2,1)} %vel.1), custom_call_target="tpu_custom_call" | custom-call | tf_op jit(solution)/shard_map/columns/pallas_call | solution.py:92
  1.9 8.7 %collective-permute-start.1 = (bf16[32,32,256]{2,1,0:T(8,128)(2,1)}, bf16[32,32,256]{2,1,0:T(8,128)(2,1)}, u32[]{:S(2)}, u32[]{:S(2)}) collective-permute-start(bf16[32,32,256]{2,1,0:T(8,128)(2,1)} %t_own.3), channel_id=1, source_target_pairs={{16,0},{32,16},{48,32},{64,48},{80,64},{96,80},{112,96},{128,112},... | collective-permute-start | bytes 1572872 | tf_op jit(solution)/shard_map/ppermute | solution.py:483
  10.7 1.9 %collective-permute-start = (bf16[32,32,256]{2,1,0:T(8,128)(2,1)}, bf16[32,32,256]{2,1,0:T(8,128)(2,1)}, u32[]{:S(2)}, u32[]{:S(2)}) collective-permute-start(bf16[32,32,256]{2,1,0:T(8,128)(2,1)} %t_own.3), channel_id=1, source_target_pairs={{0,16},{16,32},{32,48},{48,64},{64,80},{80,96},{96,112},{112,128},... | collective-permute-start | bytes 1572872 | tf_op jit(solution)/shard_map/ppermute | solution.py:478
  12.6 8.4 %collective-permute-start.3 = (bf16[7,32,256]{2,1,0:T(8,128)(2,1)S(1)}, bf16[7,32,256]{2,1,0:T(8,128)(2,1)S(1)}, u32[]{:S(2)}, u32[]{:S(2)}) collective-permute-start(bf16[7,32,256]{2,1,0:T(8,128)(2,1)S(1)} %get-tuple-element.35), channel_id=1, source_target_pairs={{16,0},{32,16},{48,32},{64,48},{80,64},{96,80},{112,96},{128,112},... | collective-permute-start | bytes 344072 | tf_op jit(solution)/shard_map/ppermute | solution.py:483
  24.2 10.6 %collective-permute-done.2.hxl = bf16[7,32,256]{2,1,0:T(8,128)(2,1)S(1)} collective-permute-done((bf16[7,32,256]{2,1,0:T(8,128)(2,1)}, bf16[7,32,256]{2,1,0:T(8,128)(2,1)S(1)}, u32[]{:S(2)}, u32[]{:S(2)}) %collective-permute-start.2) | collective-permute-done | bytes 114720 | tf_op jit(solution)/shard_map/ppermute | solution.py:478
  36.7 8.7 %collective-permute-start.4 = (bf16[7,34,256]{2,1,0:T(8,128)(2,1)S(1)}, bf16[7,34,256]{2,1,0:T(8,128)(2,1)S(1)}, u32[]{:S(2)}, u32[]{:S(2)}) collective-permute-start(bf16[7,34,256]{2,1,0:T(8,128)(2,1)S(1)} %get-tuple-element.38), channel_id=1, source_target_pairs={{0,1},{1,2},{2,3},{3,4},{4,5},{5,6},{6,7},{7,8},{8,9},{9,10},{10,1... | collective-permute-start | bytes 365576 | tf_op jit(solution)/shard_map/ppermute | solution.py:478
  47.3 2.2 %collective-permute-done.4.left.hyl = bf16[7,34,256]{2,1,0:T(8,128)(2,1)S(1)} collective-permute-done((bf16[7,34,256]{2,1,0:T(8,128)(2,1)S(1)}, bf16[7,34,256]{2,1,0:T(8,128)(2,1)S(1)}, u32[]{:S(2)}, u32[]{:S(2)}) %collective-permute-start.4) | collective-permute-done | bytes 121888 | tf_op jit(solution)/shard_map/ppermute | solution.py:478
  49.5 2.9 %collective-permute-done.5.right.hyh = bf16[7,34,256]{2,1,0:T(8,128)(2,1)S(1)} collective-permute-done((bf16[7,34,256]{2,1,0:T(8,128)(2,1)S(1)}, bf16[7,34,256]{2,1,0:T(8,128)(2,1)S(1)}, u32[]{:S(2)}, u32[]{:S(2)}) %collective-permute-start.5) | collective-permute-done | bytes 121888 | tf_op jit(solution)/shard_map/ppermute | solution.py:483
  53.5 3.4 %pick_outer.1 = (bf16[32,32,256]{2,1,0:T(8,128)(2,1)}, bf16[32,32,256]{2,1,0:T(8,128)(2,1)}) custom-call(bf16[32,32,256]{2,1,0:T(8,128)(2,1)} %collective-permute-done.t_lo, bf16[32,32,256]{2,1,0:T(8,128)(2,1)} %t_own.3, bf16[32,32,256]{2,1,0:T(8,128)(2,1)} %collective-permute-done.1.t_hi, bf16[2,768,512]{2,1,0:T(8,128)(2,1)S(1)} %get-tuple-element.40.q_ref), custom_call_target="tpu_custom_call" | custom-call | tf_op jit(solution)/shard_map/pick_outer/pallas_call | solution.py:307
  56.9 2.8 %collective-permute-start.6 = (bf16[32,32,256]{2,1,0:T(8,128)(2,1)}, bf16[32,32,256]{2,1,0:T(8,128)(2,1)}, u32[]{:S(2)}, u32[]{:S(2)}) collective-permute-start(bf16[32,32,256]{2,1,0:T(8,128)(2,1)} %get-tuple-element.48), channel_id=1, source_target_pairs={{0,1},{1,2},{2,3},{3,4},{4,5},{5,6},{6,7},{7,8},{8,9},{9,10},{10,1... | collective-permute-start | bytes 1572872 | tf_op jit(solution)/shard_map/ppermute | solution.py:478
  59.7 5.7 %collective-permute-start.7 = (bf16[32,32,256]{2,1,0:T(8,128)(2,1)}, bf16[32,32,256]{2,1,0:T(8,128)(2,1)}, u32[]{:S(2)}, u32[]{:S(2)}) collective-permute-start(bf16[32,32,256]{2,1,0:T(8,128)(2,1)} %get-tuple-element.41), channel_id=1, source_target_pairs={{1,0},{2,1},{3,2},{4,3},{5,4},{6,5},{7,6},{8,7},{9,8},{10,9},{11,1... | collective-permute-start | bytes 1572872 | tf_op jit(solution)/shard_map/ppermute | solution.py:483
  65.4 3.1 %pick_inner.1 = (bf16[32,32,256]{2,1,0:T(8,128)(2,1)}, bf16[32,32,256]{2,1,0:T(8,128)(2,1)}) custom-call(bf16[32,32,256]{2,1,0:T(8,128)(2,1)} %collective-permute-done.t_lo, bf16[32,32,256]{2,1,0:T(8,128)(2,1)} %t_own.3, bf16[32,32,256]{2,1,0:T(8,128)(2,1)} %collective-permute-done.1.t_hi, bf16[2,768,512]{2,1,0:T(8,128)(2,1)S(1)} %get-tuple-element.40.q_ref), custom_call_target="tpu_custom_call" | custom-call | tf_op jit(solution)/shard_map/pick_inner/pallas_call | solution.py:307
  70.5 6.6 %collective-permute-start.9 = (bf16[32,32,256]{2,1,0:T(8,128)(2,1)}, bf16[32,32,256]{2,1,0:T(8,128)(2,1)}, u32[]{:S(2)}, u32[]{:S(2)}) collective-permute-start(bf16[32,32,256]{2,1,0:T(8,128)(2,1)} %get-tuple-element.46), channel_id=1, source_target_pairs={{1,0},{2,1},{3,2},{4,3},{5,4},{6,5},{7,6},{8,7},{9,8},{10,9},{11,1... | collective-permute-start | bytes 1572872 | tf_op jit(solution)/shard_map/ppermute | solution.py:483
  78.5 2.3 %pick_own.1.own = bf16[64,32,256]{2,1,0:T(8,128)(2,1)S(1)} custom-call(bf16[32,32,256]{2,1,0:T(8,128)(2,1)} %collective-permute-done.t_lo, bf16[32,32,256]{2,1,0:T(8,128)(2,1)} %t_own.3, bf16[32,32,256]{2,1,0:T(8,128)(2,1)} %collective-permute-done.1.t_hi, bf16[1,768,512]{2,1,0:T(8,128)(2,1)S(1)} %copy-done.6), custom_call_target="tpu_custom_call" | custom-call | tf_op jit(solution)/shard_map/pick_own/pallas_call | solution.py:307
  80.8 3.0 %upwind_one.1 = (f32[32,32,256]{2,1,0:T(8,128)S(1)}, f32[32,256]{1,0:T(8,128)S(1)}, f32[32,256]{1,0:T(8,128)S(1)}, f32[32,256]{1,0:T(8,128)S(1)}, f32[32,256]{1,0:T(8,128)S(1)}) custom-call(f32[4]{0:T(128)S(1)} %add_convert_fusion.inside, f32[32,32,256]{2,1,0:T(8,128)S(1)} %copy-done.2, bf16[2,3,32,32,256]{4,3,2,1,0:T(8,128)(2,1)S(1)} %copy-done, ...), custom_call_target="tpu_custom_call" | custom-call | tf_op jit(solution)/shard_map/upwind_one/pallas_call | solution.py:245
  83.9 2.2 %upwind_zero.1 = (f32[32,32,256]{2,1,0:T(8,128)S(1)}, bf16[1,32,256]{2,1,0:T(8,128)(2,1)S(1)}, bf16[1,32,256]{2,1,0:T(8,128)(2,1)S(1)}, bf16[1,32,256]{2,1,0:T(8,128)(2,1)S(1)}, bf16[1,32,256]{2,1,0:T(8,128)(2,1)S(1)}) custom-call(f32[32,32,256]{2,1,0:T(8,128)S(1)} %get-tuple-element.51.p_ref.adj1, bf16[2,3,32,32,256]{4,3,2,1,0:T(8,128)(2,1)S(1)} %copy-done, ...), custom_call_target="tpu_custom_call" | custom-call | tf_op jit(solution)/shard_map/upwind_zero/pallas_call | solution.py:254
  86.1 2.5 %collective-permute-done.7.ra = bf16[32,32,256]{2,1,0:T(8,128)(2,1)} collective-permute-done((bf16[32,32,256]{2,1,0:T(8,128)(2,1)}, bf16[32,32,256]{2,1,0:T(8,128)(2,1)}, u32[]{:S(2)}, u32[]{:S(2)}) %collective-permute-start.7) | collective-permute-done | bytes 524320 | tf_op jit(solution)/shard_map/ppermute | solution.py:483
  91.7 8.4 %collective-permute-start.11 = (bf16[5,32,256]{2,1,0:T(8,128)(2,1)S(1)}, bf16[5,32,256]{2,1,0:T(8,128)(2,1)S(1)}, u32[]{:S(2)}, u32[]{:S(2)}) collective-permute-start(bf16[5,32,256]{2,1,0:T(8,128)(2,1)S(1)} %get-tuple-element.59), channel_id=1, source_target_pairs={{16,0},{32,16},{48,32},{64,48},{80,64},{96,80},{112,96},{128,112},... | collective-permute-start | bytes 245768 | tf_op jit(solution)/shard_map/ppermute | solution.py:483
  100.2 8.3 %collective-permute-done.9.rb = bf16[32,32,256]{2,1,0:T(8,128)(2,1)} collective-permute-done((bf16[32,32,256]{2,1,0:T(8,128)(2,1)}, bf16[32,32,256]{2,1,0:T(8,128)(2,1)}, u32[]{:S(2)}, u32[]{:S(2)}) %collective-permute-start.9) | collective-permute-done | bytes 524320 | tf_op jit(solution)/shard_map/ppermute | solution.py:483
  108.5 3.1 %collective-permute-done.10.xlo = bf16[5,32,256]{2,1,0:T(8,128)(2,1)S(1)} collective-permute-done((bf16[5,32,256]{2,1,0:T(8,128)(2,1)S(1)}, bf16[5,32,256]{2,1,0:T(8,128)(2,1)S(1)}, u32[]{:S(2)}, u32[]{:S(2)}) %collective-permute-start.10) | collective-permute-done | bytes 81952 | tf_op jit(solution)/shard_map/ppermute | solution.py:478
  113.3 6.4 %collective-permute-start.12 = (bf16[5,34,256]{2,1,0:T(8,128)(2,1)S(1)}, bf16[5,34,256]{2,1,0:T(8,128)(2,1)S(1)}, u32[]{:S(2)}, u32[]{:S(2)}) collective-permute-start(bf16[5,34,256]{2,1,0:T(8,128)(2,1)S(1)} %get-tuple-element.62), channel_id=1, source_target_pairs={{0,1},{1,2},{2,3},{3,4},{4,5},{5,6},{6,7},{7,8},{8,9},{9,10},{10,1... | collective-permute-start | bytes 261128 | tf_op jit(solution)/shard_map/ppermute | solution.py:478
  119.7 2.1 %collective-permute-start.13 = (bf16[5,34,256]{2,1,0:T(8,128)(2,1)S(1)}, bf16[5,34,256]{2,1,0:T(8,128)(2,1)S(1)}, u32[]{:S(2)}, u32[]{:S(2)}) collective-permute-start(bf16[5,34,256]{2,1,0:T(8,128)(2,1)S(1)} %get-tuple-element.63), channel_id=1, source_target_pairs={{1,0},{2,1},{3,2},{4,3},{5,4},{6,5},{7,6},{8,7},{9,8},{10,9},{11,1... | collective-permute-start | bytes 261128 | tf_op jit(solution)/shard_map/ppermute | solution.py:483
  122.6 3.7 %collective-permute-done.13.yhi = bf16[5,34,256]{2,1,0:T(8,128)(2,1)S(1)} collective-permute-done((bf16[5,34,256]{2,1,0:T(8,128)(2,1)S(1)}, bf16[5,34,256]{2,1,0:T(8,128)(2,1)S(1)}, u32[]{:S(2)}, u32[]{:S(2)}) %collective-permute-start.13) | collective-permute-done | bytes 87072 | tf_op jit(solution)/shard_map/ppermute | solution.py:483
  126.3 10.1 %force.1 = f32[2,3,32,32,256]{4,3,2,1,0:T(8,128)} custom-call(bf16[64,32,256]{2,1,0:T(8,128)(2,1)S(1)} %pick_own.1.own, bf16[32,32,256]{2,1,0:T(8,128)(2,1)} %collective-permute-done.6.la, bf16[32,32,256]{2,1,0:T(8,128)(2,1)} %collective-permute-done.7.ra, bf16[32,32,256]{2,1,0:T(8,128)(2,1)} %collective-permute-done.8.lb, ...), custom_call_target="tpu_custom_call" | custom-call | tf_op jit(solution)/shard_map/force/pallas_call | solution.py:465
  (39 shorter events, 16.8 us)
Async XLA Ops:
  0.0 34.8 %copy-start = (bf16[2,3,32,32,256]{4,3,2,1,0:T(8,128)(2,1)S(1)}, bf16[2,3,32,32,256]{4,3,2,1,0:T(8,128)(2,1)}, u32[]{:S(2)}) copy-start(bf16[2,3,32,32,256]{4,3,2,1,0:T(8,128)(2,1)} %vel.1) | copy-start | bytes 9437188
  0.0 23.5 %copy-start.7 = (s32[2,1,1,8]{3,2,1,0:T(1,128)S(1)}, s32[2,1,1,8]{3,2,1,0:T(1,128)}, u32[]{:S(2)}) copy-start(s32[2,1,1,8]{3,2,1,0:T(1,128)} %param.7) | copy-start | bytes 196
  1.9 51.5 %collective-permute-start.1 = (bf16[32,32,256]{2,1,0:T(8,128)(2,1)}, bf16[32,32,256]{2,1,0:T(8,128)(2,1)}, u32[]{:S(2)}, u32[]{:S(2)}) collective-permute-start(bf16[32,32,256]{2,1,0:T(8,128)(2,1)} %t_own.3), channel_id=1, source_target_pairs={{16,0},{32,16},{48,32},{64,48},{80,64},{96,80},{112,96},{128,112},... | collective-permute-start | bytes 1572872 | tf_op jit(solution)/shard_map/ppermute | solution.py:483
  10.7 42.8 %collective-permute-start = (bf16[32,32,256]{2,1,0:T(8,128)(2,1)}, bf16[32,32,256]{2,1,0:T(8,128)(2,1)}, u32[]{:S(2)}, u32[]{:S(2)}) collective-permute-start(bf16[32,32,256]{2,1,0:T(8,128)(2,1)} %t_own.3), channel_id=1, source_target_pairs={{0,16},{16,32},{32,48},{48,64},{64,80},{80,96},{96,112},{112,128},... | collective-permute-start | bytes 1572872 | tf_op jit(solution)/shard_map/ppermute | solution.py:478
  12.6 22.2 %collective-permute-start.3 = (bf16[7,32,256]{2,1,0:T(8,128)(2,1)S(1)}, bf16[7,32,256]{2,1,0:T(8,128)(2,1)S(1)}, u32[]{:S(2)}, u32[]{:S(2)}) collective-permute-start(bf16[7,32,256]{2,1,0:T(8,128)(2,1)S(1)} %get-tuple-element.35), channel_id=1, source_target_pairs={{16,0},{32,16},{48,32},{64,48},{80,64},{96,80},{112,96},{128,112},... | collective-permute-start | bytes 344072 | tf_op jit(solution)/shard_map/ppermute | solution.py:483
  21.1 13.7 %collective-permute-start.2 = (bf16[7,32,256]{2,1,0:T(8,128)(2,1)}, bf16[7,32,256]{2,1,0:T(8,128)(2,1)S(1)}, u32[]{:S(2)}, u32[]{:S(2)}) collective-permute-start(bf16[7,32,256]{2,1,0:T(8,128)(2,1)} %get-tuple-element.37), channel_id=1, source_target_pairs={{0,16},{16,32},{32,48},{48,64},{64,80},{80,96},{96,112},{112,128},... | collective-permute-start | bytes 344072 | tf_op jit(solution)/shard_map/ppermute | solution.py:478
  34.8 1.9 %copy-start.3 = (bf16[7,32,256]{2,1,0:T(8,128)(2,1)}, bf16[7,32,256]{2,1,0:T(8,128)(2,1)S(1)}, u32[]{:S(2)}) copy-start(bf16[7,32,256]{2,1,0:T(8,128)(2,1)S(1)} %collective-permute-done.2.hxl) | copy-start | bytes 344068
  34.8 1.3 copy-start.1
  36.7 12.8 %collective-permute-start.4 = (bf16[7,34,256]{2,1,0:T(8,128)(2,1)S(1)}, bf16[7,34,256]{2,1,0:T(8,128)(2,1)S(1)}, u32[]{:S(2)}, u32[]{:S(2)}) collective-permute-start(bf16[7,34,256]{2,1,0:T(8,128)(2,1)S(1)} %get-tuple-element.38), channel_id=1, source_target_pairs={{0,1},{1,2},{2,3},{3,4},{4,5},{5,6},{6,7},{7,8},{8,9},{9,10},{10,1... | collective-permute-start | bytes 365576 | tf_op jit(solution)/shard_map/ppermute | solution.py:478
  45.3 7.0 %collective-permute-start.5 = (bf16[7,34,256]{2,1,0:T(8,128)(2,1)S(1)}, bf16[7,34,256]{2,1,0:T(8,128)(2,1)S(1)}, u32[]{:S(2)}, u32[]{:S(2)}) collective-permute-start(bf16[7,34,256]{2,1,0:T(8,128)(2,1)S(1)} %get-tuple-element.39), channel_id=1, source_target_pairs={{1,0},{2,1},{3,2},{4,3},{5,4},{6,5},{7,6},{8,7},{9,8},{10,9},{11,1... | collective-permute-start | bytes 365576 | tf_op jit(solution)/shard_map/ppermute | solution.py:483
  53.5 15.1 %copy-start.5 = (bf16[1,768,512]{2,1,0:T(8,128)(2,1)}, bf16[1,768,512]{2,1,0:T(8,128)(2,1)S(1)}, u32[]{:S(2)}) copy-start(bf16[1,768,512]{2,1,0:T(8,128)(2,1)S(1)} %get-tuple-element.47.q_ref) | copy-start | bytes 2359300
  56.9 29.2 %collective-permute-start.6 = (bf16[32,32,256]{2,1,0:T(8,128)(2,1)}, bf16[32,32,256]{2,1,0:T(8,128)(2,1)}, u32[]{:S(2)}, u32[]{:S(2)}) collective-permute-start(bf16[32,32,256]{2,1,0:T(8,128)(2,1)} %get-tuple-element.48), channel_id=1, source_target_pairs={{0,1},{1,2},{2,3},{3,4},{4,5},{5,6},{6,7},{7,8},{8,9},{9,10},{10,1... | collective-permute-start | bytes 1572872 | tf_op jit(solution)/shard_map/ppermute | solution.py:478
  59.7 28.9 %collective-permute-start.7 = (bf16[32,32,256]{2,1,0:T(8,128)(2,1)}, bf16[32,32,256]{2,1,0:T(8,128)(2,1)}, u32[]{:S(2)}, u32[]{:S(2)}) collective-permute-start(bf16[32,32,256]{2,1,0:T(8,128)(2,1)} %get-tuple-element.41), channel_id=1, source_target_pairs={{1,0},{2,1},{3,2},{4,3},{5,4},{6,5},{7,6},{8,7},{9,8},{10,9},{11,1... | collective-permute-start | bytes 1572872 | tf_op jit(solution)/shard_map/ppermute | solution.py:483
  68.6 31.6 %collective-permute-start.8 = (bf16[32,32,256]{2,1,0:T(8,128)(2,1)}, bf16[32,32,256]{2,1,0:T(8,128)(2,1)}, u32[]{:S(2)}, u32[]{:S(2)}) collective-permute-start(bf16[32,32,256]{2,1,0:T(8,128)(2,1)} %get-tuple-element.49), channel_id=1, source_target_pairs={{0,1},{1,2},{2,3},{3,4},{4,5},{5,6},{6,7},{7,8},{8,9},{9,10},{10,1... | collective-permute-start | bytes 1572872 | tf_op jit(solution)/shard_map/ppermute | solution.py:478
  70.5 38.0 %collective-permute-start.9 = (bf16[32,32,256]{2,1,0:T(8,128)(2,1)}, bf16[32,32,256]{2,1,0:T(8,128)(2,1)}, u32[]{:S(2)}, u32[]{:S(2)}) collective-permute-start(bf16[32,32,256]{2,1,0:T(8,128)(2,1)} %get-tuple-element.46), channel_id=1, source_target_pairs={{1,0},{2,1},{3,2},{4,3},{5,4},{6,5},{7,6},{8,7},{9,8},{10,9},{11,1... | collective-permute-start | bytes 1572872 | tf_op jit(solution)/shard_map/ppermute | solution.py:483
  77.2 3.7 %copy-start.2 = (f32[32,32,256]{2,1,0:T(8,128)S(1)}, f32[32,32,256]{2,1,0:T(8,128)}, u32[]{:S(2)}) copy-start(f32[32,32,256]{2,1,0:T(8,128)} %p_ref.2) | copy-start | bytes 3145732
  77.2 3.6 %copy-start.4 = (bf16[7,32,256]{2,1,0:T(8,128)(2,1)S(1)}, bf16[7,32,256]{2,1,0:T(8,128)(2,1)}, u32[]{:S(2)}) copy-start(bf16[7,32,256]{2,1,0:T(8,128)(2,1)} %copy-done.3) | copy-start | bytes 344068
  77.3 1.2 copy-start.6
  89.8 21.8 %collective-permute-start.10 = (bf16[5,32,256]{2,1,0:T(8,128)(2,1)S(1)}, bf16[5,32,256]{2,1,0:T(8,128)(2,1)S(1)}, u32[]{:S(2)}, u32[]{:S(2)}) collective-permute-start(bf16[5,32,256]{2,1,0:T(8,128)(2,1)S(1)} %get-tuple-element.58), channel_id=1, source_target_pairs={{0,16},{16,32},{32,48},{48,64},{64,80},{80,96},{96,112},{112,128},... | collective-permute-start | bytes 245768 | tf_op jit(solution)/shard_map/ppermute | solution.py:478
  91.7 19.8 %collective-permute-start.11 = (bf16[5,32,256]{2,1,0:T(8,128)(2,1)S(1)}, bf16[5,32,256]{2,1,0:T(8,128)(2,1)S(1)}, u32[]{:S(2)}, u32[]{:S(2)}) collective-permute-start(bf16[5,32,256]{2,1,0:T(8,128)(2,1)S(1)} %get-tuple-element.59), channel_id=1, source_target_pairs={{16,0},{32,16},{48,32},{64,48},{80,64},{96,80},{112,96},{128,112},... | collective-permute-start | bytes 245768 | tf_op jit(solution)/shard_map/ppermute | solution.py:483
  113.3 9.3 %collective-permute-start.12 = (bf16[5,34,256]{2,1,0:T(8,128)(2,1)S(1)}, bf16[5,34,256]{2,1,0:T(8,128)(2,1)S(1)}, u32[]{:S(2)}, u32[]{:S(2)}) collective-permute-start(bf16[5,34,256]{2,1,0:T(8,128)(2,1)S(1)} %get-tuple-element.62), channel_id=1, source_target_pairs={{0,1},{1,2},{2,3},{3,4},{4,5},{5,6},{6,7},{7,8},{8,9},{9,10},{10,1... | collective-permute-start | bytes 261128 | tf_op jit(solution)/shard_map/ppermute | solution.py:478
  119.7 6.6 %collective-permute-start.13 = (bf16[5,34,256]{2,1,0:T(8,128)(2,1)S(1)}, bf16[5,34,256]{2,1,0:T(8,128)(2,1)S(1)}, u32[]{:S(2)}, u32[]{:S(2)}) collective-permute-start(bf16[5,34,256]{2,1,0:T(8,128)(2,1)S(1)} %get-tuple-element.63), channel_id=1, source_target_pairs={{1,0},{2,1},{3,2},{4,3},{5,4},{6,5},{7,6},{8,7},{9,8},{10,9},{11,1... | collective-permute-start | bytes 261128 | tf_op jit(solution)/shard_map/ppermute | solution.py:483

commit v8 on v7

--- a/solution.py
+++ b/solution.py
@@ -499,9 +499,8 @@
     )
     halo_xl = forward(high, "gx")
     halo_xh = backward(low, "gx")
-    late_template, _ = lax.optimization_barrier((template, low))
-    t_lo = forward(late_template, "gx")
-    t_hi = backward(late_template, "gx")
+    t_lo = forward(template, "gx")
+    t_hi = backward(template, "gx")
 
     ids = src_ids.reshape(slots)
     first_block = ids // (count_second * depth_blocks)

time: 137 us -> 135 us (0.985)
  waiting for transfers between devices: 33.8 us -> 31.2 us
    ppermute x7, waiting for transfers between devices: 16.5 us -> 15 us  [forward(): return lax.ppermute(value, axis, [(i, i + 1) for i in range(ends)])]
    unnamed x17 -> x21, local copies, waits for them, and re-layouts: 3.01 us -> 4.11 us
  transfers between devices with their start and end apart: 14 -> 14, of which waited for: 8 -> 8; matrix products, arithmetic and copies ran while one was open for 1% -> 1% of each run, Pallas kernels for 10% -> 11%
where the time goes in v8:
time: 135 us
  starting transfers between devices  67.8 us (50%)
  waiting for transfers between devices  31.2 us (23%)
  Pallas kernels  30.2 us (22%)
  local copies, waits for them, and re-layouts  4.2 us (3%)
    ppermute x7, starting transfers between devices, backward(): return lax.ppermute(value, axis, [(i + 1, i) for i in range(ends)])  42.1 us
    ppermute x7, starting transfers between devices, forward(): return lax.ppermute(value, axis, [(i, i + 1) for i in range(ends)])  25.7 us
    ppermute x7, waiting for transfers between devices, backward(): return lax.ppermute(value, axis, [(i + 1, i) for i in range(ends)])  16.3 us
    ppermute x7, waiting for transfers between devices, forward(): return lax.ppermute(value, axis, [(i, i + 1) for i in range(ends)])  15 us
    pallas_call x1, Pallas kernels, force(): call(functools.partial(force_kernel, groups), struct((2, 3, nx, ny, nz),...  10.1 us
    pallas_call x3, Pallas kernels, pick(): call(functools.partial(pick_kernel, planes), outs, [], name, in_specs)(*ins)  8.43 us
    unnamed x21, local copies, waits for them, and re-layouts  4.11 us
    pallas_call x1, Pallas kernels, upwind_one(): call(upwind_one_kernel, outs, scratch, 'upwind_one', in_specs)  3.03 us
  transfers between devices with their start and end apart: 14, of which 8 were waited for; matrix products, arithmetic and copies ran while one was open for 1% of the time, Pallas kernels for 11%

profile of v8, /device:TPU:26, one launch (start us, length us, event | category | flops | bytes accessed | tf_op | source)
XLA Modules:
  0.0 134.5 jit_solution(15864400791717019184)
XLA Ops:
  0.0 9.0 %collective-permute-start.1 = (bf16[32,32,256]{2,1,0:T(8,128)(2,1)}, bf16[32,32,256]{2,1,0:T(8,128)(2,1)}, u32[]{:S(2)}, u32[]{:S(2)}) collective-permute-start(bf16[32,32,256]{2,1,0:T(8,128)(2,1)} %t_own.3), channel_id=1, source_target_pairs={{16,0},{32,16},{48,32},{64,48},{80,64},{96,80},{112,96},{128,112},... | collective-permute-start | bytes 1572872 | tf_op jit(solution)/shard_map/ppermute | solution.py:483
  9.0 1.9 %collective-permute-start = (bf16[32,32,256]{2,1,0:T(8,128)(2,1)}, bf16[32,32,256]{2,1,0:T(8,128)(2,1)}, u32[]{:S(2)}, u32[]{:S(2)}) collective-permute-start(bf16[32,32,256]{2,1,0:T(8,128)(2,1)} %t_own.3), channel_id=1, source_target_pairs={{0,16},{16,32},{32,48},{48,64},{64,80},{80,96},{96,112},{112,128},... | collective-permute-start | bytes 1572872 | tf_op jit(solution)/shard_map/ppermute | solution.py:478
  12.7 2.4 %collective-permute-start.2 = (bf16[7,32,256]{2,1,0:T(8,128)(2,1)}, bf16[7,32,256]{2,1,0:T(8,128)(2,1)S(1)}, u32[]{:S(2)}, u32[]{:S(2)}) collective-permute-start(bf16[7,32,256]{2,1,0:T(8,128)(2,1)} %get-tuple-element.34), channel_id=1, source_target_pairs={{0,16},{16,32},{32,48},{48,64},{64,80},{80,96},{96,112},{112,128},... | collective-permute-start | bytes 344072 | tf_op jit(solution)/shard_map/ppermute | solution.py:478
  15.1 8.0 %collective-permute-start.3 = (bf16[7,32,256]{2,1,0:T(8,128)(2,1)S(1)}, bf16[7,32,256]{2,1,0:T(8,128)(2,1)S(1)}, u32[]{:S(2)}, u32[]{:S(2)}) collective-permute-start(bf16[7,32,256]{2,1,0:T(8,128)(2,1)S(1)} %get-tuple-element.35), channel_id=1, source_target_pairs={{16,0},{32,16},{48,32},{64,48},{80,64},{96,80},{112,96},{128,112},... | collective-permute-start | bytes 344072 | tf_op jit(solution)/shard_map/ppermute | solution.py:483
  24.4 8.7 %collective-permute-done.2.hxl = bf16[7,32,256]{2,1,0:T(8,128)(2,1)S(1)} collective-permute-done((bf16[7,32,256]{2,1,0:T(8,128)(2,1)}, bf16[7,32,256]{2,1,0:T(8,128)(2,1)S(1)}, u32[]{:S(2)}, u32[]{:S(2)}) %collective-permute-start.2) | collective-permute-done | bytes 114720 | tf_op jit(solution)/shard_map/ppermute | solution.py:478
  35.0 8.7 %collective-permute-start.4 = (bf16[7,34,256]{2,1,0:T(8,128)(2,1)S(1)}, bf16[7,34,256]{2,1,0:T(8,128)(2,1)S(1)}, u32[]{:S(2)}, u32[]{:S(2)}) collective-permute-start(bf16[7,34,256]{2,1,0:T(8,128)(2,1)S(1)} %get-tuple-element.36), channel_id=1, source_target_pairs={{0,1},{1,2},{2,3},{3,4},{4,5},{5,6},{6,7},{7,8},{8,9},{9,10},{10,1... | collective-permute-start | bytes 365576 | tf_op jit(solution)/shard_map/ppermute | solution.py:478
  43.7 1.9 %collective-permute-start.5 = (bf16[7,34,256]{2,1,0:T(8,128)(2,1)S(1)}, bf16[7,34,256]{2,1,0:T(8,128)(2,1)S(1)}, u32[]{:S(2)}, u32[]{:S(2)}) collective-permute-start(bf16[7,34,256]{2,1,0:T(8,128)(2,1)S(1)} %get-tuple-element.37), channel_id=1, source_target_pairs={{1,0},{2,1},{3,2},{4,3},{5,4},{6,5},{7,6},{8,7},{9,8},{10,9},{11,1... | collective-permute-start | bytes 365576 | tf_op jit(solution)/shard_map/ppermute | solution.py:483
  45.6 2.2 %collective-permute-done.4.left.hyl = bf16[7,34,256]{2,1,0:T(8,128)(2,1)S(1)} collective-permute-done((bf16[7,34,256]{2,1,0:T(8,128)(2,1)S(1)}, bf16[7,34,256]{2,1,0:T(8,128)(2,1)S(1)}, u32[]{:S(2)}, u32[]{:S(2)}) %collective-permute-start.4) | collective-permute-done | bytes 121888 | tf_op jit(solution)/shard_map/ppermute | solution.py:478
  47.8 2.9 %collective-permute-done.5.right.hyh = bf16[7,34,256]{2,1,0:T(8,128)(2,1)S(1)} collective-permute-done((bf16[7,34,256]{2,1,0:T(8,128)(2,1)S(1)}, bf16[7,34,256]{2,1,0:T(8,128)(2,1)S(1)}, u32[]{:S(2)}, u32[]{:S(2)}) %collective-permute-start.5) | collective-permute-done | bytes 121888 | tf_op jit(solution)/shard_map/ppermute | solution.py:483
  51.8 3.2 %pick_outer.1 = (bf16[32,32,256]{2,1,0:T(8,128)(2,1)}, bf16[32,32,256]{2,1,0:T(8,128)(2,1)}) custom-call(bf16[32,32,256]{2,1,0:T(8,128)(2,1)} %collective-permute-done.t_lo, bf16[32,32,256]{2,1,0:T(8,128)(2,1)S(1)} %copy-done.3, bf16[32,32,256]{2,1,0:T(8,128)(2,1)} %collective-permute-done.1.t_hi, bf16[2,768,512]{2,1,0:T(8,128)(2,1)S(1)} %get-tuple-element.38.q_ref), custom_call_target="tpu_custom_call" | custom-call | tf_op jit(solution)/shard_map/pick_outer/pallas_call | solution.py:307
  55.0 2.8 %collective-permute-start.6 = (bf16[32,32,256]{2,1,0:T(8,128)(2,1)}, bf16[32,32,256]{2,1,0:T(8,128)(2,1)}, u32[]{:S(2)}, u32[]{:S(2)}) collective-permute-start(bf16[32,32,256]{2,1,0:T(8,128)(2,1)} %get-tuple-element.46), channel_id=1, source_target_pairs={{0,1},{1,2},{2,3},{3,4},{4,5},{5,6},{6,7},{7,8},{8,9},{9,10},{10,1... | collective-permute-start | bytes 1572872 | tf_op jit(solution)/shard_map/ppermute | solution.py:478
  57.9 5.7 %collective-permute-start.7 = (bf16[32,32,256]{2,1,0:T(8,128)(2,1)}, bf16[32,32,256]{2,1,0:T(8,128)(2,1)}, u32[]{:S(2)}, u32[]{:S(2)}) collective-permute-start(bf16[32,32,256]{2,1,0:T(8,128)(2,1)} %get-tuple-element.39), channel_id=1, source_target_pairs={{1,0},{2,1},{3,2},{4,3},{5,4},{6,5},{7,6},{8,7},{9,8},{10,9},{11,1... | collective-permute-start | bytes 1572872 | tf_op jit(solution)/shard_map/ppermute | solution.py:483
  63.6 3.0 %pick_inner.1 = (bf16[32,32,256]{2,1,0:T(8,128)(2,1)}, bf16[32,32,256]{2,1,0:T(8,128)(2,1)}) custom-call(bf16[32,32,256]{2,1,0:T(8,128)(2,1)} %collective-permute-done.t_lo, bf16[32,32,256]{2,1,0:T(8,128)(2,1)S(1)} %copy-done.3, bf16[32,32,256]{2,1,0:T(8,128)(2,1)} %collective-permute-done.1.t_hi, bf16[2,768,512]{2,1,0:T(8,128)(2,1)S(1)} %get-tuple-element.38.q_ref), custom_call_target="tpu_custom_call" | custom-call | tf_op jit(solution)/shard_map/pick_inner/pallas_call | solution.py:307
  68.5 6.6 %collective-permute-start.9 = (bf16[32,32,256]{2,1,0:T(8,128)(2,1)}, bf16[32,32,256]{2,1,0:T(8,128)(2,1)}, u32[]{:S(2)}, u32[]{:S(2)}) collective-permute-start(bf16[32,32,256]{2,1,0:T(8,128)(2,1)} %get-tuple-element.44), channel_id=1, source_target_pairs={{1,0},{2,1},{3,2},{4,3},{5,4},{6,5},{7,6},{8,7},{9,8},{10,9},{11,1... | collective-permute-start | bytes 1572872 | tf_op jit(solution)/shard_map/ppermute | solution.py:483
  77.5 2.2 %pick_own.1.own = bf16[64,32,256]{2,1,0:T(8,128)(2,1)S(1)} custom-call(bf16[32,32,256]{2,1,0:T(8,128)(2,1)} %collective-permute-done.t_lo, bf16[32,32,256]{2,1,0:T(8,128)(2,1)S(1)} %copy-done.4, bf16[32,32,256]{2,1,0:T(8,128)(2,1)} %collective-permute-done.1.t_hi, bf16[1,768,512]{2,1,0:T(8,128)(2,1)S(1)} %copy-done.8), custom_call_target="tpu_custom_call" | custom-call | tf_op jit(solution)/shard_map/pick_own/pallas_call | solution.py:307
  79.7 3.0 %upwind_one.1 = (f32[32,32,256]{2,1,0:T(8,128)S(1)}, f32[32,256]{1,0:T(8,128)S(1)}, f32[32,256]{1,0:T(8,128)S(1)}, f32[32,256]{1,0:T(8,128)S(1)}, f32[32,256]{1,0:T(8,128)S(1)}) custom-call(f32[4]{0:T(128)S(1)} %add_convert_fusion.inside, f32[32,32,256]{2,1,0:T(8,128)S(1)} %copy-done.2, bf16[2,3,32,32,256]{4,3,2,1,0:T(8,128)(2,1)S(1)} %copy-done, ...), custom_call_target="tpu_custom_call" | custom-call | tf_op jit(solution)/shard_map/upwind_one/pallas_call | solution.py:245
  82.8 2.2 %upwind_zero.1 = (f32[32,32,256]{2,1,0:T(8,128)S(1)}, bf16[1,32,256]{2,1,0:T(8,128)(2,1)S(1)}, bf16[1,32,256]{2,1,0:T(8,128)(2,1)S(1)}, bf16[1,32,256]{2,1,0:T(8,128)(2,1)S(1)}, bf16[1,32,256]{2,1,0:T(8,128)(2,1)S(1)}) custom-call(f32[32,32,256]{2,1,0:T(8,128)S(1)} %get-tuple-element.49.p_ref.adj1, bf16[2,3,32,32,256]{4,3,2,1,0:T(8,128)(2,1)S(1)} %copy-done, ...), custom_call_target="tpu_custom_call" | custom-call | tf_op jit(solution)/shard_map/upwind_zero/pallas_call | solution.py:254
  89.9 8.4 %collective-permute-start.11 = (bf16[5,32,256]{2,1,0:T(8,128)(2,1)S(1)}, bf16[5,32,256]{2,1,0:T(8,128)(2,1)S(1)}, u32[]{:S(2)}, u32[]{:S(2)}) collective-permute-start(bf16[5,32,256]{2,1,0:T(8,128)(2,1)S(1)} %get-tuple-element.57), channel_id=1, source_target_pairs={{16,0},{32,16},{48,32},{64,48},{80,64},{96,80},{112,96},{128,112},... | collective-permute-start | bytes 245768 | tf_op jit(solution)/shard_map/ppermute | solution.py:483
  98.3 8.3 %collective-permute-done.9.rb = bf16[32,32,256]{2,1,0:T(8,128)(2,1)} collective-permute-done((bf16[32,32,256]{2,1,0:T(8,128)(2,1)}, bf16[32,32,256]{2,1,0:T(8,128)(2,1)}, u32[]{:S(2)}, u32[]{:S(2)}) %collective-permute-start.9) | collective-permute-done | bytes 524320 | tf_op jit(solution)/shard_map/ppermute | solution.py:483
  106.6 3.4 %collective-permute-done.10.xlo = bf16[5,32,256]{2,1,0:T(8,128)(2,1)S(1)} collective-permute-done((bf16[5,32,256]{2,1,0:T(8,128)(2,1)S(1)}, bf16[5,32,256]{2,1,0:T(8,128)(2,1)S(1)}, u32[]{:S(2)}, u32[]{:S(2)}) %collective-permute-start.10) | collective-permute-done | bytes 81952 | tf_op jit(solution)/shard_map/ppermute | solution.py:478
  111.8 6.1 %collective-permute-start.12 = (bf16[5,34,256]{2,1,0:T(8,128)(2,1)S(1)}, bf16[5,34,256]{2,1,0:T(8,128)(2,1)S(1)}, u32[]{:S(2)}, u32[]{:S(2)}) collective-permute-start(bf16[5,34,256]{2,1,0:T(8,128)(2,1)S(1)} %get-tuple-element.60), channel_id=1, source_target_pairs={{0,1},{1,2},{2,3},{3,4},{4,5},{5,6},{6,7},{7,8},{8,9},{9,10},{10,1... | collective-permute-start | bytes 261128 | tf_op jit(solution)/shard_map/ppermute | solution.py:478
  117.9 2.5 %collective-permute-start.13 = (bf16[5,34,256]{2,1,0:T(8,128)(2,1)S(1)}, bf16[5,34,256]{2,1,0:T(8,128)(2,1)S(1)}, u32[]{:S(2)}, u32[]{:S(2)}) collective-permute-start(bf16[5,34,256]{2,1,0:T(8,128)(2,1)S(1)} %get-tuple-element.61), channel_id=1, source_target_pairs={{1,0},{2,1},{3,2},{4,3},{5,4},{6,5},{7,6},{8,7},{9,8},{10,9},{11,1... | collective-permute-start | bytes 261128 | tf_op jit(solution)/shard_map/ppermute | solution.py:483
  121.1 3.4 %collective-permute-done.13.yhi = bf16[5,34,256]{2,1,0:T(8,128)(2,1)S(1)} collective-permute-done((bf16[5,34,256]{2,1,0:T(8,128)(2,1)S(1)}, bf16[5,34,256]{2,1,0:T(8,128)(2,1)S(1)}, u32[]{:S(2)}, u32[]{:S(2)}) %collective-permute-start.13) | collective-permute-done | bytes 87072 | tf_op jit(solution)/shard_map/ppermute | solution.py:483
  124.4 10.1 %force.1 = f32[2,3,32,32,256]{4,3,2,1,0:T(8,128)} custom-call(bf16[64,32,256]{2,1,0:T(8,128)(2,1)S(1)} %pick_own.1.own, bf16[32,32,256]{2,1,0:T(8,128)(2,1)} %collective-permute-done.6.la, bf16[32,32,256]{2,1,0:T(8,128)(2,1)} %collective-permute-done.7.ra, bf16[32,32,256]{2,1,0:T(8,128)(2,1)} %collective-permute-done.8.lb, ...), custom_call_target="tpu_custom_call" | custom-call | tf_op jit(solution)/shard_map/force/pallas_call | solution.py:465
  (43 shorter events, 17.6 us)
Async XLA Ops:
  0.0 33.1 %copy-start = (bf16[2,3,32,32,256]{4,3,2,1,0:T(8,128)(2,1)S(1)}, bf16[2,3,32,32,256]{4,3,2,1,0:T(8,128)(2,1)}, u32[]{:S(2)}) copy-start(bf16[2,3,32,32,256]{4,3,2,1,0:T(8,128)(2,1)} %vel.1) | copy-start | bytes 9437188
  0.0 23.6 %copy-start.9 = (s32[2,1,1,8]{3,2,1,0:T(1,128)S(1)}, s32[2,1,1,8]{3,2,1,0:T(1,128)}, u32[]{:S(2)}) copy-start(s32[2,1,1,8]{3,2,1,0:T(1,128)} %param.7) | copy-start | bytes 196
  0.0 51.8 %collective-permute-start.1 = (bf16[32,32,256]{2,1,0:T(8,128)(2,1)}, bf16[32,32,256]{2,1,0:T(8,128)(2,1)}, u32[]{:S(2)}, u32[]{:S(2)}) collective-permute-start(bf16[32,32,256]{2,1,0:T(8,128)(2,1)} %t_own.3), channel_id=1, source_target_pairs={{16,0},{32,16},{48,32},{64,48},{80,64},{96,80},{112,96},{128,112},... | collective-permute-start | bytes 1572872 | tf_op jit(solution)/shard_map/ppermute | solution.py:483
  9.0 42.8 %collective-permute-start = (bf16[32,32,256]{2,1,0:T(8,128)(2,1)}, bf16[32,32,256]{2,1,0:T(8,128)(2,1)}, u32[]{:S(2)}, u32[]{:S(2)}) collective-permute-start(bf16[32,32,256]{2,1,0:T(8,128)(2,1)} %t_own.3), channel_id=1, source_target_pairs={{0,16},{16,32},{32,48},{48,64},{64,80},{80,96},{96,112},{112,128},... | collective-permute-start | bytes 1572872 | tf_op jit(solution)/shard_map/ppermute | solution.py:478
  12.7 20.4 %collective-permute-start.2 = (bf16[7,32,256]{2,1,0:T(8,128)(2,1)}, bf16[7,32,256]{2,1,0:T(8,128)(2,1)S(1)}, u32[]{:S(2)}, u32[]{:S(2)}) collective-permute-start(bf16[7,32,256]{2,1,0:T(8,128)(2,1)} %get-tuple-element.34), channel_id=1, source_target_pairs={{0,16},{16,32},{32,48},{48,64},{64,80},{80,96},{96,112},{112,128},... | collective-permute-start | bytes 344072 | tf_op jit(solution)/shard_map/ppermute | solution.py:478
  15.1 18.0 %collective-permute-start.3 = (bf16[7,32,256]{2,1,0:T(8,128)(2,1)S(1)}, bf16[7,32,256]{2,1,0:T(8,128)(2,1)S(1)}, u32[]{:S(2)}, u32[]{:S(2)}) collective-permute-start(bf16[7,32,256]{2,1,0:T(8,128)(2,1)S(1)} %get-tuple-element.35), channel_id=1, source_target_pairs={{16,0},{32,16},{48,32},{64,48},{80,64},{96,80},{112,96},{128,112},... | collective-permute-start | bytes 344072 | tf_op jit(solution)/shard_map/ppermute | solution.py:483
  33.1 1.2 copy-start.1
  34.3 0.7 copy-start.5
  34.3 17.5 %copy-start.3 = (bf16[32,32,256]{2,1,0:T(8,128)(2,1)S(1)}, bf16[32,32,256]{2,1,0:T(8,128)(2,1)}, u32[]{:S(2)}) copy-start(bf16[32,32,256]{2,1,0:T(8,128)(2,1)} %t_own.3) | copy-start | bytes 1572868
  35.0 12.8 %collective-permute-start.4 = (bf16[7,34,256]{2,1,0:T(8,128)(2,1)S(1)}, bf16[7,34,256]{2,1,0:T(8,128)(2,1)S(1)}, u32[]{:S(2)}, u32[]{:S(2)}) collective-permute-start(bf16[7,34,256]{2,1,0:T(8,128)(2,1)S(1)} %get-tuple-element.36), channel_id=1, source_target_pairs={{0,1},{1,2},{2,3},{3,4},{4,5},{5,6},{6,7},{7,8},{8,9},{9,10},{10,1... | collective-permute-start | bytes 365576 | tf_op jit(solution)/shard_map/ppermute | solution.py:478
  43.7 7.0 %collective-permute-start.5 = (bf16[7,34,256]{2,1,0:T(8,128)(2,1)S(1)}, bf16[7,34,256]{2,1,0:T(8,128)(2,1)S(1)}, u32[]{:S(2)}, u32[]{:S(2)}) collective-permute-start(bf16[7,34,256]{2,1,0:T(8,128)(2,1)S(1)} %get-tuple-element.37), channel_id=1, source_target_pairs={{1,0},{2,1},{3,2},{4,3},{5,4},{6,5},{7,6},{8,7},{9,8},{10,9},{11,1... | collective-permute-start | bytes 365576 | tf_op jit(solution)/shard_map/ppermute | solution.py:483
  51.8 14.8 %copy-start.7 = (bf16[1,768,512]{2,1,0:T(8,128)(2,1)}, bf16[1,768,512]{2,1,0:T(8,128)(2,1)S(1)}, u32[]{:S(2)}) copy-start(bf16[1,768,512]{2,1,0:T(8,128)(2,1)S(1)} %get-tuple-element.45.q_ref) | copy-start | bytes 2359300
  55.0 29.9 %collective-permute-start.6 = (bf16[32,32,256]{2,1,0:T(8,128)(2,1)}, bf16[32,32,256]{2,1,0:T(8,128)(2,1)}, u32[]{:S(2)}, u32[]{:S(2)}) collective-permute-start(bf16[32,32,256]{2,1,0:T(8,128)(2,1)} %get-tuple-element.46), channel_id=1, source_target_pairs={{0,1},{1,2},{2,3},{3,4},{4,5},{5,6},{6,7},{7,8},{8,9},{9,10},{10,1... | collective-permute-start | bytes 1572872 | tf_op jit(solution)/shard_map/ppermute | solution.py:478
  57.9 28.9 %collective-permute-start.7 = (bf16[32,32,256]{2,1,0:T(8,128)(2,1)}, bf16[32,32,256]{2,1,0:T(8,128)(2,1)}, u32[]{:S(2)}, u32[]{:S(2)}) collective-permute-start(bf16[32,32,256]{2,1,0:T(8,128)(2,1)} %get-tuple-element.39), channel_id=1, source_target_pairs={{1,0},{2,1},{3,2},{4,3},{5,4},{6,5},{7,6},{8,7},{9,8},{10,9},{11,1... | collective-permute-start | bytes 1572872 | tf_op jit(solution)/shard_map/ppermute | solution.py:483
  66.6 31.7 %collective-permute-start.8 = (bf16[32,32,256]{2,1,0:T(8,128)(2,1)}, bf16[32,32,256]{2,1,0:T(8,128)(2,1)}, u32[]{:S(2)}, u32[]{:S(2)}) collective-permute-start(bf16[32,32,256]{2,1,0:T(8,128)(2,1)} %get-tuple-element.47), channel_id=1, source_target_pairs={{0,1},{1,2},{2,3},{3,4},{4,5},{5,6},{6,7},{7,8},{8,9},{9,10},{10,1... | collective-permute-start | bytes 1572872 | tf_op jit(solution)/shard_map/ppermute | solution.py:478
  68.5 38.1 %collective-permute-start.9 = (bf16[32,32,256]{2,1,0:T(8,128)(2,1)}, bf16[32,32,256]{2,1,0:T(8,128)(2,1)}, u32[]{:S(2)}, u32[]{:S(2)}) collective-permute-start(bf16[32,32,256]{2,1,0:T(8,128)(2,1)} %get-tuple-element.44), channel_id=1, source_target_pairs={{1,0},{2,1},{3,2},{4,3},{5,4},{6,5},{7,6},{8,7},{9,8},{10,9},{11,1... | collective-permute-start | bytes 1572872 | tf_op jit(solution)/shard_map/ppermute | solution.py:483
  75.1 4.6 %copy-start.2 = (f32[32,32,256]{2,1,0:T(8,128)S(1)}, f32[32,32,256]{2,1,0:T(8,128)}, u32[]{:S(2)}) copy-start(f32[32,32,256]{2,1,0:T(8,128)} %p_ref.2) | copy-start | bytes 3145732
  75.2 1.1 copy-start.4
  76.4 1.1 copy-start.8
  77.5 2.2 %copy-start.6 = (bf16[7,32,256]{2,1,0:T(8,128)(2,1)S(1)}, bf16[7,32,256]{2,1,0:T(8,128)(2,1)}, u32[]{:S(2)}) copy-start(bf16[7,32,256]{2,1,0:T(8,128)(2,1)} %copy-done.5) | copy-start | bytes 344068
  87.9 22.1 %collective-permute-start.10 = (bf16[5,32,256]{2,1,0:T(8,128)(2,1)S(1)}, bf16[5,32,256]{2,1,0:T(8,128)(2,1)S(1)}, u32[]{:S(2)}, u32[]{:S(2)}) collective-permute-start(bf16[5,32,256]{2,1,0:T(8,128)(2,1)S(1)} %get-tuple-element.56), channel_id=1, source_target_pairs={{0,16},{16,32},{32,48},{48,64},{64,80},{80,96},{96,112},{112,128},... | collective-permute-start | bytes 245768 | tf_op jit(solution)/shard_map/ppermute | solution.py:478
  89.9 20.2 %collective-permute-start.11 = (bf16[5,32,256]{2,1,0:T(8,128)(2,1)S(1)}, bf16[5,32,256]{2,1,0:T(8,128)(2,1)S(1)}, u32[]{:S(2)}, u32[]{:S(2)}) collective-permute-start(bf16[5,32,256]{2,1,0:T(8,128)(2,1)S(1)} %get-tuple-element.57), channel_id=1, source_target_pairs={{16,0},{32,16},{48,32},{64,48},{80,64},{96,80},{112,96},{128,112},... | collective-permute-start | bytes 245768 | tf_op jit(solution)/shard_map/ppermute | solution.py:483
  111.8 9.3 %collective-permute-start.12 = (bf16[5,34,256]{2,1,0:T(8,128)(2,1)S(1)}, bf16[5,34,256]{2,1,0:T(8,128)(2,1)S(1)}, u32[]{:S(2)}, u32[]{:S(2)}) collective-permute-start(bf16[5,34,256]{2,1,0:T(8,128)(2,1)S(1)} %get-tuple-element.60), channel_id=1, source_target_pairs={{0,1},{1,2},{2,3},{3,4},{4,5},{5,6},{6,7},{7,8},{8,9},{9,10},{10,1... | collective-permute-start | bytes 261128 | tf_op jit(solution)/shard_map/ppermute | solution.py:478
  117.9 6.6 %collective-permute-start.13 = (bf16[5,34,256]{2,1,0:T(8,128)(2,1)S(1)}, bf16[5,34,256]{2,1,0:T(8,128)(2,1)S(1)}, u32[]{:S(2)}, u32[]{:S(2)}) collective-permute-start(bf16[5,34,256]{2,1,0:T(8,128)(2,1)S(1)} %get-tuple-element.61), channel_id=1, source_target_pairs={{1,0},{2,1},{3,2},{4,3},{5,4},{6,5},{7,6},{8,7},{9,8},{10,9},{11,1... | collective-permute-start | bytes 261128 | tf_op jit(solution)/shard_map/ppermute | solution.py:483
